TPU v7x, 32 devices: a whole 2x2x4 slice. The times are simulated.
32 devices in a mesh: rep: 16 (over z, x, core), dom: 2 (over y).
Axes of the slice: x: 2, y: 2, z: 4, core: 2. Of those that a mesh axis runs over, the one named last changes fastest.
Arguments:
- field: float32 [16, 256, 2048], P('rep', 'dom'), may hold values from -2.5 to 2.5
- momentum: float32 [16, 256, 2048], P('rep', 'dom'), may hold values from -4 to 4
- labels: int32 [16], P('rep'), may hold values from 0 to 15, each once
- betas: float32 [16], replicated, may hold values from 0.4 to 1.6
- accept: int32 [16], P('rep'), may hold values 0 or 1
- swap_pairs: int32 [16], replicated, may hold values from 0 to 15, as said below
Outputs:
- field_out: float32 [16, 256, 2048], P('rep', 'dom')
- field_sorted: float32 [16, 256, 2048], P('rep', 'dom')
- labels_out: int32 [16], P('rep')
- energy_change: float32 [16], P('rep')
- ladder_action: float32 [16], P('rep')
Inputs may be any that keep to these rules, and one draw needn't show every extreme that they name: Each temperature index t is paired with itself, with t - 1 or with t + 1, and the pairing is symmetric: swap_pairs[swap_pairs[t]] = t. labels is a permutation of the temperature indices.
All inputs are finite; a program needn't handle non-finite values. No bound on the sum of `accept` on one device may be relied on, other than what follows from the above.
Results may differ from a plain program's by a relative error of at most 0.0003.
Values sent between devices are 32-bit elements; how exact they have to be, the bound alone decides.
No kernel may reach another device: no remote copies, remote signals or barrier semaphores. Data moves between devices by JAX's collectives and lax.ppermute only.
A program may use at most 64 MiB of HBM per device.

v0:
```python
import jax
import jax.numpy as jnp
from jax import lax
from jax.sharding import PartitionSpec as P

STEPS = 8


hopping = 0.18
quartic = 0.3
step_size = 0.05


def with_halo(cells, sides, width):
    for axis, dim in sides:
        count = lax.axis_size(axis)
        head = lax.slice_in_dim(cells, 0, width, axis=dim)
        tail = lax.slice_in_dim(cells, cells.shape[dim] - width, cells.shape[dim], axis=dim)
        cells = jnp.concatenate(
            [
                lax.ppermute(tail, axis, [(i, (i + 1) % count) for i in range(count)]),
                cells,
                lax.ppermute(head, axis, [((i + 1) % count, i) for i in range(count)]),
            ],
            axis=dim,
        )
    return cells


def force_rows(padded, coldness):
    centre = padded[1:-1]
    beside_all = padded[:-2] + padded[2:] + (jnp.roll(centre, 1, 1) + jnp.roll(centre, -1, 1))
    return coldness * (
        -2.0 * hopping * beside_all
        + 2.0 * centre
        + 4.0 * quartic * centre * (centre * centre - 1.0)
    )


def site_terms(padded, margin, strip_rows):
    values = padded[margin : margin + strip_rows]
    lower_row = padded[margin + 1 : margin + 1 + strip_rows]
    neighbours = lower_row + jnp.roll(values, -1, 1)
    squared = values * values
    return (
        -2.0 * hopping * values * neighbours + squared + quartic * (squared - 1.0) * (squared - 1.0)
    )


def trim_rows(values, margin, target):
    excess = margin - target
    return values[excess : values.shape[0] - excess]


def info_rows(label_value, action, members, lanes):
    pair = jnp.concatenate((label_value[None], action))
    front = jnp.broadcast_to(pair[None, None, :], (members, 1, 2))
    return jnp.concatenate((front, jnp.zeros((members, 1, lanes - 2), jnp.float32)), 2)


def body(field, momentum, labels, betas, accept, swap_pairs):
    strip_rows = field.shape[1]
    width = field.shape[2]
    ladder_index = jnp.arange(betas.shape[0], dtype=jnp.int32)
    chosen = ladder_index == labels[0]
    coldness = jnp.sum(jnp.where(chosen, betas, 0.0))
    new_label = jnp.sum(jnp.where(chosen, swap_pairs, 0))
    start_field = field[0]
    start_moment = momentum[0]
    current = start_field
    moment = start_moment
    margin = 0
    old_action = None
    new_action = None
    for leap_step in range(STEPS + 1):
        if margin == 0:
            stacked = with_halo(jnp.stack((current, moment)), (("dom", 1),), 3)
            current = stacked[0]
            moment = stacked[1]
            margin = 3
        padded = current
        outer = margin
        if leap_step == 0:
            old_action = site_terms(padded, outer, strip_rows)
        if leap_step == STEPS:
            new_action = site_terms(padded, outer, strip_rows)
        force_now = force_rows(padded, coldness)
        moment = trim_rows(moment, margin, outer - 1)
        current = trim_rows(padded, outer, outer - 1)
        margin = outer - 1
        factor = 0.5 * step_size if leap_step == 0 or leap_step == STEPS else step_size
        moment = moment - factor * force_now
        if leap_step < STEPS:
            current = current + step_size * moment
    change_part = jnp.sum(
        0.5 * moment * moment
        + coldness * new_action
        - (0.5 * start_moment * start_moment + coldness * old_action)
    )
    accepted = accept[0] == 1
    action_part = jnp.where(accepted, jnp.sum(new_action), jnp.sum(old_action))
    field_out = jnp.where(accepted, current, start_field)
    label_value = new_label.astype(jnp.float32)
    change, action = lax.psum((change_part[None], action_part[None]), "dom")
    members = lax.axis_size("rep")
    blocks = field_out.reshape(members, -1, width)
    outgoing = jnp.concatenate((blocks, info_rows(label_value, action, members, width)), 1)
    spread = lax.all_to_all(
        outgoing.reshape(1, -1, width), "rep", split_axis=1, concat_axis=0, tiled=True
    )
    label_values = spread[:, -1, 0]
    actions = spread[:, -1, 1]
    received = spread[:, :-1]
    held_labels = label_values.astype(jnp.int32)
    onehot = held_labels[None, :] == ladder_index[:, None]
    holder = jnp.sum(jnp.where(onehot, ladder_index[None, :], 0), 1)
    sites_total = lax.axis_size("dom") * strip_rows * width
    ladder_all = jnp.sum(jnp.where(onehot, actions[None, :], 0.0), 1) / sites_total
    ladder = lax.dynamic_slice_in_dim(ladder_all, lax.axis_index("rep"), 1)
    ordered = jnp.take(received, holder, axis=0)
    returned = lax.all_to_all(ordered, "rep", split_axis=0, concat_axis=1, tiled=True)
    return (field_out[None], returned, new_label[None], change, ladder)


def solution(mesh):
    placed = (P("rep", "dom", None), P("rep", "dom", None), P("rep"), P(), P("rep"), P())
    return jax.shard_map(
        body,
        mesh=mesh,
        in_specs=placed,
        out_specs=(P("rep", "dom", None), P("rep", "dom", None), P("rep"), P("rep"), P("rep")),
        check_vma=False,
    )
```

profile of v0, /device:TPU:9, one launch (start us, length us, event | category | flops | bytes accessed | tf_op | source)
XLA Modules:
  0.0 129.3 jit_solution(5219297042923690402)
XLA Ops:
  0.6 1.4 %constant_dynamic-update-slice_fusion.1 = f32[2,128,2048]{2,1,0:T(8,128)S(1)} fusion(f32[1,128,2048]{2,1,0:T(8,128)} %param.6), kind=kLoop, calls=%fused_computation.139 | loop fusion | bytes 2097152
  2.0 0.1 copy-done.3
  2.3 1.3 %collective-permute-start.1 = (f32[2,3,2048]{2,1,0:T(4,128)S(1)}, f32[2,3,2048]{2,1,0:T(4,128)S(1)}, u32[]{:S(2)}, u32[]{:S(2)}) collective-permute-start(f32[2,3,2048]{2,1,0:T(4,128)S(1)} %get-tuple-element.33), channel_id=1, source_target_pairs={{1,0},{0,1},{3,2},{2,3},{5,4},{4,5},{7,6},{6,7},{9,8},{8,9},{11,10... | collective-permute-start | bytes 147464 | tf_op jit(solution)/shard_map/ppermute | solution.py:23
  3.6 0.2 collective-permute-start
  4.5 0.6 fusion.80
  5.1 0.4 collective-permute-done.1
  5.5 2.0 %collective-permute-done = f32[2,3,2048]{2,1,0:T(4,128)S(1)} collective-permute-done((f32[2,3,2048]{2,1,0:T(4,128)S(1)}, f32[2,3,2048]{2,1,0:T(4,128)S(1)}, u32[]{:S(2)}, u32[]{:S(2)}) %collective-permute-start) | collective-permute-done | bytes 49184 | tf_op jit(solution)/shard_map/ppermute | solution.py:21
  7.5 0.2 pad_maximum_fusion
  7.7 0.1 slice_bitcast_fusion.5
  7.9 0.4 fusion.109
  8.3 1.5 %multiply_add_fusion.5 = (f32[132,2048]{1,0:T(8,128)S(1)}, f32[132,2048]{1,0:T(8,128)S(1)}) fusion(f32[2,134,2048]{2,1,0:T(8,128)S(1)} %pad_maximum_fusion, f32[132,1]{1,0:T(8,128)S(1)} %get-tuple-element.70, f32[132,2047]{1,0:T(8,128)S(1)} %get-tuple-element.72, f32[132,2047]{1,0:T(8,128)S(1)} %get-tuple-element.71, f32[132,1]{1,0:T(8,128)S(1)} %get-tuple-element.69, ...), kind=kLoop, calls=%fused_computation.77 | loop fusion | flops 4866048 | bytes 8650756 | tf_op jit(solution)/shard_map/add | solution.py:94
  9.9 0.4 fusion.107
  10.3 0.1 fusion.106
  10.4 1.5 %multiply_add_fusion.4 = (f32[130,2048]{1,0:T(8,128)S(1)}, f32[130,2048]{1,0:T(8,128)S(1)}) fusion(f32[132,2048]{1,0:T(8,128)S(1)} %get-tuple-element.24, f32[130,1]{1,0:T(8,128)S(1)} %get-tuple-element.66, f32[130,2047]{1,0:T(8,128)S(1)} %get-tuple-element.68, f32[130,2047]{1,0:T(8,128)S(1)} %get-tuple-element.67, f32[130,1]{1,0:T(8,128)S(1)} %get-tuple-element.65, ...), kind=kLoop, calls=%fused_computation.76 | loop fusion | flops 4792320 | bytes 8519684 | tf_op jit(solution)/shard_map/add | solution.py:94
  11.9 0.4 fusion.105
  12.4 1.5 %add_bitcast_fusion.1 = (f32[1,128,2048]{2,1,0:T(8,128)S(1)}, f32[128,2048]{1,0:T(8,128)S(1)}) fusion(f32[130,2048]{1,0:T(8,128)S(1)} %get-tuple-element.22, f32[128,1]{1,0:T(8,128)S(1)} %get-tuple-element.62, f32[128,2047]{1,0:T(8,128)S(1)} %get-tuple-element.64, f32[128,2047]{1,0:T(8,128)S(1)} %get-tuple-element.63, f32[128,1]{1,0:T(8,128)S(1)} %get-tuple-element.61, ...), kind=kLoop, calls=%fused_computation.120 | loop fusion | flops 4718592 | bytes 8388612 | tf_op jit(solution)/shard_map/stack | solution.py:77
  13.9 0.5 collective-permute-start.2
  14.4 1.0 collective-permute-start.3
  15.4 1.6 %collective-permute-done.2 = f32[2,3,2048]{2,1,0:T(4,128)S(1)} collective-permute-done((f32[2,3,2048]{2,1,0:T(4,128)S(1)}, f32[2,3,2048]{2,1,0:T(4,128)S(1)}, u32[]{:S(2)}, u32[]{:S(2)}) %collective-permute-start.2) | collective-permute-done | bytes 49184 | tf_op jit(solution)/shard_map/ppermute | solution.py:21
  17.1 0.7 collective-permute-done.3
  17.8 0.3 pad_maximum_fusion.1
  18.1 0.1 slice_bitcast_fusion.3
  18.2 0.4 fusion.103
  18.7 1.5 %multiply_add_fusion.3 = (f32[132,2048]{1,0:T(8,128)S(1)}, f32[132,2048]{1,0:T(8,128)S(1)}) fusion(f32[2,134,2048]{2,1,0:T(8,128)S(1)} %pad_maximum_fusion.1, f32[132,1]{1,0:T(8,128)S(1)} %get-tuple-element.58, f32[132,2047]{1,0:T(8,128)S(1)} %get-tuple-element.60, f32[132,2047]{1,0:T(8,128)S(1)} %get-tuple-element.59, f32[132,1]{1,0:T(8,128)S(1)} %get-tuple-element.57, ...), kind=kLoop, calls=%fused_computation.75 | loop fusion | flops 4866048 | bytes 8650756 | tf_op jit(solution)/shard_map/add | solution.py:94
  20.2 0.4 fusion.101
  20.6 0.1 fusion.100
  20.7 1.5 %multiply_add_fusion.2 = (f32[130,2048]{1,0:T(8,128)S(1)}, f32[130,2048]{1,0:T(8,128)S(1)}) fusion(f32[132,2048]{1,0:T(8,128)S(1)} %get-tuple-element.18, f32[130,1]{1,0:T(8,128)S(1)} %get-tuple-element.54, f32[130,2047]{1,0:T(8,128)S(1)} %get-tuple-element.56, f32[130,2047]{1,0:T(8,128)S(1)} %get-tuple-element.55, f32[130,1]{1,0:T(8,128)S(1)} %get-tuple-element.53, ...), kind=kLoop, calls=%fused_computation.74 | loop fusion | flops 4792320 | bytes 8519684 | tf_op jit(solution)/shard_map/add | solution.py:94
  22.3 0.4 fusion.99
  22.8 1.5 %add_bitcast_fusion = (f32[1,128,2048]{2,1,0:T(8,128)S(1)}, f32[128,2048]{1,0:T(8,128)S(1)}) fusion(f32[130,2048]{1,0:T(8,128)S(1)} %get-tuple-element.16, f32[128,1]{1,0:T(8,128)S(1)} %get-tuple-element.50, f32[128,2047]{1,0:T(8,128)S(1)} %get-tuple-element.52, f32[128,2047]{1,0:T(8,128)S(1)} %get-tuple-element.51, f32[128,1]{1,0:T(8,128)S(1)} %get-tuple-element.49, ...), kind=kLoop, calls=%fused_computation.119 | loop fusion | flops 4718592 | bytes 8388612 | tf_op jit(solution)/shard_map/stack | solution.py:77
  24.3 0.9 copy-done.1
  25.2 0.3 copy-done.2
  25.6 0.8 collective-permute-start.4
  26.3 0.7 collective-permute-start.5
  27.0 0.6 fusion.81
  27.7 1.3 %slice.515 = f32[128,2047]{1,0:T(8,128)} slice(f32[128,2048]{1,0:T(8,128)S(1)} %bitcast.130), slice={[0:128], [1:2048]} | slice | bytes 2096128 | tf_op jit(solution)/shard_map/jit(_roll_static)/slice | solution.py:43
  30.3 1.9 %pad_maximum_fusion.2 = f32[2,134,2048]{2,1,0:T(8,128)S(1)} fusion(f32[2,3,2048]{2,1,0:T(4,128)S(1)} %collective-permute-done.5, f32[1,128,2048]{2,1,0:T(8,128)} %bitcast.133, f32[1,128,2048]{2,1,0:T(8,128)} %copy-done.1, f32[2,3,2048]{2,1,0:T(4,128)S(1)} %collective-permute-done.4), kind=kLoop, calls=%fused_computation.3 | loop fusion | flops 1646592 | bytes 4390912 | tf_op jit(solution)/shard_map/concatenate | solution.py:19
  32.2 0.1 slice_bitcast_fusion.1
  32.3 0.4 fusion.97
  32.8 1.5 %multiply_add_fusion.1 = (f32[132,2048]{1,0:T(8,128)S(1)}, f32[132,2048]{1,0:T(8,128)S(1)}) fusion(f32[2,134,2048]{2,1,0:T(8,128)S(1)} %pad_maximum_fusion.2, f32[132,1]{1,0:T(8,128)S(1)} %get-tuple-element.46, f32[132,2047]{1,0:T(8,128)S(1)} %get-tuple-element.48, f32[132,2047]{1,0:T(8,128)S(1)} %get-tuple-element.47, f32[132,1]{1,0:T(8,128)S(1)} %get-tuple-element.45, ...), kind=kLoop, calls=%fused_computation.73 | loop fusion | flops 4866048 | bytes 8650756 | tf_op jit(solution)/shard_map/add | solution.py:94
  34.3 0.4 fusion.95
  34.7 0.1 fusion.94
  34.8 1.7 %multiply_add_fusion = (f32[130,2048]{1,0:T(8,128)S(1)}, f32[130,2048]{1,0:T(8,128)S(1)}) fusion(f32[132,2048]{1,0:T(8,128)S(1)} %get-tuple-element.12, f32[130,1]{1,0:T(8,128)S(1)} %get-tuple-element.42, f32[130,2047]{1,0:T(8,128)S(1)} %get-tuple-element.44, f32[130,2047]{1,0:T(8,128)S(1)} %get-tuple-element.43, f32[130,1]{1,0:T(8,128)S(1)} %get-tuple-element.41, ...), kind=kLoop, calls=%fused_computation.72 | loop fusion | flops 4792320 | bytes 8519684 | tf_op jit(solution)/shard_map/add | solution.py:94
  36.6 0.4 fusion.92
  37.0 0.7 copy-done.4
  37.8 0.3 copy-done.5
  38.1 4.7 %fusion.77 = (f32[16,8,2048]{2,1,0:T(8,128)}, f32[1,128,2048]{2,1,0:T(8,128)}, f32[]{:T(128)}, f32[]{:T(128)}, f32[]{:T(128)}) fusion(f32[130,2048]{1,0:T(8,128)S(1)} %get-tuple-element.10, pred[]{:T(512)} %bitcast, f32[1,128,2048]{2,1,0:T(8,128)S(1)} %copy-done, f32[1,128,2048]{2,1,0:T(8,128)S(1)} %copy-done.4, f32[128,1]{1,0:T(8,128)S(1)} %get-tuple-element.39, ...), kind=kLoop, calls=%fused_computation.123 | loop fusion | flops 12320765 | bytes 13680657 | tf_op jit(solution)/shard_map/reshape | solution.py:106
  44.0 4.9 %all-reduce.1 = (f32[1]{0:T(128)}, f32[1]{0:T(128)}) all-reduce(f32[1]{0:T(128)} %bitcast.20, f32[1]{0:T(128)} %bitcast.26), channel_id=1, replica_groups=mesh['rep'=16,'dom'=2] {'dom'}, use_global_device_ids=true, to_apply=%region_4.5 | all-reduce | flops 2 | bytes 16 | tf_op jit(solution)/shard_map/psum | solution.py:104
  48.9 0.7 select_maximum_fusion
  49.7 1.5 %pad_maximum_fusion.3 = f32[16,9,2048]{2,1,0:T(8,128)S(1)} fusion(f32[16,1,2048]{2,1,0:T(1,128)S(1)} %concatenate.111, f32[16,8,2048]{2,1,0:T(8,128)} %get-tuple-element.26), kind=kLoop, calls=%fused_computation.4 | loop fusion | flops 294912 | bytes 2359296 | tf_op jit(solution)/shard_map/concatenate | solution.py:107
  51.2 1.4 %reshape.79 = f32[1,144,2048]{2,0,1:T(1,128)S(1)} reshape(f32[16,9,2048]{2,1,0:T(8,128)S(1)} %pad_maximum_fusion.3) | data formatting | bytes 2359296 | tf_op jit(solution)/shard_map/reshape | solution.py:109
  52.6 38.6 %all_to_all.24 = f32[1,144,2048]{2,0,1:T(1,128)S(1)} all-to-all(f32[1,144,2048]{2,0,1:T(1,128)S(1)} %reshape.79), channel_id=1, replica_groups=mesh['rep'=16,'dom'=2] {'rep'}, dimensions={1} | all-to-all | bytes 2359296 | tf_op jit(solution)/shard_map/all_to_all | solution.py:108
  91.2 2.8 %reduce = f32[144,2048]{1,0:T(8,128)S(1)} reduce(f32[1,144,2048]{2,0,1:T(1,128)S(1)} %all_to_all.24, f32[]{:T(128)} %constant.76), dimensions={0}, to_apply=%all_to_all.8.reduce_sub_computation | reduce | bytes 2359300 | tf_op jit(solution)/shard_map/all_to_all | solution.py:108
  94.0 0.2 all_to_all.9
  94.2 0.4 fusion.79
  94.5 1.0 slice.518
  95.6 0.1 select_reduce_fusion.1
  95.7 1.8 %gather_fusion = f32[16,8,2048]{2,1,0:T(8,128)S(1)} fusion(f32[16,8,2048]{2,1,0:T(8,128)} %slice.518, s32[1024]{0:T(1024)S(1)} %pad_clamp_fusion), kind=kCustom, calls=%fused_computation | custom fusion | bytes 2097216 | tf_op jit(solution)/shard_map/jit(_take)/gather | solution.py:120
  97.6 1.1 broadcast_select_fusion
  98.7 4.7 %all-to-all-start.1 = ((f32[16,8,2048]{2,1,0:T(8,128)}), f32[16,8,2048]{2,1,0:T(8,128)S(1)}, u32[]{:S(2)}, u32[]{:S(2)}) async-start(f32[16,8,2048]{2,1,0:T(8,128)} %broadcast_select_fusion), calls=%async_computation.1 | async-start | bytes 2097152 | tf_op jit(solution)/shard_map/all_to_all | solution.py:121
  103.4 0.3 slice_reduce_fusion
  103.6 0.1 select_reduce_fusion
  103.8 0.6 dynamic_slice.3
  104.4 23.9 %all-to-all-done.1 = f32[16,8,2048]{2,1,0:T(8,128)S(1)} async-done(((f32[16,8,2048]{2,1,0:T(8,128)}), f32[16,8,2048]{2,1,0:T(8,128)S(1)}, u32[]{:S(2)}, u32[]{:S(2)}) %all-to-all-start.1) | async-done | bytes 1048608 | tf_op jit(solution)/shard_map/all_to_all | solution.py:121
  128.3 1.0 copy.19
  (29 shorter events, 0.8 us)
Async XLA Ops:
  0.6 1.5 %copy-start.3 = (f32[1,128,2048]{2,1,0:T(8,128)S(1)}, f32[1,128,2048]{2,1,0:T(8,128)}, u32[]{:S(2)}) copy-start(f32[1,128,2048]{2,1,0:T(8,128)} %param.7) | copy-start | bytes 3145732
  2.2 2.3 %copy-start.6 = (f32[16]{0:T(128)S(1)}, f32[16]{0:T(128)}, u32[]{:S(2)}) copy-start(f32[16]{0:T(128)} %param.9) | copy-start | bytes 196
  2.3 3.2 %collective-permute-start.1 = (f32[2,3,2048]{2,1,0:T(4,128)S(1)}, f32[2,3,2048]{2,1,0:T(4,128)S(1)}, u32[]{:S(2)}, u32[]{:S(2)}) collective-permute-start(f32[2,3,2048]{2,1,0:T(4,128)S(1)} %get-tuple-element.33), channel_id=1, source_target_pairs={{1,0},{0,1},{3,2},{2,3},{5,4},{4,5},{7,6},{6,7},{9,8},{8,9},{11,10... | collective-permute-start | bytes 147464 | tf_op jit(solution)/shard_map/ppermute | solution.py:23
  3.6 3.9 %collective-permute-start = (f32[2,3,2048]{2,1,0:T(4,128)S(1)}, f32[2,3,2048]{2,1,0:T(4,128)S(1)}, u32[]{:S(2)}, u32[]{:S(2)}) collective-permute-start(f32[2,3,2048]{2,1,0:T(4,128)S(1)} %get-tuple-element.32), channel_id=1, source_target_pairs={{0,1},{1,0},{2,3},{3,2},{4,5},{5,4},{6,7},{7,6},{8,9},{9,8},{10,11... | collective-permute-start | bytes 147464 | tf_op jit(solution)/shard_map/ppermute | solution.py:21
  13.9 3.2 %collective-permute-start.2 = (f32[2,3,2048]{2,1,0:T(4,128)S(1)}, f32[2,3,2048]{2,1,0:T(4,128)S(1)}, u32[]{:S(2)}, u32[]{:S(2)}) collective-permute-start(f32[2,3,2048]{2,1,0:T(4,128)S(1)} %get-tuple-element.30), channel_id=1, source_target_pairs={{0,1},{1,0},{2,3},{3,2},{4,5},{5,4},{6,7},{7,6},{8,9},{9,8},{10,11... | collective-permute-start | bytes 147464 | tf_op jit(solution)/shard_map/ppermute | solution.py:21
  14.4 3.3 %collective-permute-start.3 = (f32[2,3,2048]{2,1,0:T(4,128)S(1)}, f32[2,3,2048]{2,1,0:T(4,128)S(1)}, u32[]{:S(2)}, u32[]{:S(2)}) collective-permute-start(f32[2,3,2048]{2,1,0:T(4,128)S(1)} %get-tuple-element.31), channel_id=1, source_target_pairs={{1,0},{0,1},{3,2},{2,3},{5,4},{4,5},{7,6},{6,7},{9,8},{8,9},{11,10... | collective-permute-start | bytes 147464 | tf_op jit(solution)/shard_map/ppermute | solution.py:23
  24.2 1.0 copy-start.1
  24.2 1.3 %copy-start.2 = (f32[128,2048]{1,0:T(8,128)}, f32[128,2048]{1,0:T(8,128)S(1)}, u32[]{:S(2)}) copy-start(f32[128,2048]{1,0:T(8,128)S(1)} %get-tuple-element.15) | copy-start | bytes 3145732
  24.3 2.8 %copy-start.7 = (s32[16]{0:T(128)S(1)}, s32[16]{0:T(128)}, u32[]{:S(2)}) copy-start(s32[16]{0:T(128)} %param.11) | copy-start | bytes 196
  24.3 3.4 %copy-start = (f32[1,128,2048]{2,1,0:T(8,128)S(1)}, f32[1,128,2048]{2,1,0:T(8,128)}, u32[]{:S(2)}) copy-start(f32[1,128,2048]{2,1,0:T(8,128)} %param.6) | copy-start | bytes 3145732
  25.6 4.7 %collective-permute-start.4 = (f32[2,3,2048]{2,1,0:T(4,128)S(1)}, f32[2,3,2048]{2,1,0:T(4,128)S(1)}, u32[]{:S(2)}, u32[]{:S(2)}) collective-permute-start(f32[2,3,2048]{2,1,0:T(4,128)S(1)} %get-tuple-element.28), channel_id=1, source_target_pairs={{0,1},{1,0},{2,3},{3,2},{4,5},{5,4},{6,7},{7,6},{8,9},{9,8},{10,11... | collective-permute-start | bytes 147464 | tf_op jit(solution)/shard_map/ppermute | solution.py:21
  26.3 4.0 %collective-permute-start.5 = (f32[2,3,2048]{2,1,0:T(4,128)S(1)}, f32[2,3,2048]{2,1,0:T(4,128)S(1)}, u32[]{:S(2)}, u32[]{:S(2)}) collective-permute-start(f32[2,3,2048]{2,1,0:T(4,128)S(1)} %get-tuple-element.29), channel_id=1, source_target_pairs={{1,0},{0,1},{3,2},{2,3},{5,4},{4,5},{7,6},{6,7},{9,8},{8,9},{11,10... | collective-permute-start | bytes 147464 | tf_op jit(solution)/shard_map/ppermute | solution.py:23
  36.5 1.2 copy-start.4
  36.5 1.5 %copy-start.5 = (f32[128,2047]{1,0:T(8,128)S(1)}, f32[128,2047]{1,0:T(8,128)}, u32[]{:S(2)}) copy-start(f32[128,2047]{1,0:T(8,128)} %slice.515) | copy-start | bytes 3144196
  98.7 29.6 %all-to-all-start.1 = ((f32[16,8,2048]{2,1,0:T(8,128)}), f32[16,8,2048]{2,1,0:T(8,128)S(1)}, u32[]{:S(2)}, u32[]{:S(2)}) async-start(f32[16,8,2048]{2,1,0:T(8,128)} %broadcast_select_fusion), calls=%async_computation.1 | async-start | bytes 2097152 | tf_op jit(solution)/shard_map/all_to_all | solution.py:121
where the time goes:
time: 130 us; the launch traced here: 129 us
  blocking collectives  43.5 us (33%)
  waiting for transfers between devices  28.7 us (22%)
  other arithmetic  27.5 us (21%)
  local copies, waits for them, and re-layouts  16.2 us (12%)
  starting transfers between devices  9.18 us (7%)
  between operations  4.24 us (3%)
    all_to_all x1, blocking collectives, body(): lax.all_to_all(outgoing.reshape(1, -1, width), 'rep', split_axis=1, conca...  38.6 us
    all_to_all x1, waiting for transfers between devices, body(): lax.all_to_all(ordered, 'rep', split_axis=0, concat_axis=1, tiled=True)  23.9 us
    add x6, other arithmetic, body(): current = current + step_size * moment  9.39 us
    psum x1, blocking collectives, body(): change, action = lax.psum((change_part[None], action_part[None]), 'dom')  4.91 us
    unnamed x18, local copies, waits for them, and re-layouts  4.81 us
    reshape x1, other arithmetic, body(): blocks = field_out.reshape(members, -1, width)  4.67 us
    all_to_all x1, starting transfers between devices, body(): lax.all_to_all(ordered, 'rep', split_axis=0, concat_axis=1, tiled=True)  4.66 us
    slice x16, local copies, waits for them, and re-layouts, force_rows(): jnp.roll(centre, 1, 1) + jnp.roll(centre, -1, 1)  3.78 us
  transfers between devices with their start and end apart: 7, of which 5 were waited for; matrix products, arithmetic and copies ran while one was open for 3% of the time, Pallas kernels for 0%

commit v1 on v0

v1 whole, which is shorter than its diff:
```python
import functools

import jax
import jax.numpy as jnp
from jax import lax
from jax.experimental import pallas as pl
from jax.experimental.pallas import tpu as pltpu
from jax.sharding import PartitionSpec as P

STEPS = 8
hopping = 0.18
quartic = 0.3
step_size = 0.05

SUB = 8
LANES = 128
LINEAR = (1.0 - 2.0 * quartic) / hopping
CUBIC = 2.0 * quartic / hopping


def tile(ref, row, col):
    return ref[pl.ds(row, SUB), pl.ds(col * LANES, LANES)]


def lane_index():
    return lax.broadcasted_iota(jnp.int32, (SUB, LANES), 1)


def beside(values, lane):
    count = len(values)
    ahead = [pltpu.roll(v, 1, 1) for v in values]
    back = [pltpu.roll(v, LANES - 1, 1) for v in values]
    left = [jnp.where(lane == 0, ahead[i - 1], ahead[i]) for i in range(count)]
    right = [jnp.where(lane == LANES - 1, back[(i + 1) % count], back[i]) for i in range(count)]
    return [a + b for a, b in zip(left, right)], right


def pull(total, value):
    return total - value * (LINEAR + CUBIC * (value * value))


def pack_kernel(scale_ref, head_ref, tail_ref, head_m_ref, tail_m_ref, out_ref):
    inverse = scale_ref[1]
    lane = lane_index()
    row = lax.broadcasted_iota(jnp.int32, (SUB, LANES), 0)
    tiles = head_ref.shape[1] // LANES
    for side, ref, m_ref in ((0, head_ref, head_m_ref), (1, tail_ref, tail_m_ref)):
        base = 0 if side == 0 else SUB
        inner = SUB - base
        values = [tile(ref, base, i) for i in range(tiles)]
        others = [tile(ref, inner, i) for i in range(tiles)]
        sums, _ = beside(values, lane)
        for i in range(tiles):
            up = pltpu.roll(values[i], 1, 0)
            down = pltpu.roll(values[i], SUB - 1, 0)
            if side == 0:
                up = jnp.where(row == 0, 0.0, up)
                down = jnp.where(row == SUB - 1, pltpu.roll(others[i], SUB - 1, 0), down)
            else:
                up = jnp.where(row == 0, pltpu.roll(others[i], 1, 0), up)
                down = jnp.where(row == SUB - 1, 0.0, down)
            kick = m_ref[:, pl.ds(i * LANES, LANES)] * inverse + 0.5 * pull(
                (up + down) + sums[i], values[i]
            )
            out_ref[side, 0, :, pl.ds(i * LANES, LANES)] = values[i]
            out_ref[side, 1, :, pl.ds(i * LANES, LANES)] = kick


def path_kernel(
    per_member,
    scale_ref,
    field_ref,
    momentum_ref,
    above_ref,
    below_ref,
    out_ref,
    send_ref,
    first,
    second,
    push,
    energy,
):
    cold = scale_ref[0]
    inverse = scale_ref[1]
    unit = scale_ref[2]
    drift = scale_ref[3]
    label = scale_ref[4]
    accepted = scale_ref[5] > 0.5
    rows, width = field_ref.shape
    tiles = width // LANES
    blocks = rows // SUB
    lane = lane_index()
    sub = lax.broadcasted_iota(jnp.int32, (SUB, LANES), 0)
    own = 2 * SUB
    end = own + rows

    def load(i, carry):
        row = pl.multiple_of(i * SUB, SUB)
        for t in range(tiles):
            first[t, pl.ds(own + row, SUB), :] = tile(field_ref, row, t)
        return carry

    lax.fori_loop(0, blocks, load, 0)
    zero = jnp.zeros((SUB, LANES), jnp.float32)
    for t in range(tiles):
        cols = pl.ds(t * LANES, LANES)
        for ref, row in ((above_ref, SUB), (below_ref, end)):
            first[t, row : row + SUB, :] = ref[0, :, cols]
        for row in (0, end + SUB):
            first[t, row : row + SUB, :] = zero
            second[t, row : row + SUB, :] = zero
        top = first[t, own : own + SUB, :]
        low = first[t, end - SUB : end, :]
        for ref, row, mine in (
            (above_ref, SUB, jnp.where(sub == SUB - 1, pltpu.roll(top, SUB - 1, 0), 0.0)),
            (below_ref, end, jnp.where(sub == 0, pltpu.roll(low, 1, 0), 0.0)),
        ):
            kick = ref[1, :, cols] + 0.5 * mine
            push[t, row : row + SUB, :] = kick
            second[t, row : row + SUB, :] = ref[0, :, cols] + drift * kick

    def site(value, down, right):
        squared = value * value
        return (-2.0 * hopping) * value * (down + right) + (
            squared + quartic * (squared - 1.0) * (squared - 1.0)
        )

    def begin(i, total):
        row = pl.multiple_of(own + i * SUB, SUB)
        source = pl.multiple_of(i * SUB, SUB)
        values = [first[t, pl.ds(row, SUB), :] for t in range(tiles)]
        sums, right = beside(values, lane)
        for t in range(tiles):
            up = first[t, pl.ds(row - 1, SUB), :]
            down = first[t, pl.ds(row + 1, SUB), :]
            moment = tile(momentum_ref, source, t)
            action = site(values[t], down, right[t])
            energy[t, pl.ds(source, SUB), :] = 0.5 * moment * moment + cold * action
            total = total + action
            kick = moment * inverse + 0.5 * pull((up + down) + sums[t], values[t])
            push[t, pl.ds(row, SUB), :] = kick
            second[t, pl.ds(row, SUB), :] = values[t] + drift * kick
        return total

    old_action = lax.fori_loop(0, blocks, begin, zero)

    def sweep(before, after):
        def one(i, carry):
            row = pl.multiple_of(SUB + i * SUB, SUB)
            values = [before[t, pl.ds(row, SUB), :] for t in range(tiles)]
            sums, _ = beside(values, lane)
            for t in range(tiles):
                up = before[t, pl.ds(row - 1, SUB), :]
                down = before[t, pl.ds(row + 1, SUB), :]
                kick = push[t, pl.ds(row, SUB), :] + pull((up + down) + sums[t], values[t])
                push[t, pl.ds(row, SUB), :] = kick
                after[t, pl.ds(row, SUB), :] = values[t] + drift * kick
            return carry

        lax.fori_loop(0, blocks + 2, one, 0)

    for leap in range(STEPS - 1):
        before, after = (second, first) if leap % 2 == 0 else (first, second)
        sweep(before, after)
    last = second if (STEPS - 1) % 2 == 0 else first

    def finish(i, carry):
        change, total = carry
        row = pl.multiple_of(own + i * SUB, SUB)
        source = pl.multiple_of(i * SUB, SUB)
        values = [last[t, pl.ds(row, SUB), :] for t in range(tiles)]
        sums, right = beside(values, lane)
        for t in range(tiles):
            up = last[t, pl.ds(row - 1, SUB), :]
            down = last[t, pl.ds(row + 1, SUB), :]
            kick = push[t, pl.ds(row, SUB), :] + 0.5 * pull((up + down) + sums[t], values[t])
            moment = unit * kick
            action = site(values[t], down, right[t])
            total = total + action
            change = change + (
                (0.5 * moment * moment + cold * action) - energy[t, pl.ds(source, SUB), :]
            )
            chosen = jnp.where(accepted, values[t], tile(field_ref, source, t))
            out_ref[pl.ds(source, SUB), pl.ds(t * LANES, LANES)] = chosen
            member = i * (tiles // per_member) + t // per_member
            send_ref[member, :, pl.ds((t % per_member) * LANES, LANES)] = chosen
        return change, total

    change, new_action = lax.fori_loop(0, blocks, finish, (zero, zero))
    action = jnp.sum(jnp.where(accepted, new_action, old_action))
    change = jnp.sum(change)
    note = jnp.where(lane == 0, label, jnp.where(lane == 1, action, jnp.where(lane == 2, change, 0.0)))

    def annotate(m, carry):
        send_ref[m, :, pl.ds(per_member * LANES, LANES)] = note
        return carry

    lax.fori_loop(0, send_ref.shape[0], annotate, 0)


def place_kernel(got_ref, out_ref, note_ref, labels_ref, sem, note_sem):
    members, _, width = out_ref.shape
    for r in range(members):
        note_ref[r : r + 1, :] = got_ref[r, 0:1, width:]
    fetch = pltpu.make_async_copy(note_ref, labels_ref, note_sem)
    fetch.start()
    fetch.wait()
    copies = []
    for r in range(members):
        slot = labels_ref[r, 0].astype(jnp.int32)
        copy = pltpu.make_async_copy(got_ref.at[r, :, pl.ds(0, width)], out_ref.at[slot], sem.at[r])
        copy.start()
        copies.append(copy)
    for copy in copies:
        copy.wait()


def body(field, momentum, labels, betas, accept, swap_pairs):
    rows = field.shape[1]
    width = field.shape[2]
    members = lax.axis_size("rep")
    strips = lax.axis_size("dom")
    tiles = width // LANES
    per_member = (rows // SUB) * tiles // members
    ladder_index = jnp.arange(betas.shape[0], dtype=jnp.int32)
    chosen = ladder_index == labels[0]
    cold = jnp.sum(jnp.where(chosen, betas, 0.0))
    new_label = jnp.sum(jnp.where(chosen, swap_pairs, 0))
    unit = 2.0 * hopping * step_size * cold
    scale = jnp.stack(
        (
            cold,
            1.0 / unit,
            unit,
            step_size * unit,
            new_label.astype(jnp.float32),
            accept[0].astype(jnp.float32),
        )
    )
    start = field[0]
    moment = momentum[0]
    smem = pl.BlockSpec(memory_space=pltpu.SMEM)
    vmem = pl.BlockSpec(memory_space=pltpu.VMEM)
    last16 = rows // (2 * SUB) - 1
    last8 = rows // SUB - 1
    edges = pl.pallas_call(
        pack_kernel,
        grid=(1,),
        out_shape=jax.ShapeDtypeStruct((2, 2, SUB, width), jnp.float32),
        in_specs=[
            smem,
            pl.BlockSpec((2 * SUB, width), lambda i: (0, 0)),
            pl.BlockSpec((2 * SUB, width), lambda i: (last16, 0)),
            pl.BlockSpec((SUB, width), lambda i: (0, 0)),
            pl.BlockSpec((SUB, width), lambda i: (last8, 0)),
        ],
        out_specs=pl.BlockSpec((2, 2, SUB, width), lambda i: (0, 0, 0, 0)),
    )(scale, start, start, moment, moment)
    forward = [(i, (i + 1) % strips) for i in range(strips)]
    backward = [((i + 1) % strips, i) for i in range(strips)]
    if strips == 2:
        edges = lax.ppermute(edges, "dom", forward)
        above, below = edges[1], edges[0]
    else:
        above = lax.ppermute(edges[1], "dom", forward)
        below = lax.ppermute(edges[0], "dom", backward)
    state = pltpu.VMEM((tiles, rows + 4 * SUB, LANES), jnp.float32)
    field_out, outgoing = pl.pallas_call(
        functools.partial(path_kernel, per_member),
        out_shape=(
            jax.ShapeDtypeStruct((rows, width), jnp.float32),
            jax.ShapeDtypeStruct((members, SUB, (per_member + 1) * LANES), jnp.float32),
        ),
        in_specs=[smem, vmem, vmem, vmem, vmem],
        out_specs=(vmem, vmem),
        scratch_shapes=[state, state, state, pltpu.VMEM((tiles, rows, LANES), jnp.float32)],
    )(scale, start, moment, above, below)
    received = lax.all_to_all(outgoing, "rep", split_axis=0, concat_axis=0, tiled=True)
    piece = per_member * LANES
    ordered, notes = pl.pallas_call(
        place_kernel,
        out_shape=(
            jax.ShapeDtypeStruct((members, SUB, piece), jnp.float32),
            jax.ShapeDtypeStruct((members, LANES), jnp.float32),
        ),
        in_specs=[vmem],
        out_specs=(pl.BlockSpec(memory_space=pl.ANY), vmem),
        scratch_shapes=[
            pltpu.SMEM((members, LANES), jnp.float32),
            pltpu.SemaphoreType.DMA((members,)),
            pltpu.SemaphoreType.DMA,
        ],
    )(received)
    returned = lax.all_to_all(ordered, "rep", split_axis=0, concat_axis=0, tiled=True)
    whole = width // piece
    returned = returned.reshape(rows // SUB, whole, SUB, piece).transpose(0, 2, 1, 3)
    returned = returned.reshape(1, rows, width)
    sums = notes
    passing = notes
    for _ in range(strips - 1):
        passing = lax.ppermute(passing, "dom", forward)
        sums = sums + passing
    me = lax.axis_index("rep")
    held_labels = notes[:, 0].astype(jnp.int32)
    sites = strips * rows * width
    ladder = jnp.sum(jnp.where(held_labels == me, sums[:, 1], 0.0)) / sites
    change = jnp.sum(jnp.where(ladder_index == me, sums[:, 2], 0.0))
    return (field_out[None], returned, new_label[None], change[None], ladder[None])


def solution(mesh):
    placed = (P("rep", "dom", None), P("rep", "dom", None), P("rep"), P(), P("rep"), P())
    return jax.shard_map(
        body,
        mesh=mesh,
        in_specs=placed,
        out_specs=(P("rep", "dom", None), P("rep", "dom", None), P("rep"), P("rep"), P("rep")),
        check_vma=False,
    )
```

time: 130 us -> 110 us (0.85)
  Pallas kernels: 0 us -> 26.8 us
  other arithmetic: 27.5 us -> 3.84 us
  local copies, waits for them, and re-layouts: 16.2 us -> 2.92 us
  blocking collectives: 43.5 us -> 34.7 us
  starting transfers between devices: 9.18 us -> 7.4 us
  between operations: 4.24 us -> 5.73 us
    pallas_call x0 -> x3, Pallas kernels: none -> 26.8 us  [the longest x1 21.3 us: body(): pl.pallas_call(functools.partial(path_kernel, per_member), out_shape=(jax...]
    add x6 -> x1, other arithmetic: 9.39 us -> 0.01 us  [body(): sums = sums + passing]
    slice x26 -> x0, local copies, waits for them, and re-layouts: 7.22 us -> none  [the longest x16 3.78 us: force_rows(): jnp.roll(centre, 1, 1) + jnp.roll(centre, -1, 1)]
    psum x1 -> x0, blocking collectives: 4.91 us -> none  [body(): change, action = lax.psum((change_part[None], action_part[None]), 'dom')]
    reshape x1 -> x0, other arithmetic: 4.67 us -> none  [body(): blocks = field_out.reshape(members, -1, width)]
    concatenate x5 -> x0, other arithmetic: 4.63 us -> none  [the longest x3 2.46 us: with_halo(): jnp.concatenate([lax.ppermute(tail, axis, [(i, (i + 1) % count) for i in...]
    all_to_all x1, blocking collectives: 38.6 us -> 34.7 us  [body(): lax.all_to_all(outgoing, 'rep', split_axis=0, concat_axis=0, tiled=True)]
    unnamed x18 -> x3, local copies, waits for them, and re-layouts: 4.81 us -> 0.97 us
  transfers between devices with their start and end apart: 7 -> 3, of which waited for: 5 -> 3; matrix products, arithmetic and copies ran while one was open for 3% -> 1% of each run, Pallas kernels for 0% -> 0%
where the time goes in v1:
time: 110 us; the launch traced here: 109 us
  blocking collectives  34.7 us (32%)
  waiting for transfers between devices  27.9 us (25%)
  Pallas kernels  26.8 us (24%)
  starting transfers between devices  7.4 us (7%)
  between operations  5.73 us (5%)
  other arithmetic  3.84 us (3%)
  local copies, waits for them, and re-layouts  2.92 us (3%)
    all_to_all x1, blocking collectives, body(): lax.all_to_all(outgoing, 'rep', split_axis=0, concat_axis=0, tiled=True)  34.7 us
    pallas_call x1, Pallas kernels, body(): pl.pallas_call(functools.partial(path_kernel, per_member), out_shape=(jax...  21.3 us
    all_to_all x1, waiting for transfers between devices, body(): lax.all_to_all(ordered, 'rep', split_axis=0, concat_axis=0, tiled=True)  20.1 us
    ppermute x1, waiting for transfers between devices, body(): edges = lax.ppermute(edges, 'dom', forward)  6.16 us
    all_to_all x1, starting transfers between devices, body(): lax.all_to_all(ordered, 'rep', split_axis=0, concat_axis=0, tiled=True)  4.86 us
    pallas_call x1, Pallas kernels, body(): pl.pallas_call(place_kernel, out_shape=(jax.ShapeDtypeStruct((members, SU...  3.61 us
  transfers between devices with their start and end apart: 3, of which 3 were waited for; matrix products, arithmetic and copies ran while one was open for 1% of the time, Pallas kernels for 0%

profile of v1, /device:TPU:9, one launch (start us, length us, event | category | flops | bytes accessed | tf_op | source)
XLA Modules:
  0.0 109.2 jit_solution(14293317979392604795)
XLA Ops:
  1.3 1.3 %fusion.1 = f32[]{:T(128)} fusion(f32[16]{0:T(128)} %param.9, s32[]{:T(128)} %bitcast.17), kind=kLoop, calls=%fused_computation.9 | loop fusion | flops 47 | bytes 72 | tf_op jit(solution)/shard_map/reduce_sum | solution.py:227
  3.8 1.3 %fusion.2 = s32[]{:T(128)} fusion(s32[16]{0:T(128)} %param.11, s32[]{:T(128)} %bitcast.18), kind=kLoop, calls=%fused_computation.10 | loop fusion | flops 47 | bytes 72 | tf_op jit(solution)/shard_map/reduce_sum | solution.py:228
  6.5 1.2 %stack.24.scale_ref = f32[6]{0:T(128)} concatenate(f32[1]{0:T(128)} %bitcast.1, f32[1]{0:T(128)} %bitcast.2, f32[1]{0:T(128)} %bitcast.3, f32[1]{0:T(128)} %bitcast.4, f32[1]{0:T(128)} %bitcast.5, f32[1]{0:T(128)S(6)} %convert_element_type.12), dimensions={0} | concatenate | bytes 48 | tf_op jit(solution)/shard_map/stack | solution.py:230
  7.7 1.8 %shard_map.101 = f32[2,2,8,2048]{3,2,1,0:T(8,128)} custom-call(f32[6]{0:T(128)} %stack.24.scale_ref, f32[128,2048]{1,0:T(8,128)} %bitcast.19, f32[128,2048]{1,0:T(8,128)} %bitcast.20, f32[128,2048]{1,0:T(8,128)} %bitcast.22, f32[128,2048]{1,0:T(8,128)} %bitcast.23), custom_call_target="tpu_custom_call" | custom-call | tf_op jit(solution)/shard_map/pallas_call | solution.py:246
  9.6 1.2 %collective-permute-start = (f32[2,2,8,2048]{3,2,1,0:T(8,128)}, f32[2,2,8,2048]{3,2,1,0:T(8,128)S(1)}, u32[]{:S(2)}, u32[]{:S(2)}) collective-permute-start(f32[2,2,8,2048]{3,2,1,0:T(8,128)} %shard_map.101), channel_id=1, source_target_pairs={{0,1},{1,0},{2,3},{3,2},{4,5},{5,4},{6,7},{7,6},{8,9},{9,8},{10,11... | collective-permute-start | bytes 786440 | tf_op jit(solution)/shard_map/ppermute | solution.py:262
  10.8 6.2 %collective-permute-done = f32[2,2,8,2048]{3,2,1,0:T(8,128)S(1)} collective-permute-done((f32[2,2,8,2048]{3,2,1,0:T(8,128)}, f32[2,2,8,2048]{3,2,1,0:T(8,128)S(1)}, u32[]{:S(2)}, u32[]{:S(2)}) %collective-permute-start) | collective-permute-done | bytes 262176 | tf_op jit(solution)/shard_map/ppermute | solution.py:262
  17.0 0.7 slice_bitcast_fusion
  17.7 21.3 %shard_map.102 = (f32[128,2048]{1,0:T(8,128)}, f32[16,8,2176]{2,1,0:T(8,128)}) custom-call(f32[6]{0:T(128)} %stack.24.scale_ref, f32[128,2048]{1,0:T(8,128)} %bitcast.21, f32[128,2048]{1,0:T(8,128)} %bitcast.24, f32[2,8,2048]{2,1,0:T(8,128)} %get-tuple-element.16.above_ref, f32[2,8,2048]{2,1,0:T(8,128)} %get-tuple-element.15.below_ref), custom_call_target="tpu_custom_call" | custom-call | tf_op jit(solution)/shard_map/pallas_call | solution.py:268
  39.0 34.7 %all_to_all.10.got_ref = f32[16,8,2176]{2,1,0:T(8,128)} all-to-all(f32[16,8,2176]{2,1,0:T(8,128)} %get-tuple-element.10), channel_id=1, replica_groups=mesh['rep'=16,'dom'=2] {'rep'}, dimensions={0} | all-to-all | bytes 2228224 | tf_op jit(solution)/shard_map/all_to_all | solution.py:278
  73.7 3.6 %shard_map.103 = (f32[16,8,2048]{2,1,0:T(8,128)}, f32[16,128]{1,0:T(8,128)}) custom-call(f32[16,8,2176]{2,1,0:T(8,128)} %all_to_all.10.got_ref), custom_call_target="tpu_custom_call" | custom-call | tf_op jit(solution)/shard_map/pallas_call | solution.py:280
  77.3 0.0 copy-start
  77.3 4.9 %all-to-all-start.1 = ((f32[16,8,2048]{2,1,0:T(8,128)}), f32[16,8,2048]{2,1,0:T(8,128)S(1)}, u32[]{:S(2)}, u32[]{:S(2)}) async-start(f32[16,8,2048]{2,1,0:T(8,128)} %get-tuple-element.11), calls=%async_computation.1 | async-start | bytes 2097152 | tf_op jit(solution)/shard_map/all_to_all | solution.py:294
  82.2 0.0 copy-done
  82.2 1.3 %collective-permute-start.1 = (f32[16,128]{1,0:T(8,128)S(1)}, f32[16,128]{1,0:T(8,128)S(1)}, u32[]{:S(2)}, u32[]{:S(2)}) collective-permute-start(f32[16,128]{1,0:T(8,128)S(1)} %copy-done), channel_id=1, source_target_pairs={{0,1},{1,0},{2,3},{3,2},{4,5},{5,4},{6,7},{7,6},{8,9},{9,8},{10,11... | collective-permute-start | bytes 24584 | tf_op jit(solution)/shard_map/ppermute | solution.py:301
  83.5 1.6 %collective-permute-done.1 = f32[16,128]{1,0:T(8,128)S(1)} collective-permute-done((f32[16,128]{1,0:T(8,128)S(1)}, f32[16,128]{1,0:T(8,128)S(1)}, u32[]{:S(2)}, u32[]{:S(2)}) %collective-permute-start.1) | collective-permute-done | bytes 8224 | tf_op jit(solution)/shard_map/ppermute | solution.py:301
  85.0 0.7 fusion
  86.4 0.6 fusion.3
  87.0 20.1 %all-to-all-done.1 = f32[16,8,2048]{2,1,0:T(8,128)S(1)} async-done(((f32[16,8,2048]{2,1,0:T(8,128)}), f32[16,8,2048]{2,1,0:T(8,128)S(1)}, u32[]{:S(2)}, u32[]{:S(2)}) %all-to-all-start.1) | async-done | bytes 1048608 | tf_op jit(solution)/shard_map/all_to_all | solution.py:294
  107.1 1.0 copy.14
  (1 shorter events, 0.0 us)
Async XLA Ops:
  9.6 7.4 %collective-permute-start = (f32[2,2,8,2048]{3,2,1,0:T(8,128)}, f32[2,2,8,2048]{3,2,1,0:T(8,128)S(1)}, u32[]{:S(2)}, u32[]{:S(2)}) collective-permute-start(f32[2,2,8,2048]{3,2,1,0:T(8,128)} %shard_map.101), channel_id=1, source_target_pairs={{0,1},{1,0},{2,3},{3,2},{4,5},{5,4},{6,7},{7,6},{8,9},{9,8},{10,11... | collective-permute-start | bytes 786440 | tf_op jit(solution)/shard_map/ppermute | solution.py:262
  77.3 4.9 %copy-start = (f32[16,128]{1,0:T(8,128)S(1)}, f32[16,128]{1,0:T(8,128)}, u32[]{:S(2)}) copy-start(f32[16,128]{1,0:T(8,128)} %get-tuple-element.12) | copy-start | bytes 24580
  77.3 29.8 %all-to-all-start.1 = ((f32[16,8,2048]{2,1,0:T(8,128)}), f32[16,8,2048]{2,1,0:T(8,128)S(1)}, u32[]{:S(2)}, u32[]{:S(2)}) async-start(f32[16,8,2048]{2,1,0:T(8,128)} %get-tuple-element.11), calls=%async_computation.1 | async-start | bytes 2097152 | tf_op jit(solution)/shard_map/all_to_all | solution.py:294
  82.2 2.9 %collective-permute-start.1 = (f32[16,128]{1,0:T(8,128)S(1)}, f32[16,128]{1,0:T(8,128)S(1)}, u32[]{:S(2)}, u32[]{:S(2)}) collective-permute-start(f32[16,128]{1,0:T(8,128)S(1)} %copy-done), channel_id=1, source_target_pairs={{0,1},{1,0},{2,3},{3,2},{4,5},{5,4},{6,7},{7,6},{8,9},{9,8},{10,11... | collective-permute-start | bytes 24584 | tf_op jit(solution)/shard_map/ppermute | solution.py:301

commit v2 on v1

v2 whole, which is shorter than its diff:
```python
import functools

import jax
import jax.numpy as jnp
from jax import lax
from jax.experimental import pallas as pl
from jax.experimental.pallas import tpu as pltpu
from jax.sharding import PartitionSpec as P

STEPS = 8
hopping = 0.18
quartic = 0.3
step_size = 0.05

SUB = 8
LANES = 128
EDGE = 3
GROUP = 7


def lane_index():
    return lax.broadcasted_iota(jnp.int32, (SUB, LANES), 1)


def row_index():
    return lax.broadcasted_iota(jnp.int32, (SUB, LANES), 0)


class Scales:
    def __init__(self, cold):
        self.cold = cold
        squared = jnp.full((SUB, LANES), (4.0 * quartic * step_size * step_size) * cold)
        self.root = jnp.sqrt(squared)
        self.back = 1.0 / self.root
        self.back2 = self.back * self.back
        self.pull = (2.0 * hopping * step_size * step_size) * cold
        self.slope = -((2.0 - 4.0 * quartic) * step_size * step_size) * cold
        self.speed = step_size * self.root
        self.unspeed = 1.0 / self.speed

    def half(self, near, value):
        return 0.5 * (self.pull * near + value * (self.slope - value * value))

    def step(self, near, value, before):
        return value + ((value - before) + (self.pull * near + value * (self.slope - value * value)))

    def site(self, value, ahead):
        squared = value * value * self.back2
        return (-2.0 * hopping) * (self.back2 * (value * ahead)) + (
            squared + quartic * (squared - 1.0) * (squared - 1.0)
        )


def chosen_scalars(labels_ref, betas_ref):
    return betas_ref[labels_ref[0]]


def beside(values, lane):
    count = len(values)
    ahead = [pltpu.roll(v, 1, 1) for v in values]
    back = [pltpu.roll(v, LANES - 1, 1) for v in values]
    left = [jnp.where(lane == 0, ahead[i - 1], ahead[i]) for i in range(count)]
    right = [jnp.where(lane == LANES - 1, back[(i + 1) % count], back[i]) for i in range(count)]
    return [a + b for a, b in zip(left, right)], right


def around(ref, row, tiles, lane):
    values = [ref[t, pl.ds(row, SUB), :] for t in range(tiles)]
    sums, right = beside(values, lane)
    below = [ref[t, pl.ds(row + 1, SUB), :] for t in range(tiles)]
    near = [(ref[t, pl.ds(row - 1, SUB), :] + below[t]) + sums[t] for t in range(tiles)]
    return values, near, below, right


def advance(before, after, row, tiles, lane, scales, keep=None):
    values, near, _, _ = around(before, row, tiles, lane)
    for t in range(tiles):
        old = after[t, pl.ds(row, SUB), :]
        new = scales.step(near[t], values[t], old)
        if keep is not None:
            new = jnp.where(keep, old, new)
        after[t, pl.ds(row, SUB), :] = new


def pack_kernel(labels_ref, betas_ref, head_ref, tail_ref, head_m_ref, tail_m_ref, out_ref):
    scales = Scales(chosen_scalars(labels_ref, betas_ref))
    lane = lane_index()
    row = row_index()
    tiles = head_ref.shape[1] // LANES
    for side, ref, m_ref in ((0, head_ref, head_m_ref), (1, tail_ref, tail_m_ref)):
        base = 0 if side == 0 else SUB
        inner = SUB - base
        values = [scales.root * ref[base : base + SUB, pl.ds(i * LANES, LANES)] for i in range(tiles)]
        sums, _ = beside(values, lane)
        for i in range(tiles):
            cols = pl.ds(i * LANES, LANES)
            other = scales.root * ref[inner : inner + SUB, cols]
            up = pltpu.roll(values[i], 1, 0)
            down = pltpu.roll(values[i], SUB - 1, 0)
            if side == 0:
                up = jnp.where(row == 0, 0.0, up)
                down = jnp.where(row == SUB - 1, pltpu.roll(other, SUB - 1, 0), down)
            else:
                up = jnp.where(row == 0, pltpu.roll(other, 1, 0), up)
                down = jnp.where(row == SUB - 1, 0.0, down)
            push = scales.speed * m_ref[:, cols] + scales.half((up + down) + sums[i], values[i])
            out_ref[side, 0, :, cols] = values[i]
            out_ref[side, 1, :, cols] = values[i] + push


def slots(row_block, tiles, per_member):
    shares = tiles // per_member
    return [(row_block * shares + s, s * per_member * LANES) for s in range(shares)]


def inner_kernel(
    per_member,
    labels_ref,
    betas_ref,
    accept_ref,
    field_hbm,
    momentum_hbm,
    out_hbm,
    send_hbm,
    state_hbm,
    energy_hbm,
    sums_ref,
    field_ref,
    momentum_ref,
    chosen_ref,
    first,
    second,
    energy,
    in_sem,
    out_sem,
    send_sem,
    state_sem,
):
    rows, width = field_ref.shape
    tiles = width // LANES
    blocks = rows // SUB
    chunk = rows // 8
    loads = []
    for a, (source, target) in enumerate(((field_hbm, field_ref), (momentum_hbm, momentum_ref))):
        for k in range(8):
            part = pl.ds(k * chunk, chunk)
            copy = pltpu.make_async_copy(source.at[part, :], target.at[part, :], in_sem.at[a, k])
            copy.start()
            loads.append(copy)
    scales = Scales(chosen_scalars(labels_ref, betas_ref))
    accepted = accept_ref[0] == 1
    lane = lane_index()
    sub = row_index()
    zero = jnp.zeros((SUB, LANES), jnp.float32)
    for ref in (first, second):
        for t in range(tiles):
            ref[t, 0:SUB, :] = zero
            ref[t, SUB + rows : 2 * SUB + rows, :] = zero
    for k in range(8):
        loads[k].wait()
        for b in range(chunk // SUB):
            row = k * chunk + b * SUB
            for t in range(tiles):
                first[t, SUB + row : 2 * SUB + row, :] = (
                    scales.root * field_ref[row : row + SUB, pl.ds(t * LANES, LANES)]
                )

    def begin(block, total):
        source = pl.multiple_of(block * SUB, SUB)
        row = pl.multiple_of(SUB + block * SUB, SUB)
        values, near, below, right = around(first, row, tiles, lane)
        for t in range(tiles):
            push = scales.speed * momentum_ref[pl.ds(source, SUB), pl.ds(t * LANES, LANES)]
            moment = scales.unspeed * push
            action = scales.site(values[t], below[t] + right[t])
            energy[t, pl.ds(source, SUB), :] = 0.5 * moment * moment + scales.cold * action
            total = total + action
            second[t, pl.ds(row, SUB), :] = values[t] + (push + scales.half(near[t], values[t]))
        return total

    for k in range(8):
        loads[8 + k].wait()

    per_turn = 2

    def begin_turn(i, total):
        for b in range(per_turn):
            total = begin(i * per_turn + b, total)
        return total

    old_action = lax.fori_loop(0, blocks // per_turn, begin_turn, zero)

    group = GROUP if (blocks - 2) % GROUP == 0 else 1
    for time in range(1, STEPS):
        before, after = (second, first) if time % 2 == 1 else (first, second)
        advance(before, after, SUB, tiles, lane, scales, keep=sub <= time)
        advance(before, after, rows, tiles, lane, scales, keep=sub >= SUB - 1 - time)

        def turn(i, carry, before=before, after=after):
            for b in range(group):
                row = pl.multiple_of(2 * SUB + (i * group + b) * SUB, SUB)
                advance(before, after, row, tiles, lane, scales)
            return carry

        lax.fori_loop(0, (blocks - 2) // group, turn, 0)
    last, previous = (first, second) if STEPS % 2 == 0 else (second, first)
    stores = []
    for n, buffer in enumerate((last, previous)):
        for side, row in ((0, SUB), (1, SUB + rows - EDGE * SUB)):
            copy = pltpu.make_async_copy(
                buffer.at[:, pl.ds(row, EDGE * SUB), :], state_hbm.at[side, n], state_sem.at[side, n]
            )
            copy.start()
            stores.append(copy)
    for side, row in ((0, 0), (1, rows - 2 * SUB)):
        copy = pltpu.make_async_copy(
            energy.at[:, pl.ds(row, 2 * SUB), :], energy_hbm.at[side], state_sem.at[side, 2]
        )
        copy.start()
        stores.append(copy)

    def emit(block):
        row = block * SUB
        copies = [
            pltpu.make_async_copy(
                chosen_ref.at[pl.ds(row, SUB), :], out_hbm.at[pl.ds(row, SUB), :], out_sem.at[block]
            )
        ]
        for member, column in slots(block, tiles, per_member):
            width_here = per_member * LANES
            copies.append(
                pltpu.make_async_copy(
                    chosen_ref.at[pl.ds(row, SUB), pl.ds(column, width_here)],
                    send_hbm.at[member, :, pl.ds(0, width_here)],
                    send_sem.at[member],
                )
            )
        return copies

    def choose(block, value, t):
        row = pl.multiple_of(block * SUB, SUB)
        cols = pl.ds(t * LANES, LANES)
        kept = field_ref[pl.ds(row, SUB), cols]
        chosen_ref[pl.ds(row, SUB), cols] = jnp.where(accepted, scales.back * value, kept)

    for block in (1, blocks - 2):
        for t in range(tiles):
            choose(block, last[t, SUB + block * SUB : 2 * SUB + block * SUB, :], t)
        for copy in emit(block):
            copy.start()
            stores.append(copy)

    def finish(block, carry):
        change, total = carry
        row = pl.multiple_of(SUB + block * SUB, SUB)
        source = pl.multiple_of(block * SUB, SUB)
        values, near, below, right = around(last, row, tiles, lane)
        for t in range(tiles):
            gone = values[t] - previous[t, pl.ds(row, SUB), :]
            moment = scales.unspeed * (gone + scales.half(near[t], values[t]))
            action = scales.site(values[t], below[t] + right[t])
            total = total + action
            change = change + (
                (0.5 * moment * moment + scales.cold * action) - energy[t, pl.ds(source, SUB), :]
            )
            choose(block, values[t], t)
        return change, total

    sums = (zero, zero)
    if (blocks - 4) % per_turn == 0:
        for i in range((blocks - 4) // per_turn):
            sums = lax.fori_loop(
                0,
                1,
                lambda _, carry, i=i: functools.reduce(
                    lambda c, b: finish(2 + i * per_turn + b, c), range(per_turn), carry
                ),
                sums,
            )
            for b in range(per_turn):
                for copy in emit(2 + i * per_turn + b):
                    copy.start()
                    stores.append(copy)
    else:
        for block in range(2, blocks - 2):
            sums = finish(block, sums)
            for copy in emit(block):
                copy.start()
                stores.append(copy)
    sums_ref[0] = sums[0]
    sums_ref[1] = sums[1]
    sums_ref[2] = old_action
    for copy in stores:
        copy.wait()


def outer_kernel(
    per_member,
    halos,
    labels_ref,
    betas_ref,
    accept_ref,
    swap_ref,
    *refs,
):
    halo_refs = refs[:halos]
    (
        state_ref,
        energy_ref,
        sums_ref,
        head_ref,
        tail_ref,
        _,
        _,
        out_hbm,
        send_hbm,
        first,
        second,
        chosen_ref,
        note_ref,
        out_sem,
        send_sem,
        note_sem,
    ) = refs[halos:]
    scales = Scales(chosen_scalars(labels_ref, betas_ref))
    label = swap_ref[labels_ref[0]].astype(jnp.float32)
    accepted = accept_ref[0] == 1
    lane = lane_index()
    sub = row_index()
    tiles = first.shape[1]
    members = send_hbm.shape[0]
    blocks = out_hbm.shape[0] // SUB
    zero = jnp.zeros((SUB, LANES), jnp.float32)
    last, previous = (first, second) if STEPS % 2 == 0 else (second, first)
    old_extra = zero
    energy_extra = []
    for side in range(2):
        ref = halo_refs[side % halos]
        own = 2 * SUB if side == 0 else 0
        edge = SUB if side == 0 else EDGE * SUB
        pad = 0 if side == 0 else (EDGE + 1) * SUB
        mine = own if side == 0 else (EDGE - 1) * SUB
        for t in range(tiles):
            cols = pl.ds(t * LANES, LANES)
            for n, buffer in enumerate((last, previous)):
                buffer[side, t, own : own + EDGE * SUB, :] = state_ref[side, n, t]
                buffer[side, t, pad : pad + SUB, :] = zero
            start_halo = ref[1 - side, 0, :, cols]
            start_mine = first[side, t, mine : mine + SUB, :]
            if side == 0:
                own_part = jnp.where(sub == SUB - 1, pltpu.roll(start_mine, SUB - 1, 0), 0.0)
                halo_part = jnp.where(sub == 0, pltpu.roll(start_halo, 1, 0), 0.0)
            else:
                own_part = jnp.where(sub == 0, pltpu.roll(start_mine, 1, 0), 0.0)
                halo_part = jnp.where(sub == SUB - 1, pltpu.roll(start_halo, SUB - 1, 0), 0.0)
                missing = (-2.0 * hopping) * (scales.back2 * (start_mine * halo_part))
                old_extra = old_extra + missing
                energy_extra.append(scales.cold * missing)
            first[side, t, edge : edge + SUB, :] = start_halo
            second[side, t, edge : edge + SUB, :] = ref[1 - side, 1, :, cols] + (
                0.5 * scales.pull
            ) * own_part
            second[side, t, mine : mine + SUB, :] = (
                second[side, t, mine : mine + SUB, :] + (0.5 * scales.pull) * halo_part
            )
    for time in range(1, STEPS):
        before, after = (second, first) if time % 2 == 1 else (first, second)
        for side in range(2):
            mine = 2 * SUB if side == 0 else (EDGE - 1) * SUB
            edge = SUB if side == 0 else EDGE * SUB
            keep = sub > time if side == 0 else sub < SUB - 1 - time
            advance(before.at[side], after.at[side], edge, tiles, lane, scales)
            advance(before.at[side], after.at[side], mine, tiles, lane, scales, keep=keep)
    change = sums_ref[0]
    total = sums_ref[1]
    copies = []
    for side in range(2):
        own = 2 * SUB if side == 0 else 0
        for b in range(2):
            place = b if side == 0 else EDGE - 2 + b
            row = own + place * SUB
            values, near, below, right = around(last.at[side], row, tiles, lane)
            outermost = (side == 0 and b == 0) or (side == 1 and b == 1)
            for t in range(tiles):
                gone = values[t] - previous[side, t, pl.ds(row, SUB), :]
                moment = scales.unspeed * (gone + scales.half(near[t], values[t]))
                action = scales.site(values[t], below[t] + right[t])
                total = total + action
                old = energy_ref[side, t, b * SUB : (b + 1) * SUB, :]
                if side == 1 and outermost:
                    old = old + energy_extra[t]
                change = change + ((0.5 * moment * moment + scales.cold * action) - old)
                if outermost:
                    cols = pl.ds(t * LANES, LANES)
                    kept = head_ref[:, cols] if side == 0 else tail_ref[:, cols]
                    chosen_ref[side, :, cols] = jnp.where(accepted, scales.back * values[t], kept)
        block = 0 if side == 0 else blocks - 1
        copies.append(
            pltpu.make_async_copy(
                chosen_ref.at[side], out_hbm.at[pl.ds(block * SUB, SUB), :], out_sem.at[side]
            )
        )
        for n, (member, column) in enumerate(slots(block, tiles, per_member)):
            size = per_member * LANES
            copies.append(
                pltpu.make_async_copy(
                    chosen_ref.at[side, :, pl.ds(column, size)],
                    send_hbm.at[member, :, pl.ds(0, size)],
                    send_sem.at[side, n],
                )
            )
    for copy in copies:
        copy.start()
    old_action = sums_ref[2] + old_extra
    action = jnp.sum(jnp.where(accepted, total, old_action))
    change = jnp.sum(change)
    note_ref[...] = jnp.where(
        lane == 0, label, jnp.where(lane == 1, action, jnp.where(lane == 2, change, 0.0))
    )
    for member in range(members):
        copy = pltpu.make_async_copy(
            note_ref,
            send_hbm.at[member, :, pl.ds(per_member * LANES, LANES)],
            note_sem.at[member],
        )
        copy.start()
        copies.append(copy)
    for copy in copies:
        copy.wait()


def place_kernel(got_hbm, out_hbm, notes_hbm, pieces_ref, labels_ref, load_sem, sem, note_sem):
    members, _, width = out_hbm.shape
    notes = got_hbm.at[:, 0, pl.ds(width, LANES)]
    fetch = pltpu.make_async_copy(notes, labels_ref, note_sem.at[0])
    fetch.start()
    keep = pltpu.make_async_copy(notes, notes_hbm, note_sem.at[1])
    keep.start()
    loads = []
    for r in range(members):
        load = pltpu.make_async_copy(got_hbm.at[r, :, pl.ds(0, width)], pieces_ref.at[r], load_sem.at[r])
        load.start()
        loads.append(load)
    fetch.wait()
    copies = []
    for r in range(members):
        loads[r].wait()
        slot = labels_ref[r, 0].astype(jnp.int32)
        copy = pltpu.make_async_copy(pieces_ref.at[r], out_hbm.at[slot], sem.at[r])
        copy.start()
        copies.append(copy)
    keep.wait()
    for copy in copies:
        copy.wait()


def body(field, momentum, labels, betas, accept, swap_pairs):
    rows = field.shape[1]
    width = field.shape[2]
    members = lax.axis_size("rep")
    strips = lax.axis_size("dom")
    tiles = width // LANES
    per_member = (rows // SUB) * tiles // members
    shares = tiles // per_member
    piece = per_member * LANES
    f32 = jnp.float32
    start = field[0]
    moment = momentum[0]
    smem = pl.BlockSpec(memory_space=pltpu.SMEM)
    vmem = pl.BlockSpec(memory_space=pltpu.VMEM)
    anywhere = pl.BlockSpec(memory_space=pl.ANY)
    dma = pltpu.SemaphoreType.DMA
    last16 = rows // (2 * SUB) - 1
    last8 = rows // SUB - 1
    edges = pl.pallas_call(
        pack_kernel,
        grid=(1,),
        out_shape=jax.ShapeDtypeStruct((2, 2, SUB, width), f32),
        in_specs=[
            smem,
            smem,
            pl.BlockSpec((2 * SUB, width), lambda i: (0, 0)),
            pl.BlockSpec((2 * SUB, width), lambda i: (last16, 0)),
            pl.BlockSpec((SUB, width), lambda i: (0, 0)),
            pl.BlockSpec((SUB, width), lambda i: (last8, 0)),
        ],
        out_specs=pl.BlockSpec((2, 2, SUB, width), lambda i: (0, 0, 0, 0)),
        name="pack",
    )(labels, betas, start, start, moment, moment)
    forward = [(i, (i + 1) % strips) for i in range(strips)]
    backward = [((i + 1) % strips, i) for i in range(strips)]
    halos = (lax.ppermute(edges, "dom", forward),)
    if strips > 2:
        halos = halos + (lax.ppermute(edges, "dom", backward),)
    column = pltpu.VMEM((tiles, rows + 2 * SUB, LANES), f32)
    strip = pltpu.VMEM((rows, width), f32)
    out, outgoing, state, energy, sums = pl.pallas_call(
        functools.partial(inner_kernel, per_member),
        out_shape=(
            jax.ShapeDtypeStruct((rows, width), f32),
            jax.ShapeDtypeStruct((members, SUB, piece + LANES), f32),
            jax.ShapeDtypeStruct((2, 2, tiles, EDGE * SUB, LANES), f32),
            jax.ShapeDtypeStruct((2, tiles, 2 * SUB, LANES), f32),
            jax.ShapeDtypeStruct((3, SUB, LANES), f32),
        ),
        in_specs=[smem, smem, smem, anywhere, anywhere],
        out_specs=(anywhere, anywhere, anywhere, anywhere, vmem),
        scratch_shapes=[
            strip,
            strip,
            strip,
            column,
            column,
            pltpu.VMEM((tiles, rows, LANES), f32),
            dma((2, 8)),
            dma((rows // SUB,)),
            dma((members,)),
            dma((2, 3)),
        ],
        cost_estimate=pl.CostEstimate(
            flops=100 * rows * width, bytes_accessed=16 * rows * width, transcendentals=0
        ),
        name="inner",
    )(labels, betas, accept, start, moment)
    window = pltpu.VMEM((2, tiles, (EDGE + 2) * SUB, LANES), f32)
    count = 4 + len(halos)
    out, outgoing = pl.pallas_call(
        functools.partial(outer_kernel, per_member, len(halos)),
        grid=(1,),
        out_shape=(
            jax.ShapeDtypeStruct((rows, width), f32),
            jax.ShapeDtypeStruct((members, SUB, piece + LANES), f32),
        ),
        in_specs=[smem] * 4
        + [vmem] * (len(halos) + 3)
        + [
            pl.BlockSpec((SUB, width), lambda i: (0, 0)),
            pl.BlockSpec((SUB, width), lambda i: (last8, 0)),
            anywhere,
            anywhere,
        ],
        out_specs=(anywhere, anywhere),
        scratch_shapes=[
            window,
            window,
            pltpu.VMEM((2, SUB, width), f32),
            pltpu.VMEM((SUB, LANES), f32),
            dma((2,)),
            dma((2, shares)),
            dma((members,)),
        ],
        input_output_aliases={count + 5: 0, count + 6: 1},
        name="outer",
    )(labels, betas, accept, swap_pairs, *halos, state, energy, sums, start, start, out, outgoing)
    received = lax.all_to_all(outgoing, "rep", split_axis=0, concat_axis=0, tiled=True)
    ordered, notes = pl.pallas_call(
        place_kernel,
        out_shape=(
            jax.ShapeDtypeStruct((members, SUB, piece), f32),
            jax.ShapeDtypeStruct((members, LANES), f32),
        ),
        in_specs=[anywhere],
        out_specs=(anywhere, anywhere),
        scratch_shapes=[
            pltpu.VMEM((members, SUB, piece), f32),
            pltpu.SMEM((members, LANES), f32),
            dma((members,)),
            dma((members,)),
            dma((2,)),
        ],
        name="place",
    )(received)
    returned = lax.all_to_all(ordered, "rep", split_axis=0, concat_axis=0, tiled=True)
    returned = returned.reshape(rows // SUB, shares, SUB, piece).transpose(0, 2, 1, 3)
    returned = returned.reshape(1, rows, width)
    sums = notes
    passing = notes
    for _ in range(strips - 1):
        passing = lax.ppermute(passing, "dom", forward)
        sums = sums + passing
    me = lax.axis_index("rep")
    ladder_index = jnp.arange(betas.shape[0], dtype=jnp.int32)
    held_labels = notes[:, 0].astype(jnp.int32)
    sites = strips * rows * width
    ladder = jnp.sum(jnp.where(held_labels == me, sums[:, 1], 0.0)) / sites
    change = jnp.sum(jnp.where(ladder_index == me, sums[:, 2], 0.0))
    new_label = jnp.sum(jnp.where(ladder_index == me, held_labels, 0))
    return (out[None], returned, new_label[None], change[None], ladder[None])


def solution(mesh):
    placed = (P("rep", "dom", None), P("rep", "dom", None), P("rep"), P(), P("rep"), P())
    return jax.shard_map(
        body,
        mesh=mesh,
        in_specs=placed,
        out_specs=(P("rep", "dom", None), P("rep", "dom", None), P("rep"), P("rep"), P("rep")),
        check_vma=False,
    )
```

time: 110 us -> 90.4 us (0.82)
  Pallas kernels: 26.8 us -> 20 us
  waiting for transfers between devices: 27.9 us -> 21.9 us
  between operations: 5.73 us -> 3.77 us
  other arithmetic: 3.84 us -> 1.96 us
    ppermute x1, waiting for transfers between devices: 6.16 us -> 0.01 us  [body(): halos = (lax.ppermute(edges, 'dom', forward),)]
    pallas_call x1 -> x2, Pallas kernels: 21.3 us -> 15.9 us  [the longest x1 12.3 us: body(): pl.pallas_call(functools.partial(inner_kernel, per_member), out_shape=(ja...]
    reduce_sum x2 -> x1, other arithmetic: 2.56 us -> 0.64 us  [body(): new_label = jnp.sum(jnp.where(ladder_index == me, held_labels, 0))]
    pallas_call x1, Pallas kernels: 3.61 us -> 2.17 us  [body(): pl.pallas_call(place_kernel, out_shape=(jax.ShapeDtypeStruct((members, SU...]
    another operation x1 -> x0, local copies, waits for them, and re-layouts: 1.24 us -> none  [body(): jnp.stack((cold, 1.0 / unit, unit, step_size * unit, new_label.astype(jnp...]
  transfers between devices with their start and end apart: 3 -> 3, of which waited for: 3 -> 2; matrix products, arithmetic and copies ran while one was open for 1% -> 2% of each run, Pallas kernels for 0% -> 14%
where the time goes in v2:
time: 90.4 us; the launch traced here: 89.9 us
  blocking collectives  34.1 us (38%)
  waiting for transfers between devices  21.9 us (24%)
  Pallas kernels  20 us (22%)
  starting transfers between devices  6.39 us (7%)
  between operations  3.77 us (4%)
  other arithmetic  1.96 us (2%)
  local copies, waits for them, and re-layouts  1.87 us (2%)
    all_to_all x1, blocking collectives, body(): lax.all_to_all(outgoing, 'rep', split_axis=0, concat_axis=0, tiled=True)  34.1 us
    all_to_all x1, waiting for transfers between devices, body(): lax.all_to_all(ordered, 'rep', split_axis=0, concat_axis=0, tiled=True)  20 us
    pallas_call x1, Pallas kernels, body(): pl.pallas_call(functools.partial(inner_kernel, per_member), out_shape=(ja...  12.3 us
    all_to_all x1, starting transfers between devices, body(): lax.all_to_all(ordered, 'rep', split_axis=0, concat_axis=0, tiled=True)  4.86 us
    pallas_call x1, Pallas kernels, body(): pl.pallas_call(functools.partial(outer_kernel, per_member, len(halos)), g...  3.59 us
    pallas_call x1, Pallas kernels, body(): pl.pallas_call(place_kernel, out_shape=(jax.ShapeDtypeStruct((members, SU...  2.17 us
    pallas_call x1, Pallas kernels, body(): pl.pallas_call(pack_kernel, grid=(1,), out_shape=jax.ShapeDtypeStruct((2,...  1.89 us
    ppermute x1, waiting for transfers between devices, body(): passing = lax.ppermute(passing, 'dom', forward)  1.82 us
  transfers between devices with their start and end apart: 3, of which 2 were waited for; matrix products, arithmetic and copies ran while one was open for 2% of the time, Pallas kernels for 14%

profile of v2, /device:TPU:9, one launch (start us, length us, event | category | flops | bytes accessed | tf_op | source)
XLA Modules:
  0.0 89.9 jit_solution(10595340191382443140)
XLA Ops:
  1.3 1.9 %pack.1 = f32[2,2,8,2048]{3,2,1,0:T(8,128)} custom-call(s32[1]{0:T(128)S(6)} %copy.16.labels_ref, f32[16]{0:T(128)} %betas_ref.5, f32[128,2048]{1,0:T(8,128)} %bitcast.7, f32[128,2048]{1,0:T(8,128)} %bitcast.8, f32[128,2048]{1,0:T(8,128)} %bitcast.12, f32[128,2048]{1,0:T(8,128)} %bitcast.13), custom_call_target="tpu_custom_call" | custom-call | tf_op jit(solution)/shard_map/pack/pallas_call | solution.py:475
  3.2 1.2 %collective-permute-start = (f32[2,2,8,2048]{3,2,1,0:T(8,128)}, f32[2,2,8,2048]{3,2,1,0:T(8,128)S(1)}, u32[]{:S(2)}, u32[]{:S(2)}) collective-permute-start(f32[2,2,8,2048]{3,2,1,0:T(8,128)} %pack.1), channel_id=1, source_target_pairs={{0,1},{1,0},{2,3},{3,2},{4,5},{5,4},{6,7},{7,6},{8,9},{9,8},{10,11... | collective-permute-start | bytes 786440 | tf_op jit(solution)/shard_map/ppermute | solution.py:492
  5.1 12.3 %inner.1 = (f32[128,2048]{1,0:T(8,128)}, f32[16,8,2176]{2,1,0:T(8,128)}, f32[2,2,16,24,128]{4,3,2,1,0:T(8,128)}, f32[2,16,16,128]{3,2,1,0:T(8,128)}, f32[3,8,128]{2,1,0:T(8,128)}) custom-call(s32[1]{0:T(128)S(6)} %copy.16.labels_ref, f32[16]{0:T(128)} %betas_ref.5, s32[1]{0:T(128)S(6)} %copy.17.accept_ref, f32[128,2048]{1,0:T(8,128)} %bitcast.9, ...), custom_call_target="tpu_custom_call" | custom-call | flops 26214400 | bytes 4194304 | tf_op jit(solution)/shard_map/inner/pallas_call | solution.py:497
  17.4 0.0 collective-permute-done.refs_0_
  17.4 0.0 copy-start
  17.4 0.7 copy-done
  18.1 3.6 %outer.1 = (f32[128,2048]{1,0:T(8,128)}, f32[16,8,2176]{2,1,0:T(8,128)}) custom-call(s32[1]{0:T(128)S(6)} %copy.16.labels_ref, f32[16]{0:T(128)} %betas_ref.5, s32[1]{0:T(128)S(6)} %copy.17.accept_ref, s32[16]{0:T(128)} %swap_ref.1, f32[2,2,8,2048]{3,2,1,0:T(8,128)} %copy-done, ...), custom_call_target="tpu_custom_call", output_to_operand_aliasing={{0}: (10, {}), {1}: (11, {})} | custom-call | tf_op jit(solution)/shard_map/outer/pallas_call | solution.py:527
  21.7 34.1 %all_to_all.10.got_hbm = f32[16,8,2176]{2,1,0:T(8,128)} all-to-all(f32[16,8,2176]{2,1,0:T(8,128)} %get-tuple-element.20), channel_id=1, replica_groups=mesh['rep'=16,'dom'=2] {'rep'}, dimensions={0} | all-to-all | bytes 2228224 | tf_op jit(solution)/shard_map/all_to_all | solution.py:555
  55.8 2.2 %place.1 = (f32[16,8,2048]{2,1,0:T(8,128)}, f32[16,128]{1,0:T(8,128)}) custom-call(f32[16,8,2176]{2,1,0:T(8,128)} %all_to_all.10.got_hbm), custom_call_target="tpu_custom_call" | custom-call | tf_op jit(solution)/shard_map/place/pallas_call | solution.py:556
  58.0 0.0 copy-start.1
  58.0 4.9 %all-to-all-start.1 = ((f32[16,8,2048]{2,1,0:T(8,128)}), f32[16,8,2048]{2,1,0:T(8,128)S(1)}, u32[]{:S(2)}, u32[]{:S(2)}) async-start(f32[16,8,2048]{2,1,0:T(8,128)} %get-tuple-element.21), calls=%async_computation.1 | async-start | bytes 2097152 | tf_op jit(solution)/shard_map/all_to_all | solution.py:573
  62.9 0.0 copy-done.1
  62.9 0.3 collective-permute-start.1
  63.2 0.1 convert_reduce_fusion
  63.3 0.6 fusion
  63.9 1.8 %collective-permute-done.1 = f32[16,128]{1,0:T(8,128)S(1)} collective-permute-done((f32[16,128]{1,0:T(8,128)S(1)}, f32[16,128]{1,0:T(8,128)S(1)}, u32[]{:S(2)}, u32[]{:S(2)}) %collective-permute-start.1) | collective-permute-done | bytes 8224 | tf_op jit(solution)/shard_map/ppermute | solution.py:579
  65.8 0.2 slice_reduce_fusion
  65.9 0.6 fusion.2
  67.2 0.6 fusion.1
  67.8 20.0 %all-to-all-done.1 = f32[16,8,2048]{2,1,0:T(8,128)S(1)} async-done(((f32[16,8,2048]{2,1,0:T(8,128)}), f32[16,8,2048]{2,1,0:T(8,128)S(1)}, u32[]{:S(2)}, u32[]{:S(2)}) %all-to-all-start.1) | async-done | bytes 1048608 | tf_op jit(solution)/shard_map/all_to_all | solution.py:573
  87.8 1.0 %copy.18 = f32[1,128,2048]{2,1,0:T(8,128)} copy(f32[1,128,2048]{2,1,0:T(8,128)S(1)} %bitcast.15) | data formatting | bytes 2097152
  (1 shorter events, 0.0 us)
Async XLA Ops:
  3.2 14.2 %collective-permute-start = (f32[2,2,8,2048]{3,2,1,0:T(8,128)}, f32[2,2,8,2048]{3,2,1,0:T(8,128)S(1)}, u32[]{:S(2)}, u32[]{:S(2)}) collective-permute-start(f32[2,2,8,2048]{3,2,1,0:T(8,128)} %pack.1), channel_id=1, source_target_pairs={{0,1},{1,0},{2,3},{3,2},{4,5},{5,4},{6,7},{7,6},{8,9},{9,8},{10,11... | collective-permute-start | bytes 786440 | tf_op jit(solution)/shard_map/ppermute | solution.py:492
  17.4 0.7 copy-start
  58.0 4.9 %copy-start.1 = (f32[16,128]{1,0:T(8,128)S(1)}, f32[16,128]{1,0:T(8,128)}, u32[]{:S(2)}) copy-start(f32[16,128]{1,0:T(8,128)} %get-tuple-element.22) | copy-start | bytes 24580
  58.0 29.8 %all-to-all-start.1 = ((f32[16,8,2048]{2,1,0:T(8,128)}), f32[16,8,2048]{2,1,0:T(8,128)S(1)}, u32[]{:S(2)}, u32[]{:S(2)}) async-start(f32[16,8,2048]{2,1,0:T(8,128)} %get-tuple-element.21), calls=%async_computation.1 | async-start | bytes 2097152 | tf_op jit(solution)/shard_map/all_to_all | solution.py:573
  62.9 2.9 %collective-permute-start.1 = (f32[16,128]{1,0:T(8,128)S(1)}, f32[16,128]{1,0:T(8,128)S(1)}, u32[]{:S(2)}, u32[]{:S(2)}) collective-permute-start(f32[16,128]{1,0:T(8,128)S(1)} %copy-done.1), channel_id=1, source_target_pairs={{0,1},{1,0},{2,3},{3,2},{4,5},{5,4},{6,7},{7,6},{8,9},{9,8},{10,11... | collective-permute-start | bytes 24584 | tf_op jit(solution)/shard_map/ppermute | solution.py:579

commit v3 on v2

--- a/solution.py
+++ b/solution.py
@@ -16,6 +16,7 @@
 LANES = 128
 EDGE = 3
 GROUP = 7
+WHOLE_VMEM = 67043328
 
 
 def lane_index():
@@ -104,8 +105,8 @@
                 up = jnp.where(row == 0, pltpu.roll(other, 1, 0), up)
                 down = jnp.where(row == SUB - 1, 0.0, down)
             push = scales.speed * m_ref[:, cols] + scales.half((up + down) + sums[i], values[i])
-            out_ref[side, 0, :, cols] = values[i]
-            out_ref[side, 1, :, cols] = values[i] + push
+            out_ref[side, 0, i] = values[i]
+            out_ref[side, 1, i] = values[i] + push
 
 
 def slots(row_block, tiles, per_member):
@@ -231,7 +232,7 @@
             copies.append(
                 pltpu.make_async_copy(
                     chosen_ref.at[pl.ds(row, SUB), pl.ds(column, width_here)],
-                    send_hbm.at[member, :, pl.ds(0, width_here)],
+                    send_hbm.at[member],
                     send_sem.at[member],
                 )
             )
@@ -305,8 +306,8 @@
 ):
     halo_refs = refs[:halos]
     (
-        state_ref,
-        energy_ref,
+        state_hbm,
+        energy_hbm,
         sums_ref,
         head_ref,
         tail_ref,
@@ -314,38 +315,50 @@
         _,
         out_hbm,
         send_hbm,
+        note_ref,
         first,
         second,
+        energy_ref,
+        halo_ref,
         chosen_ref,
-        note_ref,
+        in_sem,
         out_sem,
         send_sem,
-        note_sem,
     ) = refs[halos:]
+    last, previous = (first, second) if STEPS % 2 == 0 else (second, first)
+    loads = []
+    for side in range(2):
+        own = 2 * SUB if side == 0 else 0
+        parts = [
+            (state_hbm.at[side, n], buffer.at[side, :, pl.ds(own, EDGE * SUB), :])
+            for n, buffer in enumerate((last, previous))
+        ]
+        parts.append((halo_refs[side % halos].at[1 - side], halo_ref.at[side]))
+        parts.append((energy_hbm.at[side], energy_ref.at[side]))
+        for n, (source, target) in enumerate(parts):
+            copy = pltpu.make_async_copy(source, target, in_sem.at[side, n])
+            copy.start()
+            loads.append(copy)
     scales = Scales(chosen_scalars(labels_ref, betas_ref))
     label = swap_ref[labels_ref[0]].astype(jnp.float32)
     accepted = accept_ref[0] == 1
     lane = lane_index()
     sub = row_index()
     tiles = first.shape[1]
-    members = send_hbm.shape[0]
     blocks = out_hbm.shape[0] // SUB
     zero = jnp.zeros((SUB, LANES), jnp.float32)
-    last, previous = (first, second) if STEPS % 2 == 0 else (second, first)
     old_extra = zero
     energy_extra = []
+    for copy in loads:
+        copy.wait()
     for side in range(2):
-        ref = halo_refs[side % halos]
-        own = 2 * SUB if side == 0 else 0
         edge = SUB if side == 0 else EDGE * SUB
         pad = 0 if side == 0 else (EDGE + 1) * SUB
-        mine = own if side == 0 else (EDGE - 1) * SUB
+        mine = 2 * SUB if side == 0 else (EDGE - 1) * SUB
         for t in range(tiles):
-            cols = pl.ds(t * LANES, LANES)
-            for n, buffer in enumerate((last, previous)):
-                buffer[side, t, own : own + EDGE * SUB, :] = state_ref[side, n, t]
+            for buffer in (last, previous):
                 buffer[side, t, pad : pad + SUB, :] = zero
-            start_halo = ref[1 - side, 0, :, cols]
+            start_halo = halo_ref[side, 0, t]
             start_mine = first[side, t, mine : mine + SUB, :]
             if side == 0:
                 own_part = jnp.where(sub == SUB - 1, pltpu.roll(start_mine, SUB - 1, 0), 0.0)
@@ -357,7 +370,7 @@
                 old_extra = old_extra + missing
                 energy_extra.append(scales.cold * missing)
             first[side, t, edge : edge + SUB, :] = start_halo
-            second[side, t, edge : edge + SUB, :] = ref[1 - side, 1, :, cols] + (
+            second[side, t, edge : edge + SUB, :] = halo_ref[side, 1, t] + (
                 0.5 * scales.pull
             ) * own_part
             second[side, t, mine : mine + SUB, :] = (
@@ -405,7 +418,7 @@
             copies.append(
                 pltpu.make_async_copy(
                     chosen_ref.at[side, :, pl.ds(column, size)],
-                    send_hbm.at[member, :, pl.ds(0, size)],
+                    send_hbm.at[member],
                     send_sem.at[side, n],
                 )
             )
@@ -416,42 +429,53 @@
     change = jnp.sum(change)
     note_ref[...] = jnp.where(
         lane == 0, label, jnp.where(lane == 1, action, jnp.where(lane == 2, change, 0.0))
-    )
-    for member in range(members):
-        copy = pltpu.make_async_copy(
-            note_ref,
-            send_hbm.at[member, :, pl.ds(per_member * LANES, LANES)],
-            note_sem.at[member],
-        )
+    )[0:1]
+    for copy in copies:
+        copy.wait()
+
+
+def place_kernel(got_ref, notes_hbm, out_hbm, labels_ref, sem, note_sem):
+    members = out_hbm.shape[0]
+    me = lax.axis_index("rep")
+    fetch = pltpu.make_async_copy(notes_hbm, labels_ref, note_sem)
+    fetch.start()
+    fetch.wait()
+    copies = []
+    for r in range(members):
+        slot = labels_ref[lax.rem(members + r - me, members), 0].astype(jnp.int32)
+        copy = pltpu.make_async_copy(got_ref.at[r], out_hbm.at[slot], sem.at[r])
         copy.start()
         copies.append(copy)
     for copy in copies:
         copy.wait()
 
 
-def place_kernel(got_hbm, out_hbm, notes_hbm, pieces_ref, labels_ref, load_sem, sem, note_sem):
-    members, _, width = out_hbm.shape
-    notes = got_hbm.at[:, 0, pl.ds(width, LANES)]
-    fetch = pltpu.make_async_copy(notes, labels_ref, note_sem.at[0])
-    fetch.start()
-    keep = pltpu.make_async_copy(notes, notes_hbm, note_sem.at[1])
-    keep.start()
-    loads = []
-    for r in range(members):
-        load = pltpu.make_async_copy(got_hbm.at[r, :, pl.ds(0, width)], pieces_ref.at[r], load_sem.at[r])
-        load.start()
-        loads.append(load)
-    fetch.wait()
-    copies = []
-    for r in range(members):
-        loads[r].wait()
-        slot = labels_ref[r, 0].astype(jnp.int32)
-        copy = pltpu.make_async_copy(pieces_ref.at[r], out_hbm.at[slot], sem.at[r])
-        copy.start()
-        copies.append(copy)
-    keep.wait()
-    for copy in copies:
-        copy.wait()
+def ladder_kernel(sites, notes_ref, both_ref, label_ref, change_ref, ladder_ref):
+    notes = notes_ref[...]
+    lane = lax.broadcasted_iota(jnp.int32, notes.shape, 1)
+    me = lax.axis_index("rep")
+    mine = (lane == 0) & (notes.astype(jnp.int32) == me)
+    actions = pltpu.roll(notes, LANES - 1, 1)
+    ladder_ref[0] = jnp.sum(jnp.where(mine, actions, 0.0)) / sites
+    both = both_ref[...]
+    place = lax.broadcasted_iota(jnp.int32, both.shape, 1)
+    label_ref[0] = jnp.sum(jnp.where(place == 0, both, 0.0)).astype(jnp.int32)
+    change_ref[0] = jnp.sum(jnp.where(place == 2, both, 0.0))
+
+
+def gather_notes(note, axis, radix=4):
+    count = lax.axis_size(axis)
+    held = note
+    stride = 1
+    while stride < count:
+        parts = [held]
+        for k in range(1, radix):
+            if k * stride < count:
+                pairs = [((i + k * stride) % count, i) for i in range(count)]
+                parts.append(lax.ppermute(held, axis, pairs))
+        held = jnp.concatenate(parts, 0)[:count]
+        stride *= radix
+    return held
 
 
 def body(field, momentum, labels, betas, accept, swap_pairs):
@@ -469,13 +493,14 @@
     smem = pl.BlockSpec(memory_space=pltpu.SMEM)
     vmem = pl.BlockSpec(memory_space=pltpu.VMEM)
     anywhere = pl.BlockSpec(memory_space=pl.ANY)
+    inhbm = pl.BlockSpec(memory_space=pltpu.HBM)
     dma = pltpu.SemaphoreType.DMA
     last16 = rows // (2 * SUB) - 1
     last8 = rows // SUB - 1
     edges = pl.pallas_call(
         pack_kernel,
         grid=(1,),
-        out_shape=jax.ShapeDtypeStruct((2, 2, SUB, width), f32),
+        out_shape=jax.ShapeDtypeStruct((2, 2, tiles, SUB, LANES), f32),
         in_specs=[
             smem,
             smem,
@@ -484,7 +509,7 @@
             pl.BlockSpec((SUB, width), lambda i: (0, 0)),
             pl.BlockSpec((SUB, width), lambda i: (last8, 0)),
         ],
-        out_specs=pl.BlockSpec((2, 2, SUB, width), lambda i: (0, 0, 0, 0)),
+        out_specs=pl.BlockSpec((2, 2, tiles, SUB, LANES), lambda i: (0, 0, 0, 0, 0)),
         name="pack",
     )(labels, betas, start, start, moment, moment)
     forward = [(i, (i + 1) % strips) for i in range(strips)]
@@ -498,13 +523,13 @@
         functools.partial(inner_kernel, per_member),
         out_shape=(
             jax.ShapeDtypeStruct((rows, width), f32),
-            jax.ShapeDtypeStruct((members, SUB, piece + LANES), f32),
+            jax.ShapeDtypeStruct((members, SUB, piece), f32),
             jax.ShapeDtypeStruct((2, 2, tiles, EDGE * SUB, LANES), f32),
             jax.ShapeDtypeStruct((2, tiles, 2 * SUB, LANES), f32),
             jax.ShapeDtypeStruct((3, SUB, LANES), f32),
         ),
-        in_specs=[smem, smem, smem, anywhere, anywhere],
-        out_specs=(anywhere, anywhere, anywhere, anywhere, vmem),
+        in_specs=[smem, smem, smem, inhbm, inhbm],
+        out_specs=(inhbm, inhbm, inhbm, inhbm, vmem),
         scratch_shapes=[
             strip,
             strip,
@@ -520,72 +545,79 @@
         cost_estimate=pl.CostEstimate(
             flops=100 * rows * width, bytes_accessed=16 * rows * width, transcendentals=0
         ),
+        compiler_params=pltpu.CompilerParams(vmem_limit_bytes=WHOLE_VMEM),
         name="inner",
     )(labels, betas, accept, start, moment)
     window = pltpu.VMEM((2, tiles, (EDGE + 2) * SUB, LANES), f32)
     count = 4 + len(halos)
-    out, outgoing = pl.pallas_call(
+    out, outgoing, note = pl.pallas_call(
         functools.partial(outer_kernel, per_member, len(halos)),
         grid=(1,),
         out_shape=(
             jax.ShapeDtypeStruct((rows, width), f32),
-            jax.ShapeDtypeStruct((members, SUB, piece + LANES), f32),
+            jax.ShapeDtypeStruct((members, SUB, piece), f32),
+            jax.ShapeDtypeStruct((1, LANES), f32),
         ),
         in_specs=[smem] * 4
-        + [vmem] * (len(halos) + 3)
+        + [anywhere] * len(halos)
+        + [inhbm, inhbm, vmem]
         + [
             pl.BlockSpec((SUB, width), lambda i: (0, 0)),
             pl.BlockSpec((SUB, width), lambda i: (last8, 0)),
-            anywhere,
-            anywhere,
+            inhbm,
+            inhbm,
         ],
-        out_specs=(anywhere, anywhere),
+        out_specs=(inhbm, inhbm, vmem),
         scratch_shapes=[
             window,
             window,
+            pltpu.VMEM((2, tiles, 2 * SUB, LANES), f32),
+            pltpu.VMEM((2, 2, tiles, SUB, LANES), f32),
             pltpu.VMEM((2, SUB, width), f32),
-            pltpu.VMEM((SUB, LANES), f32),
+            dma((2, 4)),
             dma((2,)),
             dma((2, shares)),
-            dma((members,)),
         ],
         input_output_aliases={count + 5: 0, count + 6: 1},
         name="outer",
     )(labels, betas, accept, swap_pairs, *halos, state, energy, sums, start, start, out, outgoing)
     received = lax.all_to_all(outgoing, "rep", split_axis=0, concat_axis=0, tiled=True)
-    ordered, notes = pl.pallas_call(
+    passing = note
+    both = note
+    for _ in range(strips - 1):
+        passing = lax.ppermute(passing, "dom", forward)
+        both = both + passing
+    both = jnp.where(jnp.arange(LANES)[None, :] == 0, note, both)
+    notes = gather_notes(both, "rep")
+    ordered = pl.pallas_call(
         place_kernel,
-        out_shape=(
-            jax.ShapeDtypeStruct((members, SUB, piece), f32),
-            jax.ShapeDtypeStruct((members, LANES), f32),
-        ),
-        in_specs=[anywhere],
-        out_specs=(anywhere, anywhere),
+        out_shape=jax.ShapeDtypeStruct((members, SUB, piece), f32),
+        in_specs=[anywhere, anywhere],
+        out_specs=inhbm,
         scratch_shapes=[
-            pltpu.VMEM((members, SUB, piece), f32),
             pltpu.SMEM((members, LANES), f32),
             dma((members,)),
-            dma((members,)),
-            dma((2,)),
+            dma,
         ],
+        compiler_params=pltpu.CompilerParams(vmem_limit_bytes=4 << 20),
         name="place",
-    )(received)
+    )(received, notes)
     returned = lax.all_to_all(ordered, "rep", split_axis=0, concat_axis=0, tiled=True)
     returned = returned.reshape(rows // SUB, shares, SUB, piece).transpose(0, 2, 1, 3)
     returned = returned.reshape(1, rows, width)
-    sums = notes
-    passing = notes
-    for _ in range(strips - 1):
-        passing = lax.ppermute(passing, "dom", forward)
-        sums = sums + passing
-    me = lax.axis_index("rep")
-    ladder_index = jnp.arange(betas.shape[0], dtype=jnp.int32)
-    held_labels = notes[:, 0].astype(jnp.int32)
-    sites = strips * rows * width
-    ladder = jnp.sum(jnp.where(held_labels == me, sums[:, 1], 0.0)) / sites
-    change = jnp.sum(jnp.where(ladder_index == me, sums[:, 2], 0.0))
-    new_label = jnp.sum(jnp.where(ladder_index == me, held_labels, 0))
-    return (out[None], returned, new_label[None], change[None], ladder[None])
+    new_label, change, ladder = pl.pallas_call(
+        functools.partial(ladder_kernel, strips * rows * width),
+        out_shape=(
+            jax.ShapeDtypeStruct((1,), jnp.int32),
+            jax.ShapeDtypeStruct((1,), f32),
+            jax.ShapeDtypeStruct((1,), f32),
+        ),
+        in_specs=[vmem, vmem],
+        out_specs=(smem, smem, smem),
+        compiler_params=pltpu.CompilerParams(vmem_limit_bytes=4 << 20),
+        name="ladder",
+    )(notes, both)
+    return (out[None], returned, new_label, change, ladder)
 
 
 def solution(mesh):

time: 90.4 us -> 94.5 us (1.045)
  blocking collectives: 34.1 us -> 0 us
  waiting for transfers between devices: 21.9 us -> 45.6 us
  starting transfers between devices: 6.39 us -> 23.4 us
  other arithmetic: 1.96 us -> 0.01 us
  between operations: 3.77 us -> 2 us
  Pallas kernels: 20 us -> 21.5 us
    all_to_all x1 -> x0, blocking collectives: 34.1 us -> none  [body(): lax.all_to_all(outgoing, 'rep', split_axis=0, concat_axis=0, tiled=True)]
    ppermute x0 -> x6, waiting for transfers between devices: none -> 18.9 us  [gather_notes(): parts.append(lax.ppermute(held, axis, pairs))]
    all_to_all x0 -> x1, starting transfers between devices: none -> 6.84 us  [body(): lax.all_to_all(outgoing, 'rep', split_axis=0, concat_axis=0, tiled=True)]
    ppermute x0 -> x6, starting transfers between devices: none -> 6.35 us  [gather_notes(): parts.append(lax.ppermute(held, axis, pairs))]
    all_to_all x1, waiting for transfers between devices: 20 us -> 24.2 us  [body(): lax.all_to_all(ordered, 'rep', split_axis=0, concat_axis=0, tiled=True)]
    all_to_all x1, starting transfers between devices: 4.86 us -> 8.71 us  [body(): lax.all_to_all(ordered, 'rep', split_axis=0, concat_axis=0, tiled=True)]
    reduce_sum x3 -> x0, other arithmetic: 1.84 us -> none  [the longest x1 0.64 us: body(): new_label = jnp.sum(jnp.where(ladder_index == me, held_labels, 0))]
    pallas_call x1, Pallas kernels: 3.59 us -> 4.79 us  [body(): pl.pallas_call(functools.partial(outer_kernel, per_member, len(halos)), g...]
  transfers between devices with their start and end apart: 3 -> 10, of which waited for: 2 -> 6; matrix products, arithmetic and copies ran while one was open for 2% -> 0% of each run, Pallas kernels for 14% -> 14%
where the time goes in v3:
time: 94.5 us; the launch traced here: 94.1 us
  waiting for transfers between devices  45.6 us (48%)
  starting transfers between devices  23.4 us (25%)
  Pallas kernels  21.5 us (23%)
  between operations  2 us (2%)
  local copies, waits for them, and re-layouts  1.66 us (2%)
    all_to_all x1, waiting for transfers between devices, body(): lax.all_to_all(ordered, 'rep', split_axis=0, concat_axis=0, tiled=True)  24.2 us
    ppermute x6, waiting for transfers between devices, gather_notes(): parts.append(lax.ppermute(held, axis, pairs))  18.9 us
    pallas_call x1, Pallas kernels, body(): pl.pallas_call(functools.partial(inner_kernel, per_member), out_shape=(ja...  12.3 us
    all_to_all x1, starting transfers between devices, body(): lax.all_to_all(ordered, 'rep', split_axis=0, concat_axis=0, tiled=True)  8.71 us
    all_to_all x1, starting transfers between devices, body(): lax.all_to_all(outgoing, 'rep', split_axis=0, concat_axis=0, tiled=True)  6.84 us
    ppermute x6, starting transfers between devices, gather_notes(): parts.append(lax.ppermute(held, axis, pairs))  6.35 us
    pallas_call x1, Pallas kernels, body(): pl.pallas_call(functools.partial(outer_kernel, per_member, len(halos)), g...  4.79 us
    ppermute x1, waiting for transfers between devices, body(): passing = lax.ppermute(passing, 'dom', forward)  2.49 us
  transfers between devices with their start and end apart: 10, of which 6 were waited for; matrix products, arithmetic and copies ran while one was open for 0% of the time, Pallas kernels for 14%

profile of v3, /device:TPU:9, one launch (start us, length us, event | category | flops | bytes accessed | tf_op | source)
XLA Modules:
  0.0 94.1 jit_solution(13231178349412023429)
XLA Ops:
  1.3 1.9 %pack.1 = f32[2,2,16,8,128]{4,3,2,1,0:T(8,128)} custom-call(s32[1]{0:T(128)S(6)} %copy.16.labels_ref, f32[16]{0:T(128)} %betas_ref.5, f32[128,2048]{1,0:T(8,128)} %bitcast.4, f32[128,2048]{1,0:T(8,128)} %bitcast.5, f32[128,2048]{1,0:T(8,128)} %bitcast.9, f32[128,2048]{1,0:T(8,128)} %bitcast.10), custom_call_target="tpu_custom_call" | custom-call | tf_op jit(solution)/shard_map/pack/pallas_call | solution.py:500
  3.2 1.2 %collective-permute-start = (f32[2,2,16,8,128]{4,3,2,1,0:T(8,128)}, f32[2,2,16,8,128]{4,3,2,1,0:T(8,128)}, u32[]{:S(2)}, u32[]{:S(2)}) collective-permute-start(f32[2,2,16,8,128]{4,3,2,1,0:T(8,128)} %pack.1), channel_id=1, source_target_pairs={{0,1},{1,0},{2,3},{3,2},{4,5},{5,4},{6,7},{7,6},{8,9},{9,8},{10,11... | collective-permute-start | bytes 786440 | tf_op jit(solution)/shard_map/ppermute | solution.py:517
  5.1 12.3 %inner.1 = (f32[128,2048]{1,0:T(8,128)}, f32[16,8,2048]{2,1,0:T(8,128)}, f32[2,2,16,24,128]{4,3,2,1,0:T(8,128)}, f32[2,16,16,128]{3,2,1,0:T(8,128)}, f32[3,8,128]{2,1,0:T(8,128)}) custom-call(s32[1]{0:T(128)S(6)} %copy.16.labels_ref, f32[16]{0:T(128)} %betas_ref.5, s32[1]{0:T(128)S(6)} %copy.17.accept_ref, f32[128,2048]{1,0:T(8,128)} %bitcast.6, ...), custom_call_target="tpu_custom_call" | custom-call | flops 26214400 | bytes 4194304 | tf_op jit(solution)/shard_map/inner/pallas_call | solution.py:522
  17.4 0.0 collective-permute-done.refs_0_
  17.4 4.8 %outer.1 = (f32[128,2048]{1,0:T(8,128)}, f32[16,8,2048]{2,1,0:T(8,128)}, f32[1,128]{1,0:T(1,128)}) custom-call(s32[1]{0:T(128)S(6)} %copy.16.labels_ref, f32[16]{0:T(128)} %betas_ref.5, s32[1]{0:T(128)S(6)} %copy.17.accept_ref, s32[16]{0:T(128)} %swap_ref.1, ...), custom_call_target="tpu_custom_call", output_to_operand_aliasing={{0}: (10, {}), {1}: (11, {})} | custom-call | tf_op jit(solution)/shard_map/outer/pallas_call | solution.py:553
  22.2 6.8 %all-to-all-start = ((f32[16,8,2048]{2,1,0:T(8,128)}), f32[16,8,2048]{2,1,0:T(8,128)S(1)}, u32[]{:S(2)}, u32[]{:S(2)}) async-start(f32[16,8,2048]{2,1,0:T(8,128)} %get-tuple-element.22), calls=%async_computation | async-start | bytes 2097152 | tf_op jit(solution)/shard_map/all_to_all | solution.py:584
  29.0 0.0 copy-start
  29.1 0.6 copy-done
  29.7 0.2 collective-permute-start.1
  29.9 2.5 %collective-permute-done.1 = f32[1,128]{1,0:T(1,128)S(1)} collective-permute-done((f32[1,128]{1,0:T(1,128)S(1)}, f32[1,128]{1,0:T(1,128)S(1)}, u32[]{:S(2)}, u32[]{:S(2)}) %collective-permute-start.1) | collective-permute-done | bytes 544 | tf_op jit(solution)/shard_map/ppermute | solution.py:588
  32.4 2.3 %collective-permute-start.4 = (f32[1,128]{1,0:T(1,128)S(1)}, f32[1,128]{1,0:T(1,128)S(1)}, u32[]{:S(2)}, u32[]{:S(2)}) collective-permute-start(f32[1,128]{1,0:T(1,128)S(1)} %compare_select_fusion.both_ref), channel_id=1, source_target_pairs={{6,0},{8,2},{10,4},{12,6},{14,8},{16,10},{18,12},{20,14},{22,16},{... | collective-permute-start | bytes 1544 | tf_op jit(solution)/shard_map/ppermute | solution.py:475
  34.7 0.0 collective-permute-start.3
  34.7 2.5 %collective-permute-start.2 = (f32[1,128]{1,0:T(1,128)S(1)}, f32[1,128]{1,0:T(1,128)S(1)}, u32[]{:S(2)}, u32[]{:S(2)}) collective-permute-start(f32[1,128]{1,0:T(1,128)S(1)} %compare_select_fusion.both_ref), channel_id=1, source_target_pairs={{2,0},{4,2},{6,4},{8,6},{10,8},{12,10},{14,12},{16,14},{18,16},{20... | collective-permute-start | bytes 1544 | tf_op jit(solution)/shard_map/ppermute | solution.py:475
  37.3 16.7 %collective-permute-done.4 = f32[1,128]{1,0:T(1,128)S(1)} collective-permute-done((f32[1,128]{1,0:T(1,128)S(1)}, f32[1,128]{1,0:T(1,128)S(1)}, u32[]{:S(2)}, u32[]{:S(2)}) %collective-permute-start.4) | collective-permute-done | bytes 544 | tf_op jit(solution)/shard_map/ppermute | solution.py:475
  54.0 0.0 collective-permute-done.3
  54.0 0.0 collective-permute-done.2
  54.0 0.1 collective-permute-start.7
  54.0 0.1 collective-permute-start.6
  54.1 1.4 %collective-permute-start.5 = (f32[4,128]{1,0:T(4,128)S(1)}, f32[4,128]{1,0:T(4,128)S(1)}, u32[]{:S(2)}, u32[]{:S(2)}) collective-permute-start(f32[4,128]{1,0:T(4,128)S(1)} %pad_maximum_fusion), channel_id=1, source_target_pairs={{8,0},{10,2},{12,4},{14,6},{16,8},{18,10},{20,12},{22,14},{24,16},... | collective-permute-start | bytes 6152 | tf_op jit(solution)/shard_map/ppermute | solution.py:475
  55.5 1.0 %collective-permute-done.7 = f32[4,128]{1,0:T(4,128)S(1)} collective-permute-done((f32[4,128]{1,0:T(4,128)S(1)}, f32[4,128]{1,0:T(4,128)S(1)}, u32[]{:S(2)}, u32[]{:S(2)}) %collective-permute-start.7) | collective-permute-done | bytes 2080 | tf_op jit(solution)/shard_map/ppermute | solution.py:475
  56.5 1.0 %collective-permute-done.6 = f32[4,128]{1,0:T(4,128)S(1)} collective-permute-done((f32[4,128]{1,0:T(4,128)S(1)}, f32[4,128]{1,0:T(4,128)S(1)}, u32[]{:S(2)}, u32[]{:S(2)}) %collective-permute-start.6) | collective-permute-done | bytes 2080 | tf_op jit(solution)/shard_map/ppermute | solution.py:475
  57.4 0.2 collective-permute-done.5
  57.7 0.0 all-to-all-done.got_ref
  57.7 1.8 %place.1 = f32[16,8,2048]{2,1,0:T(8,128)} custom-call(f32[16,8,2048]{2,1,0:T(8,128)S(1)} %all-to-all-done.got_ref, f32[16,128]{1,0:T(8,128)S(1)} %concatenate.8.notes_hbm.notes_ref), custom_call_target="tpu_custom_call" | custom-call | tf_op jit(solution)/shard_map/place/pallas_call | solution.py:592
  59.5 8.7 %all-to-all-start.1 = ((f32[16,8,2048]{2,1,0:T(8,128)}), f32[16,8,2048]{2,1,0:T(8,128)S(1)}, u32[]{:S(2)}, u32[]{:S(2)}) async-start(f32[16,8,2048]{2,1,0:T(8,128)} %place.1), calls=%async_computation.1 | async-start | bytes 2097152 | tf_op jit(solution)/shard_map/all_to_all | solution.py:605
  68.2 0.7 ladder.1
  68.9 24.2 %all-to-all-done.1 = f32[16,8,2048]{2,1,0:T(8,128)S(1)} async-done(((f32[16,8,2048]{2,1,0:T(8,128)}), f32[16,8,2048]{2,1,0:T(8,128)S(1)}, u32[]{:S(2)}, u32[]{:S(2)}) %all-to-all-start.1) | async-done | bytes 1048608 | tf_op jit(solution)/shard_map/all_to_all | solution.py:605
  93.1 1.0 %copy.18 = f32[1,128,2048]{2,1,0:T(8,128)} copy(f32[1,128,2048]{2,1,0:T(8,128)S(1)} %bitcast.12) | data formatting | bytes 2097152
  (3 shorter events, 0.1 us)
Async XLA Ops:
  3.2 14.2 %collective-permute-start = (f32[2,2,16,8,128]{4,3,2,1,0:T(8,128)}, f32[2,2,16,8,128]{4,3,2,1,0:T(8,128)}, u32[]{:S(2)}, u32[]{:S(2)}) collective-permute-start(f32[2,2,16,8,128]{4,3,2,1,0:T(8,128)} %pack.1), channel_id=1, source_target_pairs={{0,1},{1,0},{2,3},{3,2},{4,5},{5,4},{6,7},{7,6},{8,9},{9,8},{10,11... | collective-permute-start | bytes 786440 | tf_op jit(solution)/shard_map/ppermute | solution.py:517
  22.2 35.5 %all-to-all-start = ((f32[16,8,2048]{2,1,0:T(8,128)}), f32[16,8,2048]{2,1,0:T(8,128)S(1)}, u32[]{:S(2)}, u32[]{:S(2)}) async-start(f32[16,8,2048]{2,1,0:T(8,128)} %get-tuple-element.22), calls=%async_computation | async-start | bytes 2097152 | tf_op jit(solution)/shard_map/all_to_all | solution.py:584
  29.0 0.7 copy-start
  29.7 2.7 %collective-permute-start.1 = (f32[1,128]{1,0:T(1,128)S(1)}, f32[1,128]{1,0:T(1,128)S(1)}, u32[]{:S(2)}, u32[]{:S(2)}) collective-permute-start(f32[1,128]{1,0:T(1,128)S(1)} %copy-done), channel_id=1, source_target_pairs={{0,1},{1,0},{2,3},{3,2},{4,5},{5,4},{6,7},{7,6},{8,9},{9,8},{10,11... | collective-permute-start | bytes 1544 | tf_op jit(solution)/shard_map/ppermute | solution.py:588
  32.4 21.5 %collective-permute-start.4 = (f32[1,128]{1,0:T(1,128)S(1)}, f32[1,128]{1,0:T(1,128)S(1)}, u32[]{:S(2)}, u32[]{:S(2)}) collective-permute-start(f32[1,128]{1,0:T(1,128)S(1)} %compare_select_fusion.both_ref), channel_id=1, source_target_pairs={{6,0},{8,2},{10,4},{12,6},{14,8},{16,10},{18,12},{20,14},{22,16},{... | collective-permute-start | bytes 1544 | tf_op jit(solution)/shard_map/ppermute | solution.py:475
  34.7 19.2 %collective-permute-start.3 = (f32[1,128]{1,0:T(1,128)S(1)}, f32[1,128]{1,0:T(1,128)S(1)}, u32[]{:S(2)}, u32[]{:S(2)}) collective-permute-start(f32[1,128]{1,0:T(1,128)S(1)} %compare_select_fusion.both_ref), channel_id=1, source_target_pairs={{4,0},{6,2},{8,4},{10,6},{12,8},{14,10},{16,12},{18,14},{20,16},{2... | collective-permute-start | bytes 1544 | tf_op jit(solution)/shard_map/ppermute | solution.py:475
  34.7 19.2 %collective-permute-start.2 = (f32[1,128]{1,0:T(1,128)S(1)}, f32[1,128]{1,0:T(1,128)S(1)}, u32[]{:S(2)}, u32[]{:S(2)}) collective-permute-start(f32[1,128]{1,0:T(1,128)S(1)} %compare_select_fusion.both_ref), channel_id=1, source_target_pairs={{2,0},{4,2},{6,4},{8,6},{10,8},{12,10},{14,12},{16,14},{18,16},{20... | collective-permute-start | bytes 1544 | tf_op jit(solution)/shard_map/ppermute | solution.py:475
  54.0 2.5 %collective-permute-start.7 = (f32[4,128]{1,0:T(4,128)S(1)}, f32[4,128]{1,0:T(4,128)S(1)}, u32[]{:S(2)}, u32[]{:S(2)}) collective-permute-start(f32[4,128]{1,0:T(4,128)S(1)} %pad_maximum_fusion), channel_id=1, source_target_pairs={{24,0},{26,2},{28,4},{30,6},{0,8},{2,10},{4,12},{6,14},{8,16},{10,... | collective-permute-start | bytes 6152 | tf_op jit(solution)/shard_map/ppermute | solution.py:475
  54.0 3.4 %collective-permute-start.6 = (f32[4,128]{1,0:T(4,128)S(1)}, f32[4,128]{1,0:T(4,128)S(1)}, u32[]{:S(2)}, u32[]{:S(2)}) collective-permute-start(f32[4,128]{1,0:T(4,128)S(1)} %pad_maximum_fusion), channel_id=1, source_target_pairs={{16,0},{18,2},{20,4},{22,6},{24,8},{26,10},{28,12},{30,14},{0,16},... | collective-permute-start | bytes 6152 | tf_op jit(solution)/shard_map/ppermute | solution.py:475
  54.1 3.5 %collective-permute-start.5 = (f32[4,128]{1,0:T(4,128)S(1)}, f32[4,128]{1,0:T(4,128)S(1)}, u32[]{:S(2)}, u32[]{:S(2)}) collective-permute-start(f32[4,128]{1,0:T(4,128)S(1)} %pad_maximum_fusion), channel_id=1, source_target_pairs={{8,0},{10,2},{12,4},{14,6},{16,8},{18,10},{20,12},{22,14},{24,16},... | collective-permute-start | bytes 6152 | tf_op jit(solution)/shard_map/ppermute | solution.py:475
  59.5 33.6 %all-to-all-start.1 = ((f32[16,8,2048]{2,1,0:T(8,128)}), f32[16,8,2048]{2,1,0:T(8,128)S(1)}, u32[]{:S(2)}, u32[]{:S(2)}) async-start(f32[16,8,2048]{2,1,0:T(8,128)} %place.1), calls=%async_computation.1 | async-start | bytes 2097152 | tf_op jit(solution)/shard_map/all_to_all | solution.py:605

commit v4 on v2

--- a/solution.py
+++ b/solution.py
@@ -16,6 +16,7 @@
 LANES = 128
 EDGE = 3
 GROUP = 7
+WHOLE_VMEM = 67043328
 
 
 def lane_index():
@@ -104,8 +105,8 @@
                 up = jnp.where(row == 0, pltpu.roll(other, 1, 0), up)
                 down = jnp.where(row == SUB - 1, 0.0, down)
             push = scales.speed * m_ref[:, cols] + scales.half((up + down) + sums[i], values[i])
-            out_ref[side, 0, :, cols] = values[i]
-            out_ref[side, 1, :, cols] = values[i] + push
+            out_ref[side, 0, i] = values[i]
+            out_ref[side, 1, i] = values[i] + push
 
 
 def slots(row_block, tiles, per_member):
@@ -120,7 +121,6 @@
     accept_ref,
     field_hbm,
     momentum_hbm,
-    out_hbm,
     send_hbm,
     state_hbm,
     energy_hbm,
@@ -132,7 +132,6 @@
     second,
     energy,
     in_sem,
-    out_sem,
     send_sem,
     state_sem,
 ):
@@ -221,11 +220,7 @@
 
     def emit(block):
         row = block * SUB
-        copies = [
-            pltpu.make_async_copy(
-                chosen_ref.at[pl.ds(row, SUB), :], out_hbm.at[pl.ds(row, SUB), :], out_sem.at[block]
-            )
-        ]
+        copies = []
         for member, column in slots(block, tiles, per_member):
             width_here = per_member * LANES
             copies.append(
@@ -305,23 +300,37 @@
 ):
     halo_refs = refs[:halos]
     (
-        state_ref,
-        energy_ref,
+        state_hbm,
+        energy_hbm,
         sums_ref,
         head_ref,
         tail_ref,
         _,
-        _,
-        out_hbm,
         send_hbm,
         first,
         second,
+        energy_ref,
+        halo_ref,
         chosen_ref,
         note_ref,
-        out_sem,
+        in_sem,
         send_sem,
         note_sem,
     ) = refs[halos:]
+    last, previous = (first, second) if STEPS % 2 == 0 else (second, first)
+    loads = []
+    for side in range(2):
+        own = 2 * SUB if side == 0 else 0
+        parts = [
+            (state_hbm.at[side, n], buffer.at[side, :, pl.ds(own, EDGE * SUB), :])
+            for n, buffer in enumerate((last, previous))
+        ]
+        parts.append((halo_refs[side % halos].at[1 - side], halo_ref.at[side]))
+        parts.append((energy_hbm.at[side], energy_ref.at[side]))
+        for n, (source, target) in enumerate(parts):
+            copy = pltpu.make_async_copy(source, target, in_sem.at[side, n])
+            copy.start()
+            loads.append(copy)
     scales = Scales(chosen_scalars(labels_ref, betas_ref))
     label = swap_ref[labels_ref[0]].astype(jnp.float32)
     accepted = accept_ref[0] == 1
@@ -329,23 +338,20 @@
     sub = row_index()
     tiles = first.shape[1]
     members = send_hbm.shape[0]
-    blocks = out_hbm.shape[0] // SUB
+    blocks = members * per_member // tiles
     zero = jnp.zeros((SUB, LANES), jnp.float32)
-    last, previous = (first, second) if STEPS % 2 == 0 else (second, first)
     old_extra = zero
     energy_extra = []
+    for copy in loads:
+        copy.wait()
     for side in range(2):
-        ref = halo_refs[side % halos]
-        own = 2 * SUB if side == 0 else 0
         edge = SUB if side == 0 else EDGE * SUB
         pad = 0 if side == 0 else (EDGE + 1) * SUB
-        mine = own if side == 0 else (EDGE - 1) * SUB
+        mine = 2 * SUB if side == 0 else (EDGE - 1) * SUB
         for t in range(tiles):
-            cols = pl.ds(t * LANES, LANES)
-            for n, buffer in enumerate((last, previous)):
-                buffer[side, t, own : own + EDGE * SUB, :] = state_ref[side, n, t]
+            for buffer in (last, previous):
                 buffer[side, t, pad : pad + SUB, :] = zero
-            start_halo = ref[1 - side, 0, :, cols]
+            start_halo = halo_ref[side, 0, t]
             start_mine = first[side, t, mine : mine + SUB, :]
             if side == 0:
                 own_part = jnp.where(sub == SUB - 1, pltpu.roll(start_mine, SUB - 1, 0), 0.0)
@@ -357,7 +363,7 @@
                 old_extra = old_extra + missing
                 energy_extra.append(scales.cold * missing)
             first[side, t, edge : edge + SUB, :] = start_halo
-            second[side, t, edge : edge + SUB, :] = ref[1 - side, 1, :, cols] + (
+            second[side, t, edge : edge + SUB, :] = halo_ref[side, 1, t] + (
                 0.5 * scales.pull
             ) * own_part
             second[side, t, mine : mine + SUB, :] = (
@@ -395,11 +401,6 @@
                     kept = head_ref[:, cols] if side == 0 else tail_ref[:, cols]
                     chosen_ref[side, :, cols] = jnp.where(accepted, scales.back * values[t], kept)
         block = 0 if side == 0 else blocks - 1
-        copies.append(
-            pltpu.make_async_copy(
-                chosen_ref.at[side], out_hbm.at[pl.ds(block * SUB, SUB), :], out_sem.at[side]
-            )
-        )
         for n, (member, column) in enumerate(slots(block, tiles, per_member)):
             size = per_member * LANES
             copies.append(
@@ -429,29 +430,37 @@
         copy.wait()
 
 
-def place_kernel(got_hbm, out_hbm, notes_hbm, pieces_ref, labels_ref, load_sem, sem, note_sem):
+def place_kernel(got_ref, _, out_hbm, notes_hbm, labels_ref, sem, note_sem):
     members, _, width = out_hbm.shape
-    notes = got_hbm.at[:, 0, pl.ds(width, LANES)]
+    notes = got_ref.at[:, 0, pl.ds(width, LANES)]
     fetch = pltpu.make_async_copy(notes, labels_ref, note_sem.at[0])
     fetch.start()
     keep = pltpu.make_async_copy(notes, notes_hbm, note_sem.at[1])
     keep.start()
-    loads = []
-    for r in range(members):
-        load = pltpu.make_async_copy(got_hbm.at[r, :, pl.ds(0, width)], pieces_ref.at[r], load_sem.at[r])
-        load.start()
-        loads.append(load)
     fetch.wait()
     copies = []
     for r in range(members):
-        loads[r].wait()
         slot = labels_ref[r, 0].astype(jnp.int32)
-        copy = pltpu.make_async_copy(pieces_ref.at[r], out_hbm.at[slot], sem.at[r])
+        copy = pltpu.make_async_copy(got_ref.at[r, :, pl.ds(0, width)], out_hbm.at[slot], sem.at[r])
         copy.start()
         copies.append(copy)
     keep.wait()
     for copy in copies:
         copy.wait()
+
+
+def ladder_kernel(sites, notes_ref, sums_ref, label_ref, change_ref, ladder_ref):
+    me = lax.axis_index("rep")
+    notes = notes_ref[...]
+    sums = sums_ref[...]
+    lane = lax.broadcasted_iota(jnp.int32, notes.shape, 1)
+    replica = lax.broadcasted_iota(jnp.int32, notes.shape, 0)
+    held = (lane == 0) & (notes.astype(jnp.int32) == me)
+    actions = pltpu.roll(sums, LANES - 1, 1)
+    ladder_ref[0] = jnp.sum(jnp.where(held, actions, 0.0)) / sites
+    own = replica == me
+    label_ref[0] = jnp.sum(jnp.where(own & (lane == 0), notes, 0.0)).astype(jnp.int32)
+    change_ref[0] = jnp.sum(jnp.where(own & (lane == 2), sums, 0.0))
 
 
 def body(field, momentum, labels, betas, accept, swap_pairs):
@@ -469,13 +478,14 @@
     smem = pl.BlockSpec(memory_space=pltpu.SMEM)
     vmem = pl.BlockSpec(memory_space=pltpu.VMEM)
     anywhere = pl.BlockSpec(memory_space=pl.ANY)
+    inhbm = pl.BlockSpec(memory_space=pltpu.HBM)
     dma = pltpu.SemaphoreType.DMA
     last16 = rows // (2 * SUB) - 1
     last8 = rows // SUB - 1
     edges = pl.pallas_call(
         pack_kernel,
         grid=(1,),
-        out_shape=jax.ShapeDtypeStruct((2, 2, SUB, width), f32),
+        out_shape=jax.ShapeDtypeStruct((2, 2, tiles, SUB, LANES), f32),
         in_specs=[
             smem,
             smem,
@@ -484,7 +494,7 @@
             pl.BlockSpec((SUB, width), lambda i: (0, 0)),
             pl.BlockSpec((SUB, width), lambda i: (last8, 0)),
         ],
-        out_specs=pl.BlockSpec((2, 2, SUB, width), lambda i: (0, 0, 0, 0)),
+        out_specs=pl.BlockSpec((2, 2, tiles, SUB, LANES), lambda i: (0, 0, 0, 0, 0)),
         name="pack",
     )(labels, betas, start, start, moment, moment)
     forward = [(i, (i + 1) % strips) for i in range(strips)]
@@ -492,19 +502,23 @@
     halos = (lax.ppermute(edges, "dom", forward),)
     if strips > 2:
         halos = halos + (lax.ppermute(edges, "dom", backward),)
+
+    def strip_of(pieces):
+        grouped = pieces.reshape(rows // SUB, shares, SUB, piece).transpose(0, 2, 1, 3)
+        return grouped.reshape(1, rows, width)
+
     column = pltpu.VMEM((tiles, rows + 2 * SUB, LANES), f32)
     strip = pltpu.VMEM((rows, width), f32)
-    out, outgoing, state, energy, sums = pl.pallas_call(
+    outgoing, state, energy, sums = pl.pallas_call(
         functools.partial(inner_kernel, per_member),
         out_shape=(
-            jax.ShapeDtypeStruct((rows, width), f32),
             jax.ShapeDtypeStruct((members, SUB, piece + LANES), f32),
             jax.ShapeDtypeStruct((2, 2, tiles, EDGE * SUB, LANES), f32),
             jax.ShapeDtypeStruct((2, tiles, 2 * SUB, LANES), f32),
             jax.ShapeDtypeStruct((3, SUB, LANES), f32),
         ),
-        in_specs=[smem, smem, smem, anywhere, anywhere],
-        out_specs=(anywhere, anywhere, anywhere, anywhere, vmem),
+        in_specs=[smem, smem, smem, inhbm, inhbm],
+        out_specs=(inhbm, inhbm, inhbm, vmem),
         scratch_shapes=[
             strip,
             strip,
@@ -513,79 +527,81 @@
             column,
             pltpu.VMEM((tiles, rows, LANES), f32),
             dma((2, 8)),
-            dma((rows // SUB,)),
             dma((members,)),
             dma((2, 3)),
         ],
         cost_estimate=pl.CostEstimate(
             flops=100 * rows * width, bytes_accessed=16 * rows * width, transcendentals=0
         ),
+        compiler_params=pltpu.CompilerParams(vmem_limit_bytes=WHOLE_VMEM),
         name="inner",
     )(labels, betas, accept, start, moment)
     window = pltpu.VMEM((2, tiles, (EDGE + 2) * SUB, LANES), f32)
     count = 4 + len(halos)
-    out, outgoing = pl.pallas_call(
+    outgoing = pl.pallas_call(
         functools.partial(outer_kernel, per_member, len(halos)),
         grid=(1,),
-        out_shape=(
-            jax.ShapeDtypeStruct((rows, width), f32),
-            jax.ShapeDtypeStruct((members, SUB, piece + LANES), f32),
-        ),
+        out_shape=jax.ShapeDtypeStruct((members, SUB, piece + LANES), f32),
         in_specs=[smem] * 4
-        + [vmem] * (len(halos) + 3)
+        + [anywhere] * len(halos)
+        + [inhbm, inhbm, vmem]
         + [
             pl.BlockSpec((SUB, width), lambda i: (0, 0)),
             pl.BlockSpec((SUB, width), lambda i: (last8, 0)),
-            anywhere,
-            anywhere,
+            inhbm,
         ],
-        out_specs=(anywhere, anywhere),
+        out_specs=inhbm,
         scratch_shapes=[
             window,
             window,
+            pltpu.VMEM((2, tiles, 2 * SUB, LANES), f32),
+            pltpu.VMEM((2, 2, tiles, SUB, LANES), f32),
             pltpu.VMEM((2, SUB, width), f32),
             pltpu.VMEM((SUB, LANES), f32),
-            dma((2,)),
+            dma((2, 4)),
             dma((2, shares)),
             dma((members,)),
         ],
-        input_output_aliases={count + 5: 0, count + 6: 1},
+        input_output_aliases={count + 5: 0},
         name="outer",
-    )(labels, betas, accept, swap_pairs, *halos, state, energy, sums, start, start, out, outgoing)
+    )(labels, betas, accept, swap_pairs, *halos, state, energy, sums, start, start, outgoing)
     received = lax.all_to_all(outgoing, "rep", split_axis=0, concat_axis=0, tiled=True)
+    out = strip_of(outgoing[:, :, :piece])
     ordered, notes = pl.pallas_call(
         place_kernel,
         out_shape=(
             jax.ShapeDtypeStruct((members, SUB, piece), f32),
             jax.ShapeDtypeStruct((members, LANES), f32),
         ),
-        in_specs=[anywhere],
-        out_specs=(anywhere, anywhere),
+        in_specs=[anywhere, anywhere],
+        out_specs=(inhbm, inhbm),
         scratch_shapes=[
-            pltpu.VMEM((members, SUB, piece), f32),
             pltpu.SMEM((members, LANES), f32),
-            dma((members,)),
             dma((members,)),
             dma((2,)),
         ],
+        compiler_params=pltpu.CompilerParams(vmem_limit_bytes=4 << 20),
         name="place",
-    )(received)
+    )(received, out)
     returned = lax.all_to_all(ordered, "rep", split_axis=0, concat_axis=0, tiled=True)
-    returned = returned.reshape(rows // SUB, shares, SUB, piece).transpose(0, 2, 1, 3)
-    returned = returned.reshape(1, rows, width)
-    sums = notes
     passing = notes
+    both = notes
     for _ in range(strips - 1):
         passing = lax.ppermute(passing, "dom", forward)
-        sums = sums + passing
-    me = lax.axis_index("rep")
-    ladder_index = jnp.arange(betas.shape[0], dtype=jnp.int32)
-    held_labels = notes[:, 0].astype(jnp.int32)
-    sites = strips * rows * width
-    ladder = jnp.sum(jnp.where(held_labels == me, sums[:, 1], 0.0)) / sites
-    change = jnp.sum(jnp.where(ladder_index == me, sums[:, 2], 0.0))
-    new_label = jnp.sum(jnp.where(ladder_index == me, held_labels, 0))
-    return (out[None], returned, new_label[None], change[None], ladder[None])
+        both = both + passing
+    new_label, change, ladder = pl.pallas_call(
+        functools.partial(ladder_kernel, strips * rows * width),
+        out_shape=(
+            jax.ShapeDtypeStruct((1,), jnp.int32),
+            jax.ShapeDtypeStruct((1,), f32),
+            jax.ShapeDtypeStruct((1,), f32),
+        ),
+        in_specs=[vmem, vmem],
+        out_specs=(smem, smem, smem),
+        compiler_params=pltpu.CompilerParams(vmem_limit_bytes=4 << 20),
+        name="ladder",
+    )(notes, both)
+    return (out, strip_of(returned), new_label, change, ladder)
 
 
 def solution(mesh):

time: 90.4 us -> 87.8 us (0.971)
  blocking collectives: 34.1 us -> 0 us
  waiting for transfers between devices: 21.9 us -> 50.1 us
  starting transfers between devices: 6.39 us -> 13.3 us
  other arithmetic: 1.96 us -> 0.01 us
  between operations: 3.77 us -> 2.01 us
    all_to_all x1 -> x0, blocking collectives: 34.1 us -> none  [body(): lax.all_to_all(outgoing, 'rep', split_axis=0, concat_axis=0, tiled=True)]
    all_to_all x0 -> x1, waiting for transfers between devices: none -> 26.1 us  [body(): lax.all_to_all(outgoing, 'rep', split_axis=0, concat_axis=0, tiled=True)]
    all_to_all x0 -> x1, starting transfers between devices: none -> 6.97 us  [body(): lax.all_to_all(outgoing, 'rep', split_axis=0, concat_axis=0, tiled=True)]
    reduce_sum x3 -> x0, other arithmetic: 1.84 us -> none  [the longest x1 0.64 us: body(): new_label = jnp.sum(jnp.where(ladder_index == me, held_labels, 0))]
    all_to_all x1, waiting for transfers between devices: 20 us -> 21.4 us  [body(): lax.all_to_all(ordered, 'rep', split_axis=0, concat_axis=0, tiled=True)]
    pallas_call x1, Pallas kernels: 3.59 us -> 4.62 us  [body(): pl.pallas_call(functools.partial(outer_kernel, per_member, len(halos)), g...]
  transfers between devices with their start and end apart: 3 -> 4, of which waited for: 2 -> 3; matrix products, arithmetic and copies ran while one was open for 2% -> 0% of each run, Pallas kernels for 14% -> 14%
where the time goes in v4:
time: 87.8 us; the launch traced here: 87.3 us
  waiting for transfers between devices  50.1 us (57%)
  Pallas kernels  20.9 us (24%)
  starting transfers between devices  13.3 us (15%)
  between operations  2.01 us (2%)
  local copies, waits for them, and re-layouts  1.07 us (1%)
    all_to_all x1, waiting for transfers between devices, body(): lax.all_to_all(outgoing, 'rep', split_axis=0, concat_axis=0, tiled=True)  26.1 us
    all_to_all x1, waiting for transfers between devices, body(): lax.all_to_all(ordered, 'rep', split_axis=0, concat_axis=0, tiled=True)  21.4 us
    pallas_call x1, Pallas kernels, body(): pl.pallas_call(functools.partial(inner_kernel, per_member), out_shape=(ja...  11.9 us
    all_to_all x1, starting transfers between devices, body(): lax.all_to_all(outgoing, 'rep', split_axis=0, concat_axis=0, tiled=True)  6.97 us
    all_to_all x1, starting transfers between devices, body(): lax.all_to_all(ordered, 'rep', split_axis=0, concat_axis=0, tiled=True)  4.85 us
    pallas_call x1, Pallas kernels, body(): pl.pallas_call(functools.partial(outer_kernel, per_member, len(halos)), g...  4.62 us
    ppermute x1, waiting for transfers between devices, body(): passing = lax.ppermute(passing, 'dom', forward)  2.57 us
    pallas_call x1, Pallas kernels, body(): pl.pallas_call(pack_kernel, grid=(1,), out_shape=jax.ShapeDtypeStruct((2,...  1.87 us
  transfers between devices with their start and end apart: 4, of which 3 were waited for; matrix products, arithmetic and copies ran while one was open for 0% of the time, Pallas kernels for 14%

profile of v4, /device:TPU:9, one launch (start us, length us, event | category | flops | bytes accessed | tf_op | source)
XLA Modules:
  0.0 87.3 jit_solution(14343189657394651244)
XLA Ops:
  1.3 1.9 %pack.1 = f32[2,2,16,8,128]{4,3,2,1,0:T(8,128)} custom-call(s32[1]{0:T(128)S(6)} %copy.14.labels_ref, f32[16]{0:T(128)} %betas_ref.5, f32[128,2048]{1,0:T(8,128)} %bitcast.5, f32[128,2048]{1,0:T(8,128)} %bitcast.6, f32[128,2048]{1,0:T(8,128)} %bitcast.10, f32[128,2048]{1,0:T(8,128)} %bitcast.11), custom_call_target="tpu_custom_call" | custom-call | tf_op jit(solution)/shard_map/pack/pallas_call | solution.py:485
  3.2 1.2 %collective-permute-start = (f32[2,2,16,8,128]{4,3,2,1,0:T(8,128)}, f32[2,2,16,8,128]{4,3,2,1,0:T(8,128)}, u32[]{:S(2)}, u32[]{:S(2)}) collective-permute-start(f32[2,2,16,8,128]{4,3,2,1,0:T(8,128)} %pack.1), channel_id=1, source_target_pairs={{0,1},{1,0},{2,3},{3,2},{4,5},{5,4},{6,7},{7,6},{8,9},{9,8},{10,11... | collective-permute-start | bytes 786440 | tf_op jit(solution)/shard_map/ppermute | solution.py:502
  5.0 11.9 %inner.1 = (f32[16,8,2176]{2,1,0:T(8,128)}, f32[2,2,16,24,128]{4,3,2,1,0:T(8,128)}, f32[2,16,16,128]{3,2,1,0:T(8,128)}, f32[3,8,128]{2,1,0:T(8,128)}) custom-call(s32[1]{0:T(128)S(6)} %copy.14.labels_ref, f32[16]{0:T(128)} %betas_ref.5, s32[1]{0:T(128)S(6)} %copy.15.accept_ref, f32[128,2048]{1,0:T(8,128)} %bitcast.7, f32[128,2048]{1,0:T(8,128)} %bitcast.12), custom_call_target="tpu_custom_call" | custom-call | flops 26214400 | bytes 4194304 | tf_op jit(solution)/shard_map/inner/pallas_call | solution.py:512
  16.9 0.0 collective-permute-done.refs_0_
  16.9 4.6 %outer.1 = f32[16,8,2176]{2,1,0:T(8,128)} custom-call(s32[1]{0:T(128)S(6)} %copy.14.labels_ref, f32[16]{0:T(128)} %betas_ref.5, s32[1]{0:T(128)S(6)} %copy.15.accept_ref, s32[16]{0:T(128)} %swap_ref.1, f32[2,2,16,8,128]{4,3,2,1,0:T(8,128)} %collective-permute-done.refs_0_, ...), custom_call_target="tpu_custom_call", output_to_operand_aliasing={{}: (10, {})} | custom-call | tf_op jit(solution)/shard_map/outer/pallas_call | solution.py:541
  21.6 0.0 copy-start.1
  21.6 7.0 %all-to-all-start = ((f32[16,8,2176]{2,1,0:T(8,128)}), f32[16,8,2176]{2,1,0:T(8,128)S(1)}, u32[]{:S(2)}, u32[]{:S(2)}) async-start(f32[16,8,2176]{2,1,0:T(8,128)} %outer.1), calls=%async_computation | async-start | bytes 2228224 | tf_op jit(solution)/shard_map/all_to_all | solution.py:568
  28.6 0.0 copy-done.1
  28.6 0.1 slice_bitcast_fusion._
  28.7 0.0 copy-start
  28.7 26.1 %all-to-all-done.got_ref = f32[16,8,2176]{2,1,0:T(8,128)S(1)} async-done(((f32[16,8,2176]{2,1,0:T(8,128)}), f32[16,8,2176]{2,1,0:T(8,128)S(1)}, u32[]{:S(2)}, u32[]{:S(2)}) %all-to-all-start) | async-done | bytes 1114144 | tf_op jit(solution)/shard_map/all_to_all | solution.py:568
  54.8 1.8 %place.1 = (f32[16,8,2048]{2,1,0:T(8,128)}, f32[16,128]{1,0:T(8,128)S(1)}) custom-call(f32[16,8,2176]{2,1,0:T(8,128)S(1)} %all-to-all-done.got_ref, f32[1,128,2048]{2,1,0:T(8,128)S(1)} %slice_bitcast_fusion._), custom_call_target="tpu_custom_call" | custom-call | tf_op jit(solution)/shard_map/place/pallas_call | solution.py:570
  56.6 0.0 copy-done
  56.6 4.9 %all-to-all-start.1 = ((f32[16,8,2048]{2,1,0:T(8,128)}), f32[16,8,2048]{2,1,0:T(8,128)S(1)}, u32[]{:S(2)}, u32[]{:S(2)}) async-start(f32[16,8,2048]{2,1,0:T(8,128)} %get-tuple-element.18), calls=%async_computation.1 | async-start | bytes 2097152 | tf_op jit(solution)/shard_map/all_to_all | solution.py:586
  61.5 0.2 collective-permute-start.1
  61.7 2.6 %collective-permute-done.1 = f32[16,128]{1,0:T(8,128)S(1)} collective-permute-done((f32[16,128]{1,0:T(8,128)S(1)}, f32[16,128]{1,0:T(8,128)S(1)}, u32[]{:S(2)}, u32[]{:S(2)}) %collective-permute-start.1) | collective-permute-done | bytes 8224 | tf_op jit(solution)/shard_map/ppermute | solution.py:590
  64.3 0.7 ladder.1
  65.0 21.4 %all-to-all-done.1 = f32[16,8,2048]{2,1,0:T(8,128)S(1)} async-done(((f32[16,8,2048]{2,1,0:T(8,128)}), f32[16,8,2048]{2,1,0:T(8,128)S(1)}, u32[]{:S(2)}, u32[]{:S(2)}) %all-to-all-start.1) | async-done | bytes 1048608 | tf_op jit(solution)/shard_map/all_to_all | solution.py:586
  86.4 1.0 %copy.16 = f32[1,128,2048]{2,1,0:T(8,128)} copy(f32[1,128,2048]{2,1,0:T(8,128)S(1)} %bitcast.13) | data formatting | bytes 2097152
  (1 shorter events, 0.0 us)
Async XLA Ops:
  3.2 13.8 %collective-permute-start = (f32[2,2,16,8,128]{4,3,2,1,0:T(8,128)}, f32[2,2,16,8,128]{4,3,2,1,0:T(8,128)}, u32[]{:S(2)}, u32[]{:S(2)}) collective-permute-start(f32[2,2,16,8,128]{4,3,2,1,0:T(8,128)} %pack.1), channel_id=1, source_target_pairs={{0,1},{1,0},{2,3},{3,2},{4,5},{5,4},{6,7},{7,6},{8,9},{9,8},{10,11... | collective-permute-start | bytes 786440 | tf_op jit(solution)/shard_map/ppermute | solution.py:502
  21.6 7.0 %copy-start.1 = (f32[16,8,2176]{2,1,0:T(8,128)S(1)}, f32[16,8,2176]{2,1,0:T(8,128)}, u32[]{:S(2)}) copy-start(f32[16,8,2176]{2,1,0:T(8,128)} %outer.1) | copy-start | bytes 3342340
  21.6 33.2 %all-to-all-start = ((f32[16,8,2176]{2,1,0:T(8,128)}), f32[16,8,2176]{2,1,0:T(8,128)S(1)}, u32[]{:S(2)}, u32[]{:S(2)}) async-start(f32[16,8,2176]{2,1,0:T(8,128)} %outer.1), calls=%async_computation | async-start | bytes 2228224 | tf_op jit(solution)/shard_map/all_to_all | solution.py:568
  28.7 27.9 %copy-start = (f32[1,128,2048]{2,1,0:T(8,128)}, f32[1,128,2048]{2,1,0:T(8,128)S(1)}, u32[]{:S(2)}) copy-start(f32[1,128,2048]{2,1,0:T(8,128)S(1)} %slice_bitcast_fusion._) | copy-start | bytes 3145732
  56.6 29.8 %all-to-all-start.1 = ((f32[16,8,2048]{2,1,0:T(8,128)}), f32[16,8,2048]{2,1,0:T(8,128)S(1)}, u32[]{:S(2)}, u32[]{:S(2)}) async-start(f32[16,8,2048]{2,1,0:T(8,128)} %get-tuple-element.18), calls=%async_computation.1 | async-start | bytes 2097152 | tf_op jit(solution)/shard_map/all_to_all | solution.py:586
  61.5 2.8 %collective-permute-start.1 = (f32[16,128]{1,0:T(8,128)S(1)}, f32[16,128]{1,0:T(8,128)S(1)}, u32[]{:S(2)}, u32[]{:S(2)}) collective-permute-start(f32[16,128]{1,0:T(8,128)S(1)} %get-tuple-element.19.notes_ref), channel_id=1, source_target_pairs={{0,1},{1,0},{2,3},{3,2},{4,5},{5,4},{6,7},{7,6},{8,9},{9,8},{10,11... | collective-permute-start | bytes 24584 | tf_op jit(solution)/shard_map/ppermute | solution.py:590

commit v5 on v4

--- a/solution.py
+++ b/solution.py
@@ -15,7 +15,7 @@
 SUB = 8
 LANES = 128
 EDGE = 3
-GROUP = 7
+GROUP = 14
 WHOLE_VMEM = 67043328
 
 
@@ -37,7 +37,11 @@
         self.pull = (2.0 * hopping * step_size * step_size) * cold
         self.slope = -((2.0 - 4.0 * quartic) * step_size * step_size) * cold
         self.speed = step_size * self.root
-        self.unspeed = 1.0 / self.speed
+        self.linear = ((1.0 - 2.0 * quartic) * cold) * self.back2
+        self.square = (quartic * cold) * (self.back2 * self.back2)
+        self.bond = ((2.0 * hopping) * cold) * self.back2
+        unspeed = 1.0 / self.speed
+        self.kinetic = 0.5 * (unspeed * unspeed)
 
     def half(self, near, value):
         return 0.5 * (self.pull * near + value * (self.slope - value * value))
@@ -46,10 +50,11 @@
         return value + ((value - before) + (self.pull * near + value * (self.slope - value * value)))
 
     def site(self, value, ahead):
-        squared = value * value * self.back2
-        return (-2.0 * hopping) * (self.back2 * (value * ahead)) + (
-            squared + quartic * (squared - 1.0) * (squared - 1.0)
-        )
+        squared = value * value
+        return squared * (self.linear + self.square * squared) - self.bond * (value * ahead)
+
+    def action(self, total, sites):
+        return jnp.sum(total) / self.cold + quartic * sites
 
 
 def chosen_scalars(labels_ref, betas_ref):
@@ -66,18 +71,27 @@
 
 
 def around(ref, row, tiles, lane):
-    values = [ref[t, pl.ds(row, SUB), :] for t in range(tiles)]
-    sums, right = beside(values, lane)
-    below = [ref[t, pl.ds(row + 1, SUB), :] for t in range(tiles)]
-    near = [(ref[t, pl.ds(row - 1, SUB), :] + below[t]) + sums[t] for t in range(tiles)]
-    return values, near, below, right
+    load = lambda t: ref[t % tiles, pl.ds(row, SUB), :]
+    ahead = pltpu.roll(load(tiles - 1), 1, 1)
+    value = load(0)
+    first_back = pltpu.roll(value, LANES - 1, 1)
+    back = first_back
+    for t in range(tiles):
+        following = load(t + 1)
+        behind, ahead = ahead, pltpu.roll(value, 1, 1)
+        back_next = first_back if t == tiles - 1 else pltpu.roll(following, LANES - 1, 1)
+        left = jnp.where(lane == 0, behind, ahead)
+        right = jnp.where(lane == LANES - 1, back_next, back)
+        below = ref[t, pl.ds(row + 1, SUB), :]
+        near = (ref[t, pl.ds(row - 1, SUB), :] + below) + (left + right)
+        yield t, value, near, below, right
+        value, back = following, back_next
 
 
 def advance(before, after, row, tiles, lane, scales, keep=None):
-    values, near, _, _ = around(before, row, tiles, lane)
-    for t in range(tiles):
+    for t, value, near, _, _ in around(before, row, tiles, lane):
         old = after[t, pl.ds(row, SUB), :]
-        new = scales.step(near[t], values[t], old)
+        new = scales.step(near, value, old)
         if keep is not None:
             new = jnp.where(keep, old, new)
         after[t, pl.ds(row, SUB), :] = new
@@ -167,14 +181,12 @@
     def begin(block, total):
         source = pl.multiple_of(block * SUB, SUB)
         row = pl.multiple_of(SUB + block * SUB, SUB)
-        values, near, below, right = around(first, row, tiles, lane)
-        for t in range(tiles):
+        for t, value, near, below, right in around(first, row, tiles, lane):
             push = scales.speed * momentum_ref[pl.ds(source, SUB), pl.ds(t * LANES, LANES)]
-            moment = scales.unspeed * push
-            action = scales.site(values[t], below[t] + right[t])
-            energy[t, pl.ds(source, SUB), :] = 0.5 * moment * moment + scales.cold * action
+            action = scales.site(value, below + right)
+            energy[t, pl.ds(source, SUB), :] = scales.kinetic * (push * push) + action
             total = total + action
-            second[t, pl.ds(row, SUB), :] = values[t] + (push + scales.half(near[t], values[t]))
+            second[t, pl.ds(row, SUB), :] = value + (push + scales.half(near, value))
         return total
 
     for k in range(8):
@@ -201,7 +213,10 @@
                 advance(before, after, row, tiles, lane, scales)
             return carry
 
-        lax.fori_loop(0, (blocks - 2) // group, turn, 0)
+        if group == blocks - 2:
+            turn(0, 0)
+        else:
+            lax.fori_loop(0, (blocks - 2) // group, turn, 0)
     last, previous = (first, second) if STEPS % 2 == 0 else (second, first)
     stores = []
     for n, buffer in enumerate((last, previous)):
@@ -249,16 +264,15 @@
         change, total = carry
         row = pl.multiple_of(SUB + block * SUB, SUB)
         source = pl.multiple_of(block * SUB, SUB)
-        values, near, below, right = around(last, row, tiles, lane)
-        for t in range(tiles):
-            gone = values[t] - previous[t, pl.ds(row, SUB), :]
-            moment = scales.unspeed * (gone + scales.half(near[t], values[t]))
-            action = scales.site(values[t], below[t] + right[t])
+        for t, value, near, below, right in around(last, row, tiles, lane):
+            gone = value - previous[t, pl.ds(row, SUB), :]
+            moment = gone + scales.half(near, value)
+            action = scales.site(value, below + right)
             total = total + action
             change = change + (
-                (0.5 * moment * moment + scales.cold * action) - energy[t, pl.ds(source, SUB), :]
+                (scales.kinetic * (moment * moment) + action) - energy[t, pl.ds(source, SUB), :]
             )
-            choose(block, values[t], t)
+            choose(block, value, t)
         return change, total
 
     sums = (zero, zero)
@@ -359,9 +373,9 @@
             else:
                 own_part = jnp.where(sub == 0, pltpu.roll(start_mine, 1, 0), 0.0)
                 halo_part = jnp.where(sub == SUB - 1, pltpu.roll(start_halo, SUB - 1, 0), 0.0)
-                missing = (-2.0 * hopping) * (scales.back2 * (start_mine * halo_part))
+                missing = -scales.bond * (start_mine * halo_part)
                 old_extra = old_extra + missing
-                energy_extra.append(scales.cold * missing)
+                energy_extra.append(missing)
             first[side, t, edge : edge + SUB, :] = start_halo
             second[side, t, edge : edge + SUB, :] = halo_ref[side, 1, t] + (
                 0.5 * scales.pull
@@ -385,21 +399,20 @@
         for b in range(2):
             place = b if side == 0 else EDGE - 2 + b
             row = own + place * SUB
-            values, near, below, right = around(last.at[side], row, tiles, lane)
             outermost = (side == 0 and b == 0) or (side == 1 and b == 1)
-            for t in range(tiles):
-                gone = values[t] - previous[side, t, pl.ds(row, SUB), :]
-                moment = scales.unspeed * (gone + scales.half(near[t], values[t]))
-                action = scales.site(values[t], below[t] + right[t])
+            for t, value, near, below, right in around(last.at[side], row, tiles, lane):
+                gone = value - previous[side, t, pl.ds(row, SUB), :]
+                moment = gone + scales.half(near, value)
+                action = scales.site(value, below + right)
                 total = total + action
                 old = energy_ref[side, t, b * SUB : (b + 1) * SUB, :]
                 if side == 1 and outermost:
                     old = old + energy_extra[t]
-                change = change + ((0.5 * moment * moment + scales.cold * action) - old)
+                change = change + ((scales.kinetic * (moment * moment) + action) - old)
                 if outermost:
                     cols = pl.ds(t * LANES, LANES)
                     kept = head_ref[:, cols] if side == 0 else tail_ref[:, cols]
-                    chosen_ref[side, :, cols] = jnp.where(accepted, scales.back * values[t], kept)
+                    chosen_ref[side, :, cols] = jnp.where(accepted, scales.back * value, kept)
         block = 0 if side == 0 else blocks - 1
         for n, (member, column) in enumerate(slots(block, tiles, per_member)):
             size = per_member * LANES
@@ -413,7 +426,8 @@
     for copy in copies:
         copy.start()
     old_action = sums_ref[2] + old_extra
-    action = jnp.sum(jnp.where(accepted, total, old_action))
+    sites = blocks * SUB * tiles * LANES
+    action = scales.action(jnp.where(accepted, total, old_action), sites)
     change = jnp.sum(change)
     note_ref[...] = jnp.where(
         lane == 0, label, jnp.where(lane == 1, action, jnp.where(lane == 2, change, 0.0))

time: 87.8 us -> 85.9 us (0.978)
  Pallas kernels: 20.9 us -> 19 us
    pallas_call x1, Pallas kernels: 11.9 us -> 10 us  [body(): pl.pallas_call(functools.partial(inner_kernel, per_member), out_shape=(ja...]
  transfers between devices with their start and end apart: 4 -> 4, of which waited for: 3 -> 3; matrix products, arithmetic and copies ran while one was open for 0% -> 0% of each run, Pallas kernels for 14% -> 13%
where the time goes in v5:
time: 85.9 us; the launch traced here: 85.5 us
  waiting for transfers between devices  50.1 us (58%)
  Pallas kernels  19 us (22%)
  starting transfers between devices  13.3 us (15%)
  between operations  2.01 us (2%)
  local copies, waits for them, and re-layouts  1.07 us (1%)
    all_to_all x1, waiting for transfers between devices, body(): lax.all_to_all(outgoing, 'rep', split_axis=0, concat_axis=0, tiled=True)  26.1 us
    all_to_all x1, waiting for transfers between devices, body(): lax.all_to_all(ordered, 'rep', split_axis=0, concat_axis=0, tiled=True)  21.4 us
    pallas_call x1, Pallas kernels, body(): pl.pallas_call(functools.partial(inner_kernel, per_member), out_shape=(ja...  10 us
    all_to_all x1, starting transfers between devices, body(): lax.all_to_all(outgoing, 'rep', split_axis=0, concat_axis=0, tiled=True)  6.97 us
    all_to_all x1, starting transfers between devices, body(): lax.all_to_all(ordered, 'rep', split_axis=0, concat_axis=0, tiled=True)  4.85 us
    pallas_call x1, Pallas kernels, body(): pl.pallas_call(functools.partial(outer_kernel, per_member, len(halos)), g...  4.58 us
    ppermute x1, waiting for transfers between devices, body(): passing = lax.ppermute(passing, 'dom', forward)  2.57 us
    pallas_call x1, Pallas kernels, body(): pl.pallas_call(pack_kernel, grid=(1,), out_shape=jax.ShapeDtypeStruct((2,...  1.87 us
  transfers between devices with their start and end apart: 4, of which 3 were waited for; matrix products, arithmetic and copies ran while one was open for 0% of the time, Pallas kernels for 13%

profile of v5, /device:TPU:9, one launch (start us, length us, event | category | flops | bytes accessed | tf_op | source)
XLA Modules:
  0.0 85.5 jit_solution(6397383108860889415)
XLA Ops:
  1.3 1.9 %pack.1 = f32[2,2,16,8,128]{4,3,2,1,0:T(8,128)} custom-call(s32[1]{0:T(128)S(6)} %copy.14.labels_ref, f32[16]{0:T(128)} %betas_ref.5, f32[128,2048]{1,0:T(8,128)} %bitcast.5, f32[128,2048]{1,0:T(8,128)} %bitcast.6, f32[128,2048]{1,0:T(8,128)} %bitcast.10, f32[128,2048]{1,0:T(8,128)} %bitcast.11), custom_call_target="tpu_custom_call" | custom-call | tf_op jit(solution)/shard_map/pack/pallas_call | solution.py:499
  3.2 1.2 %collective-permute-start = (f32[2,2,16,8,128]{4,3,2,1,0:T(8,128)}, f32[2,2,16,8,128]{4,3,2,1,0:T(8,128)}, u32[]{:S(2)}, u32[]{:S(2)}) collective-permute-start(f32[2,2,16,8,128]{4,3,2,1,0:T(8,128)} %pack.1), channel_id=1, source_target_pairs={{0,1},{1,0},{2,3},{3,2},{4,5},{5,4},{6,7},{7,6},{8,9},{9,8},{10,11... | collective-permute-start | bytes 786440 | tf_op jit(solution)/shard_map/ppermute | solution.py:516
  5.0 10.0 %inner.1 = (f32[16,8,2176]{2,1,0:T(8,128)}, f32[2,2,16,24,128]{4,3,2,1,0:T(8,128)}, f32[2,16,16,128]{3,2,1,0:T(8,128)}, f32[3,8,128]{2,1,0:T(8,128)}) custom-call(s32[1]{0:T(128)S(6)} %copy.14.labels_ref, f32[16]{0:T(128)} %betas_ref.5, s32[1]{0:T(128)S(6)} %copy.15.accept_ref, f32[128,2048]{1,0:T(8,128)} %bitcast.7, f32[128,2048]{1,0:T(8,128)} %bitcast.12), custom_call_target="tpu_custom_call" | custom-call | flops 26214400 | bytes 4194304 | tf_op jit(solution)/shard_map/inner/pallas_call | solution.py:526
  15.1 0.0 collective-permute-done.refs_0_
  15.1 4.6 %outer.1 = f32[16,8,2176]{2,1,0:T(8,128)} custom-call(s32[1]{0:T(128)S(6)} %copy.14.labels_ref, f32[16]{0:T(128)} %betas_ref.5, s32[1]{0:T(128)S(6)} %copy.15.accept_ref, s32[16]{0:T(128)} %swap_ref.1, f32[2,2,16,8,128]{4,3,2,1,0:T(8,128)} %collective-permute-done.refs_0_, ...), custom_call_target="tpu_custom_call", output_to_operand_aliasing={{}: (10, {})} | custom-call | tf_op jit(solution)/shard_map/outer/pallas_call | solution.py:555
  19.7 0.0 copy-start.1
  19.7 7.0 %all-to-all-start = ((f32[16,8,2176]{2,1,0:T(8,128)}), f32[16,8,2176]{2,1,0:T(8,128)S(1)}, u32[]{:S(2)}, u32[]{:S(2)}) async-start(f32[16,8,2176]{2,1,0:T(8,128)} %outer.1), calls=%async_computation | async-start | bytes 2228224 | tf_op jit(solution)/shard_map/all_to_all | solution.py:582
  26.7 0.0 copy-done.1
  26.7 0.1 slice_bitcast_fusion._
  26.8 0.0 copy-start
  26.8 26.1 %all-to-all-done.got_ref = f32[16,8,2176]{2,1,0:T(8,128)S(1)} async-done(((f32[16,8,2176]{2,1,0:T(8,128)}), f32[16,8,2176]{2,1,0:T(8,128)S(1)}, u32[]{:S(2)}, u32[]{:S(2)}) %all-to-all-start) | async-done | bytes 1114144 | tf_op jit(solution)/shard_map/all_to_all | solution.py:582
  52.9 1.8 %place.1 = (f32[16,8,2048]{2,1,0:T(8,128)}, f32[16,128]{1,0:T(8,128)S(1)}) custom-call(f32[16,8,2176]{2,1,0:T(8,128)S(1)} %all-to-all-done.got_ref, f32[1,128,2048]{2,1,0:T(8,128)S(1)} %slice_bitcast_fusion._), custom_call_target="tpu_custom_call" | custom-call | tf_op jit(solution)/shard_map/place/pallas_call | solution.py:584
  54.7 0.0 copy-done
  54.7 4.9 %all-to-all-start.1 = ((f32[16,8,2048]{2,1,0:T(8,128)}), f32[16,8,2048]{2,1,0:T(8,128)S(1)}, u32[]{:S(2)}, u32[]{:S(2)}) async-start(f32[16,8,2048]{2,1,0:T(8,128)} %get-tuple-element.18), calls=%async_computation.1 | async-start | bytes 2097152 | tf_op jit(solution)/shard_map/all_to_all | solution.py:600
  59.6 0.2 collective-permute-start.1
  59.8 2.6 %collective-permute-done.1 = f32[16,128]{1,0:T(8,128)S(1)} collective-permute-done((f32[16,128]{1,0:T(8,128)S(1)}, f32[16,128]{1,0:T(8,128)S(1)}, u32[]{:S(2)}, u32[]{:S(2)}) %collective-permute-start.1) | collective-permute-done | bytes 8224 | tf_op jit(solution)/shard_map/ppermute | solution.py:604
  62.4 0.7 ladder.1
  63.1 21.4 %all-to-all-done.1 = f32[16,8,2048]{2,1,0:T(8,128)S(1)} async-done(((f32[16,8,2048]{2,1,0:T(8,128)}), f32[16,8,2048]{2,1,0:T(8,128)S(1)}, u32[]{:S(2)}, u32[]{:S(2)}) %all-to-all-start.1) | async-done | bytes 1048608 | tf_op jit(solution)/shard_map/all_to_all | solution.py:600
  84.5 1.0 %copy.16 = f32[1,128,2048]{2,1,0:T(8,128)} copy(f32[1,128,2048]{2,1,0:T(8,128)S(1)} %bitcast.13) | data formatting | bytes 2097152
  (1 shorter events, 0.0 us)
Async XLA Ops:
  3.2 11.9 %collective-permute-start = (f32[2,2,16,8,128]{4,3,2,1,0:T(8,128)}, f32[2,2,16,8,128]{4,3,2,1,0:T(8,128)}, u32[]{:S(2)}, u32[]{:S(2)}) collective-permute-start(f32[2,2,16,8,128]{4,3,2,1,0:T(8,128)} %pack.1), channel_id=1, source_target_pairs={{0,1},{1,0},{2,3},{3,2},{4,5},{5,4},{6,7},{7,6},{8,9},{9,8},{10,11... | collective-permute-start | bytes 786440 | tf_op jit(solution)/shard_map/ppermute | solution.py:516
  19.7 7.0 %copy-start.1 = (f32[16,8,2176]{2,1,0:T(8,128)S(1)}, f32[16,8,2176]{2,1,0:T(8,128)}, u32[]{:S(2)}) copy-start(f32[16,8,2176]{2,1,0:T(8,128)} %outer.1) | copy-start | bytes 3342340
  19.7 33.2 %all-to-all-start = ((f32[16,8,2176]{2,1,0:T(8,128)}), f32[16,8,2176]{2,1,0:T(8,128)S(1)}, u32[]{:S(2)}, u32[]{:S(2)}) async-start(f32[16,8,2176]{2,1,0:T(8,128)} %outer.1), calls=%async_computation | async-start | bytes 2228224 | tf_op jit(solution)/shard_map/all_to_all | solution.py:582
  26.8 27.9 %copy-start = (f32[1,128,2048]{2,1,0:T(8,128)}, f32[1,128,2048]{2,1,0:T(8,128)S(1)}, u32[]{:S(2)}) copy-start(f32[1,128,2048]{2,1,0:T(8,128)S(1)} %slice_bitcast_fusion._) | copy-start | bytes 3145732
  54.7 29.8 %all-to-all-start.1 = ((f32[16,8,2048]{2,1,0:T(8,128)}), f32[16,8,2048]{2,1,0:T(8,128)S(1)}, u32[]{:S(2)}, u32[]{:S(2)}) async-start(f32[16,8,2048]{2,1,0:T(8,128)} %get-tuple-element.18), calls=%async_computation.1 | async-start | bytes 2097152 | tf_op jit(solution)/shard_map/all_to_all | solution.py:600
  59.6 2.8 %collective-permute-start.1 = (f32[16,128]{1,0:T(8,128)S(1)}, f32[16,128]{1,0:T(8,128)S(1)}, u32[]{:S(2)}, u32[]{:S(2)}) collective-permute-start(f32[16,128]{1,0:T(8,128)S(1)} %get-tuple-element.19.notes_ref), channel_id=1, source_target_pairs={{0,1},{1,0},{2,3},{3,2},{4,5},{5,4},{6,7},{7,6},{8,9},{9,8},{10,11... | collective-permute-start | bytes 24584 | tf_op jit(solution)/shard_map/ppermute | solution.py:604

commit v6 on v5

--- a/solution.py
+++ b/solution.py
@@ -57,8 +57,11 @@
         return jnp.sum(total) / self.cold + quartic * sites
 
 
-def chosen_scalars(labels_ref, betas_ref):
-    return betas_ref[labels_ref[0]]
+def fetch(copies):
+    started = [pltpu.make_async_copy(*copy) for copy in copies]
+    for copy in started:
+        copy.start()
+    return started
 
 
 def beside(values, lane):
@@ -97,12 +100,30 @@
         after[t, pl.ds(row, SUB), :] = new
 
 
-def pack_kernel(labels_ref, betas_ref, head_ref, tail_ref, head_m_ref, tail_m_ref, out_ref):
-    scales = Scales(chosen_scalars(labels_ref, betas_ref))
+def pack_kernel(
+    betas_ref, labels_hbm, field_hbm, momentum_hbm, out_ref, labels_ref, field_ref, moment_ref, sem
+):
+    rows = field_hbm.shape[0]
+    loads = fetch(
+        [(labels_hbm, labels_ref, sem.at[0])]
+        + [
+            (field_hbm.at[pl.ds(start, 2 * SUB), :], field_ref.at[side], sem.at[1 + side])
+            for side, start in enumerate((0, rows - 2 * SUB))
+        ]
+        + [
+            (momentum_hbm.at[pl.ds(start, SUB), :], moment_ref.at[side], sem.at[3 + side])
+            for side, start in enumerate((0, rows - SUB))
+        ]
+    )
+    for load in loads:
+        load.wait()
+    scales = Scales(betas_ref[labels_ref[0]])
     lane = lane_index()
     row = row_index()
-    tiles = head_ref.shape[1] // LANES
-    for side, ref, m_ref in ((0, head_ref, head_m_ref), (1, tail_ref, tail_m_ref)):
+    tiles = field_ref.shape[2] // LANES
+    for side in range(2):
+        ref = field_ref.at[side]
+        m_ref = moment_ref.at[side]
         base = 0 if side == 0 else SUB
         inner = SUB - base
         values = [scales.root * ref[base : base + SUB, pl.ds(i * LANES, LANES)] for i in range(tiles)]
@@ -130,15 +151,17 @@
 
 def inner_kernel(
     per_member,
-    labels_ref,
     betas_ref,
-    accept_ref,
+    labels_hbm,
+    accept_hbm,
     field_hbm,
     momentum_hbm,
     send_hbm,
     state_hbm,
     energy_hbm,
     sums_ref,
+    labels_ref,
+    accept_ref,
     field_ref,
     momentum_ref,
     chosen_ref,
@@ -148,19 +171,27 @@
     in_sem,
     send_sem,
     state_sem,
+    scalar_sem,
 ):
     rows, width = field_ref.shape
     tiles = width // LANES
     blocks = rows // SUB
     chunk = rows // 8
-    loads = []
-    for a, (source, target) in enumerate(((field_hbm, field_ref), (momentum_hbm, momentum_ref))):
-        for k in range(8):
-            part = pl.ds(k * chunk, chunk)
-            copy = pltpu.make_async_copy(source.at[part, :], target.at[part, :], in_sem.at[a, k])
-            copy.start()
-            loads.append(copy)
-    scales = Scales(chosen_scalars(labels_ref, betas_ref))
+    scalars = fetch(
+        [(labels_hbm, labels_ref, scalar_sem.at[0]), (accept_hbm, accept_ref, scalar_sem.at[1])]
+    )
+
+    def load(a, k):
+        source, target = ((field_hbm, field_ref), (momentum_hbm, momentum_ref))[a]
+        part = pl.ds(pl.multiple_of(k * chunk, chunk), chunk)
+        return pltpu.make_async_copy(source.at[part, :], target.at[part, :], in_sem.at[a, k])
+
+    for k in range(8):
+        load(0, k).start()
+        load(1, k).start()
+    for copy in scalars:
+        copy.wait()
+    scales = Scales(betas_ref[labels_ref[0]])
     accepted = accept_ref[0] == 1
     lane = lane_index()
     sub = row_index()
@@ -169,13 +200,14 @@
         for t in range(tiles):
             ref[t, 0:SUB, :] = zero
             ref[t, SUB + rows : 2 * SUB + rows, :] = zero
-    for k in range(8):
-        loads[k].wait()
+
+    def bring(k):
+        load(0, k).wait()
         for b in range(chunk // SUB):
-            row = k * chunk + b * SUB
+            row = pl.multiple_of(k * chunk + b * SUB, SUB)
             for t in range(tiles):
-                first[t, SUB + row : 2 * SUB + row, :] = (
-                    scales.root * field_ref[row : row + SUB, pl.ds(t * LANES, LANES)]
+                first[t, pl.ds(pl.multiple_of(SUB + row, SUB), SUB), :] = (
+                    scales.root * field_ref[pl.ds(row, SUB), pl.ds(t * LANES, LANES)]
                 )
 
     def begin(block, total):
@@ -189,17 +221,20 @@
             second[t, pl.ds(row, SUB), :] = value + (push + scales.half(near, value))
         return total
 
-    for k in range(8):
-        loads[8 + k].wait()
-
     per_turn = 2
 
-    def begin_turn(i, total):
-        for b in range(per_turn):
-            total = begin(i * per_turn + b, total)
+    def open_chunk(k, total):
+        load(1, k).wait()
+        for b in range(chunk // SUB):
+            total = begin(k * (chunk // SUB) + b, total)
         return total
 
-    old_action = lax.fori_loop(0, blocks // per_turn, begin_turn, zero)
+    def open_turn(k, total):
+        bring(k + 1)
+        return open_chunk(k, total)
+
+    bring(0)
+    old_action = open_chunk(7, lax.fori_loop(0, 7, open_turn, zero))
 
     group = GROUP if (blocks - 2) % GROUP == 0 else 1
     for time in range(1, STEPS):
@@ -306,10 +341,10 @@
 def outer_kernel(
     per_member,
     halos,
-    labels_ref,
     betas_ref,
-    accept_ref,
     swap_ref,
+    labels_hbm,
+    accept_hbm,
     *refs,
 ):
     halo_refs = refs[:halos]
@@ -321,6 +356,8 @@
         tail_ref,
         _,
         send_hbm,
+        labels_ref,
+        accept_ref,
         first,
         second,
         energy_ref,
@@ -330,7 +367,11 @@
         in_sem,
         send_sem,
         note_sem,
+        scalar_sem,
     ) = refs[halos:]
+    scalars = fetch(
+        [(labels_hbm, labels_ref, scalar_sem.at[0]), (accept_hbm, accept_ref, scalar_sem.at[1])]
+    )
     last, previous = (first, second) if STEPS % 2 == 0 else (second, first)
     loads = []
     for side in range(2):
@@ -341,11 +382,10 @@
         ]
         parts.append((halo_refs[side % halos].at[1 - side], halo_ref.at[side]))
         parts.append((energy_hbm.at[side], energy_ref.at[side]))
-        for n, (source, target) in enumerate(parts):
-            copy = pltpu.make_async_copy(source, target, in_sem.at[side, n])
-            copy.start()
-            loads.append(copy)
-    scales = Scales(chosen_scalars(labels_ref, betas_ref))
+        loads.append(fetch([part + (in_sem.at[side, n],) for n, part in enumerate(parts)]))
+    for copy in scalars:
+        copy.wait()
+    scales = Scales(betas_ref[labels_ref[0]])
     label = swap_ref[labels_ref[0]].astype(jnp.float32)
     accepted = accept_ref[0] == 1
     lane = lane_index()
@@ -356,9 +396,9 @@
     zero = jnp.zeros((SUB, LANES), jnp.float32)
     old_extra = zero
     energy_extra = []
-    for copy in loads:
-        copy.wait()
     for side in range(2):
+        for copy in loads[side][:3]:
+            copy.wait()
         edge = SUB if side == 0 else EDGE * SUB
         pad = 0 if side == 0 else (EDGE + 1) * SUB
         mine = 2 * SUB if side == 0 else (EDGE - 1) * SUB
@@ -395,6 +435,7 @@
     total = sums_ref[1]
     copies = []
     for side in range(2):
+        loads[side][3].wait()
         own = 2 * SUB if side == 0 else 0
         for b in range(2):
             place = b if side == 0 else EDGE - 2 + b
@@ -494,23 +535,21 @@
     anywhere = pl.BlockSpec(memory_space=pl.ANY)
     inhbm = pl.BlockSpec(memory_space=pltpu.HBM)
     dma = pltpu.SemaphoreType.DMA
-    last16 = rows // (2 * SUB) - 1
     last8 = rows // SUB - 1
+    scalar = pltpu.SMEM((1,), jnp.int32)
     edges = pl.pallas_call(
         pack_kernel,
-        grid=(1,),
         out_shape=jax.ShapeDtypeStruct((2, 2, tiles, SUB, LANES), f32),
-        in_specs=[
-            smem,
-            smem,
-            pl.BlockSpec((2 * SUB, width), lambda i: (0, 0)),
-            pl.BlockSpec((2 * SUB, width), lambda i: (last16, 0)),
-            pl.BlockSpec((SUB, width), lambda i: (0, 0)),
-            pl.BlockSpec((SUB, width), lambda i: (last8, 0)),
+        in_specs=[smem, inhbm, inhbm, inhbm],
+        out_specs=vmem,
+        scratch_shapes=[
+            scalar,
+            pltpu.VMEM((2, 2 * SUB, width), f32),
+            pltpu.VMEM((2, SUB, width), f32),
+            dma((5,)),
         ],
-        out_specs=pl.BlockSpec((2, 2, tiles, SUB, LANES), lambda i: (0, 0, 0, 0, 0)),
         name="pack",
-    )(labels, betas, start, start, moment, moment)
+    )(betas, labels, start, moment)
     forward = [(i, (i + 1) % strips) for i in range(strips)]
     backward = [((i + 1) % strips, i) for i in range(strips)]
     halos = (lax.ppermute(edges, "dom", forward),)
@@ -531,9 +570,11 @@
             jax.ShapeDtypeStruct((2, tiles, 2 * SUB, LANES), f32),
             jax.ShapeDtypeStruct((3, SUB, LANES), f32),
         ),
-        in_specs=[smem, smem, smem, inhbm, inhbm],
+        in_specs=[smem, inhbm, inhbm, inhbm, inhbm],
         out_specs=(inhbm, inhbm, inhbm, vmem),
         scratch_shapes=[
+            scalar,
+            scalar,
             strip,
             strip,
             strip,
@@ -543,20 +584,21 @@
             dma((2, 8)),
             dma((members,)),
             dma((2, 3)),
+            dma((2,)),
         ],
         cost_estimate=pl.CostEstimate(
             flops=100 * rows * width, bytes_accessed=16 * rows * width, transcendentals=0
         ),
         compiler_params=pltpu.CompilerParams(vmem_limit_bytes=WHOLE_VMEM),
         name="inner",
-    )(labels, betas, accept, start, moment)
+    )(betas, labels, accept, start, moment)
     window = pltpu.VMEM((2, tiles, (EDGE + 2) * SUB, LANES), f32)
     count = 4 + len(halos)
     outgoing = pl.pallas_call(
         functools.partial(outer_kernel, per_member, len(halos)),
         grid=(1,),
         out_shape=jax.ShapeDtypeStruct((members, SUB, piece + LANES), f32),
-        in_specs=[smem] * 4
+        in_specs=[smem, smem, inhbm, inhbm]
         + [anywhere] * len(halos)
         + [inhbm, inhbm, vmem]
         + [
@@ -566,6 +608,8 @@
         ],
         out_specs=inhbm,
         scratch_shapes=[
+            scalar,
+            scalar,
             window,
             window,
             pltpu.VMEM((2, tiles, 2 * SUB, LANES), f32),
@@ -575,10 +619,11 @@
             dma((2, 4)),
             dma((2, shares)),
             dma((members,)),
+            dma((2,)),
         ],
         input_output_aliases={count + 5: 0},
         name="outer",
-    )(labels, betas, accept, swap_pairs, *halos, state, energy, sums, start, start, outgoing)
+    )(betas, swap_pairs, labels, accept, *halos, state, energy, sums, start, start, outgoing)
     received = lax.all_to_all(outgoing, "rep", split_axis=0, concat_axis=0, tiled=True)
     out = strip_of(outgoing[:, :, :piece])
     ordered, notes = pl.pallas_call(

time: 85.9 us -> 86.3 us (level)
  transfers between devices with their start and end apart: 4 -> 4, of which waited for: 3 -> 3; matrix products, arithmetic and copies ran while one was open for 0% -> 0% of each run, Pallas kernels for 13% -> 12%
where the time goes in v6:
time: 86.3 us; the launch traced here: 85.8 us
  waiting for transfers between devices  50.1 us (58%)
  Pallas kernels  19.3 us (22%)
  starting transfers between devices  13.4 us (16%)
  between operations  2.02 us (2%)
  local copies, waits for them, and re-layouts  1.07 us (1%)
    all_to_all x1, waiting for transfers between devices, body(): lax.all_to_all(outgoing, 'rep', split_axis=0, concat_axis=0, tiled=True)  26.1 us
    all_to_all x1, waiting for transfers between devices, body(): lax.all_to_all(ordered, 'rep', split_axis=0, concat_axis=0, tiled=True)  21.4 us
    pallas_call x1, Pallas kernels, body(): pl.pallas_call(functools.partial(inner_kernel, per_member), out_shape=(ja...  9.6 us
    all_to_all x1, starting transfers between devices, body(): lax.all_to_all(outgoing, 'rep', split_axis=0, concat_axis=0, tiled=True)  6.97 us
    all_to_all x1, starting transfers between devices, body(): lax.all_to_all(ordered, 'rep', split_axis=0, concat_axis=0, tiled=True)  4.85 us
    pallas_call x1, Pallas kernels, body(): pl.pallas_call(functools.partial(outer_kernel, per_member, len(halos)), g...  4.63 us
    ppermute x1, waiting for transfers between devices, body(): passing = lax.ppermute(passing, 'dom', forward)  2.57 us
    pallas_call x1, Pallas kernels, body(): pl.pallas_call(pack_kernel, out_shape=jax.ShapeDtypeStruct((2, 2, tiles,...  2.57 us
  transfers between devices with their start and end apart: 4, of which 3 were waited for; matrix products, arithmetic and copies ran while one was open for 0% of the time, Pallas kernels for 12%

profile of v6, /device:TPU:9, one launch (start us, length us, event | category | flops | bytes accessed | tf_op | source)
XLA Modules:
  0.0 85.8 jit_solution(1050025563714527054)
XLA Ops:
  1.3 2.6 %pack.1 = f32[2,2,16,8,128]{4,3,2,1,0:T(8,128)} custom-call(f32[16]{0:T(128)} %betas_ref.5, s32[1]{0:T(128)S(6)} %copy.14.labels_hbm, f32[128,2048]{1,0:T(8,128)} %bitcast.5, f32[128,2048]{1,0:T(8,128)} %bitcast.9), custom_call_target="tpu_custom_call" | custom-call | tf_op jit(solution)/shard_map/pack/pallas_call | solution.py:540
  3.9 1.3 %collective-permute-start = (f32[2,2,16,8,128]{4,3,2,1,0:T(8,128)}, f32[2,2,16,8,128]{4,3,2,1,0:T(8,128)}, u32[]{:S(2)}, u32[]{:S(2)}) collective-permute-start(f32[2,2,16,8,128]{4,3,2,1,0:T(8,128)} %pack.1), channel_id=1, source_target_pairs={{0,1},{1,0},{2,3},{3,2},{4,5},{5,4},{6,7},{7,6},{8,9},{9,8},{10,11... | collective-permute-start | bytes 786440 | tf_op jit(solution)/shard_map/ppermute | solution.py:555
  5.8 9.6 %inner.1 = (f32[16,8,2176]{2,1,0:T(8,128)}, f32[2,2,16,24,128]{4,3,2,1,0:T(8,128)}, f32[2,16,16,128]{3,2,1,0:T(8,128)}, f32[3,8,128]{2,1,0:T(8,128)}) custom-call(f32[16]{0:T(128)} %betas_ref.5, s32[1]{0:T(128)S(6)} %copy.14.labels_hbm, s32[1]{0:T(128)S(6)} %copy.15.accept_hbm, f32[128,2048]{1,0:T(8,128)} %bitcast.6, f32[128,2048]{1,0:T(8,128)} %bitcast.10), custom_call_target="tpu_custom_call" | custom-call | flops 26214400 | bytes 4194304 | tf_op jit(solution)/shard_map/inner/pallas_call | solution.py:565
  15.4 0.0 collective-permute-done.refs_0_
  15.4 4.6 %outer.1 = f32[16,8,2176]{2,1,0:T(8,128)} custom-call(f32[16]{0:T(128)} %betas_ref.5, s32[16]{0:T(128)} %swap_ref.1, s32[1]{0:T(128)S(6)} %copy.14.labels_hbm, s32[1]{0:T(128)S(6)} %copy.15.accept_hbm, f32[2,2,16,8,128]{4,3,2,1,0:T(8,128)} %collective-permute-done.refs_0_, ...), custom_call_target="tpu_custom_call", output_to_operand_aliasing={{}: (10, {})} | custom-call | tf_op jit(solution)/shard_map/outer/pallas_call | solution.py:597
  20.1 0.0 copy-start.1
  20.1 7.0 %all-to-all-start = ((f32[16,8,2176]{2,1,0:T(8,128)}), f32[16,8,2176]{2,1,0:T(8,128)S(1)}, u32[]{:S(2)}, u32[]{:S(2)}) async-start(f32[16,8,2176]{2,1,0:T(8,128)} %outer.1), calls=%async_computation | async-start | bytes 2228224 | tf_op jit(solution)/shard_map/all_to_all | solution.py:627
  27.0 0.0 copy-done.1
  27.1 0.1 slice_bitcast_fusion._
  27.2 0.0 copy-start
  27.2 26.1 %all-to-all-done.got_ref = f32[16,8,2176]{2,1,0:T(8,128)S(1)} async-done(((f32[16,8,2176]{2,1,0:T(8,128)}), f32[16,8,2176]{2,1,0:T(8,128)S(1)}, u32[]{:S(2)}, u32[]{:S(2)}) %all-to-all-start) | async-done | bytes 1114144 | tf_op jit(solution)/shard_map/all_to_all | solution.py:627
  53.3 1.8 %place.1 = (f32[16,8,2048]{2,1,0:T(8,128)}, f32[16,128]{1,0:T(8,128)S(1)}) custom-call(f32[16,8,2176]{2,1,0:T(8,128)S(1)} %all-to-all-done.got_ref, f32[1,128,2048]{2,1,0:T(8,128)S(1)} %slice_bitcast_fusion._), custom_call_target="tpu_custom_call" | custom-call | tf_op jit(solution)/shard_map/place/pallas_call | solution.py:629
  55.1 0.0 copy-done
  55.1 4.9 %all-to-all-start.1 = ((f32[16,8,2048]{2,1,0:T(8,128)}), f32[16,8,2048]{2,1,0:T(8,128)S(1)}, u32[]{:S(2)}, u32[]{:S(2)}) async-start(f32[16,8,2048]{2,1,0:T(8,128)} %get-tuple-element.18), calls=%async_computation.1 | async-start | bytes 2097152 | tf_op jit(solution)/shard_map/all_to_all | solution.py:645
  59.9 0.2 collective-permute-start.1
  60.2 2.6 %collective-permute-done.1 = f32[16,128]{1,0:T(8,128)S(1)} collective-permute-done((f32[16,128]{1,0:T(8,128)S(1)}, f32[16,128]{1,0:T(8,128)S(1)}, u32[]{:S(2)}, u32[]{:S(2)}) %collective-permute-start.1) | collective-permute-done | bytes 8224 | tf_op jit(solution)/shard_map/ppermute | solution.py:649
  62.7 0.7 ladder.1
  63.5 21.4 %all-to-all-done.1 = f32[16,8,2048]{2,1,0:T(8,128)S(1)} async-done(((f32[16,8,2048]{2,1,0:T(8,128)}), f32[16,8,2048]{2,1,0:T(8,128)S(1)}, u32[]{:S(2)}, u32[]{:S(2)}) %all-to-all-start.1) | async-done | bytes 1048608 | tf_op jit(solution)/shard_map/all_to_all | solution.py:645
  84.9 1.0 %copy.16 = f32[1,128,2048]{2,1,0:T(8,128)} copy(f32[1,128,2048]{2,1,0:T(8,128)S(1)} %bitcast.11) | data formatting | bytes 2097152
  (1 shorter events, 0.0 us)
Async XLA Ops:
  3.9 11.6 %collective-permute-start = (f32[2,2,16,8,128]{4,3,2,1,0:T(8,128)}, f32[2,2,16,8,128]{4,3,2,1,0:T(8,128)}, u32[]{:S(2)}, u32[]{:S(2)}) collective-permute-start(f32[2,2,16,8,128]{4,3,2,1,0:T(8,128)} %pack.1), channel_id=1, source_target_pairs={{0,1},{1,0},{2,3},{3,2},{4,5},{5,4},{6,7},{7,6},{8,9},{9,8},{10,11... | collective-permute-start | bytes 786440 | tf_op jit(solution)/shard_map/ppermute | solution.py:555
  20.1 7.0 %copy-start.1 = (f32[16,8,2176]{2,1,0:T(8,128)S(1)}, f32[16,8,2176]{2,1,0:T(8,128)}, u32[]{:S(2)}) copy-start(f32[16,8,2176]{2,1,0:T(8,128)} %outer.1) | copy-start | bytes 3342340
  20.1 33.2 %all-to-all-start = ((f32[16,8,2176]{2,1,0:T(8,128)}), f32[16,8,2176]{2,1,0:T(8,128)S(1)}, u32[]{:S(2)}, u32[]{:S(2)}) async-start(f32[16,8,2176]{2,1,0:T(8,128)} %outer.1), calls=%async_computation | async-start | bytes 2228224 | tf_op jit(solution)/shard_map/all_to_all | solution.py:627
  27.2 27.9 %copy-start = (f32[1,128,2048]{2,1,0:T(8,128)}, f32[1,128,2048]{2,1,0:T(8,128)S(1)}, u32[]{:S(2)}) copy-start(f32[1,128,2048]{2,1,0:T(8,128)S(1)} %slice_bitcast_fusion._) | copy-start | bytes 3145732
  55.1 29.8 %all-to-all-start.1 = ((f32[16,8,2048]{2,1,0:T(8,128)}), f32[16,8,2048]{2,1,0:T(8,128)S(1)}, u32[]{:S(2)}, u32[]{:S(2)}) async-start(f32[16,8,2048]{2,1,0:T(8,128)} %get-tuple-element.18), calls=%async_computation.1 | async-start | bytes 2097152 | tf_op jit(solution)/shard_map/all_to_all | solution.py:645
  59.9 2.8 %collective-permute-start.1 = (f32[16,128]{1,0:T(8,128)S(1)}, f32[16,128]{1,0:T(8,128)S(1)}, u32[]{:S(2)}, u32[]{:S(2)}) collective-permute-start(f32[16,128]{1,0:T(8,128)S(1)} %get-tuple-element.19.notes_ref), channel_id=1, source_target_pairs={{0,1},{1,0},{2,3},{3,2},{4,5},{5,4},{6,7},{7,6},{8,9},{9,8},{10,11... | collective-permute-start | bytes 24584 | tf_op jit(solution)/shard_map/ppermute | solution.py:649

commit v7 on v5

--- a/solution.py
+++ b/solution.py
@@ -61,31 +61,58 @@
     return betas_ref[labels_ref[0]]
 
 
-def beside(values, lane):
-    count = len(values)
-    ahead = [pltpu.roll(v, 1, 1) for v in values]
-    back = [pltpu.roll(v, LANES - 1, 1) for v in values]
-    left = [jnp.where(lane == 0, ahead[i - 1], ahead[i]) for i in range(count)]
-    right = [jnp.where(lane == LANES - 1, back[(i + 1) % count], back[i]) for i in range(count)]
-    return [a + b for a, b in zip(left, right)], right
+def paired(values, lane):
+    half = len(values) // 2
+    even = (lane & 1) == 0
+    evens = [
+        jnp.where(even, values[u], pltpu.roll(values[u + half], 1, 1)) for u in range(half)
+    ]
+    odds = [
+        jnp.where(even, pltpu.roll(values[u], LANES - 1, 1), values[u + half]) for u in range(half)
+    ]
+    return evens + odds
+
+
+def unpaired(evens, odds, lane):
+    even = (lane & 1) == 0
+    return (
+        jnp.where(even, evens, pltpu.roll(odds, 1, 1)),
+        jnp.where(even, pltpu.roll(evens, LANES - 1, 1), odds),
+    )
+
+
+def beside(load, tiles, lane):
+    half = tiles // 2
+    final = load(tiles - 1)
+    behind = jnp.where(lane == 0, pltpu.roll(final, 1, 1), pltpu.roll(final, 3, 1))
+    evens = load(0)
+    begin = evens
+    ahead = pltpu.roll(evens, LANES - 2, 1)
+    for u in range(half):
+        odds = load(u + half)
+        forward = pltpu.roll(odds, 2, 1)
+        left = jnp.where(lane < 2, behind, forward)
+        if u + 1 < half:
+            following = load(u + 1)
+            ahead_next = pltpu.roll(following, LANES - 2, 1)
+        else:
+            following = begin
+            ahead_next = jnp.where(
+                lane == LANES - 1, pltpu.roll(begin, LANES - 1, 1), pltpu.roll(begin, LANES - 3, 1)
+            )
+        right = jnp.where(lane >= LANES - 2, ahead_next, ahead)
+        yield u, evens, odds, left, right
+        behind, evens, ahead = forward, following, ahead_next
 
 
 def around(ref, row, tiles, lane):
-    load = lambda t: ref[t % tiles, pl.ds(row, SUB), :]
-    ahead = pltpu.roll(load(tiles - 1), 1, 1)
-    value = load(0)
-    first_back = pltpu.roll(value, LANES - 1, 1)
-    back = first_back
-    for t in range(tiles):
-        following = load(t + 1)
-        behind, ahead = ahead, pltpu.roll(value, 1, 1)
-        back_next = first_back if t == tiles - 1 else pltpu.roll(following, LANES - 1, 1)
-        left = jnp.where(lane == 0, behind, ahead)
-        right = jnp.where(lane == LANES - 1, back_next, back)
-        below = ref[t, pl.ds(row + 1, SUB), :]
-        near = (ref[t, pl.ds(row - 1, SUB), :] + below) + (left + right)
-        yield t, value, near, below, right
-        value, back = following, back_next
+    half = tiles // 2
+    load = lambda t: ref[t, pl.ds(row, SUB), :]
+    for u, evens, odds, left, right in beside(load, tiles, lane):
+        for t, value, before, after in ((u, evens, left, odds), (u + half, odds, evens, right)):
+            below = ref[t, pl.ds(row + 1, SUB), :]
+            near = (ref[t, pl.ds(row - 1, SUB), :] + below) + (before + after)
+            yield t, value, near, below, after
 
 
 def advance(before, after, row, tiles, lane, scales, keep=None):
@@ -105,22 +132,35 @@
     for side, ref, m_ref in ((0, head_ref, head_m_ref), (1, tail_ref, tail_m_ref)):
         base = 0 if side == 0 else SUB
         inner = SUB - base
-        values = [scales.root * ref[base : base + SUB, pl.ds(i * LANES, LANES)] for i in range(tiles)]
-        sums, _ = beside(values, lane)
-        for i in range(tiles):
-            cols = pl.ds(i * LANES, LANES)
-            other = scales.root * ref[inner : inner + SUB, cols]
-            up = pltpu.roll(values[i], 1, 0)
-            down = pltpu.roll(values[i], SUB - 1, 0)
-            if side == 0:
-                up = jnp.where(row == 0, 0.0, up)
-                down = jnp.where(row == SUB - 1, pltpu.roll(other, SUB - 1, 0), down)
-            else:
-                up = jnp.where(row == 0, pltpu.roll(other, 1, 0), up)
-                down = jnp.where(row == SUB - 1, 0.0, down)
-            push = scales.speed * m_ref[:, cols] + scales.half((up + down) + sums[i], values[i])
-            out_ref[side, 0, i] = values[i]
-            out_ref[side, 1, i] = values[i] + push
+        parts = []
+        for start in (base, inner):
+            parts.append(
+                paired(
+                    [
+                        scales.root * ref[start : start + SUB, pl.ds(t * LANES, LANES)]
+                        for t in range(tiles)
+                    ],
+                    lane,
+                )
+            )
+        values, others = parts
+        pushes = paired(
+            [scales.speed * m_ref[:, pl.ds(t * LANES, LANES)] for t in range(tiles)], lane
+        )
+        for u, evens, odds, left, right in beside(lambda t: values[t], tiles, lane):
+            half = tiles // 2
+            for t, value, near in ((u, evens, left + odds), (u + half, odds, evens + right)):
+                up = pltpu.roll(value, 1, 0)
+                down = pltpu.roll(value, SUB - 1, 0)
+                if side == 0:
+                    up = jnp.where(row == 0, 0.0, up)
+                    down = jnp.where(row == SUB - 1, pltpu.roll(others[t], SUB - 1, 0), down)
+                else:
+                    up = jnp.where(row == 0, pltpu.roll(others[t], 1, 0), up)
+                    down = jnp.where(row == SUB - 1, 0.0, down)
+                push = pushes[t] + scales.half((up + down) + near, value)
+                out_ref[side, 0, t] = value
+                out_ref[side, 1, t] = value + push
 
 
 def slots(row_block, tiles, per_member):
@@ -153,13 +193,15 @@
     tiles = width // LANES
     blocks = rows // SUB
     chunk = rows // 8
-    loads = []
-    for a, (source, target) in enumerate(((field_hbm, field_ref), (momentum_hbm, momentum_ref))):
-        for k in range(8):
-            part = pl.ds(k * chunk, chunk)
-            copy = pltpu.make_async_copy(source.at[part, :], target.at[part, :], in_sem.at[a, k])
-            copy.start()
-            loads.append(copy)
+
+    def load(a, k):
+        source, target = ((field_hbm, field_ref), (momentum_hbm, momentum_ref))[a]
+        part = pl.ds(pl.multiple_of(k * chunk, chunk), chunk)
+        return pltpu.make_async_copy(source.at[part, :], target.at[part, :], in_sem.at[a, k])
+
+    for k in range(8):
+        load(0, k).start()
+        load(1, k).start()
     scales = Scales(chosen_scalars(labels_ref, betas_ref))
     accepted = accept_ref[0] == 1
     lane = lane_index()
@@ -169,37 +211,49 @@
         for t in range(tiles):
             ref[t, 0:SUB, :] = zero
             ref[t, SUB + rows : 2 * SUB + rows, :] = zero
-    for k in range(8):
-        loads[k].wait()
+
+    def bring(k):
+        load(0, k).wait()
         for b in range(chunk // SUB):
-            row = k * chunk + b * SUB
-            for t in range(tiles):
-                first[t, SUB + row : 2 * SUB + row, :] = (
-                    scales.root * field_ref[row : row + SUB, pl.ds(t * LANES, LANES)]
-                )
+            row = pl.multiple_of(k * chunk + b * SUB, SUB)
+            values = [
+                scales.root * field_ref[pl.ds(row, SUB), pl.ds(t * LANES, LANES)] for t in range(tiles)
+            ]
+            for t, value in enumerate(paired(values, lane)):
+                first[t, pl.ds(pl.multiple_of(SUB + row, SUB), SUB), :] = value
 
     def begin(block, total):
         source = pl.multiple_of(block * SUB, SUB)
         row = pl.multiple_of(SUB + block * SUB, SUB)
+        pushes = paired(
+            [
+                scales.speed * momentum_ref[pl.ds(source, SUB), pl.ds(t * LANES, LANES)]
+                for t in range(tiles)
+            ],
+            lane,
+        )
         for t, value, near, below, right in around(first, row, tiles, lane):
-            push = scales.speed * momentum_ref[pl.ds(source, SUB), pl.ds(t * LANES, LANES)]
+            push = pushes[t]
             action = scales.site(value, below + right)
             energy[t, pl.ds(source, SUB), :] = scales.kinetic * (push * push) + action
             total = total + action
             second[t, pl.ds(row, SUB), :] = value + (push + scales.half(near, value))
         return total
 
-    for k in range(8):
-        loads[8 + k].wait()
-
     per_turn = 2
 
-    def begin_turn(i, total):
-        for b in range(per_turn):
-            total = begin(i * per_turn + b, total)
+    def open_chunk(k, total):
+        load(1, k).wait()
+        for b in range(chunk // SUB):
+            total = begin(k * (chunk // SUB) + b, total)
         return total
 
-    old_action = lax.fori_loop(0, blocks // per_turn, begin_turn, zero)
+    def open_turn(k, total):
+        bring(k + 1)
+        return open_chunk(k, total)
+
+    bring(0)
+    old_action = open_chunk(7, lax.fori_loop(0, 7, open_turn, zero))
 
     group = GROUP if (blocks - 2) % GROUP == 0 else 1
     for time in range(1, STEPS):
@@ -247,15 +301,17 @@
             )
         return copies
 
-    def choose(block, value, t):
+    def choose(block, evens, odds, u):
         row = pl.multiple_of(block * SUB, SUB)
-        cols = pl.ds(t * LANES, LANES)
-        kept = field_ref[pl.ds(row, SUB), cols]
-        chosen_ref[pl.ds(row, SUB), cols] = jnp.where(accepted, scales.back * value, kept)
+        for t, value in zip((u, u + tiles // 2), unpaired(evens, odds, lane)):
+            cols = pl.ds(t * LANES, LANES)
+            kept = field_ref[pl.ds(row, SUB), cols]
+            chosen_ref[pl.ds(row, SUB), cols] = jnp.where(accepted, scales.back * value, kept)
 
     for block in (1, blocks - 2):
-        for t in range(tiles):
-            choose(block, last[t, SUB + block * SUB : 2 * SUB + block * SUB, :], t)
+        part = pl.ds(SUB + block * SUB, SUB)
+        for u in range(tiles // 2):
+            choose(block, last[u, part, :], last[u + tiles // 2, part, :], u)
         for copy in emit(block):
             copy.start()
             stores.append(copy)
@@ -272,7 +328,10 @@
             change = change + (
                 (scales.kinetic * (moment * moment) + action) - energy[t, pl.ds(source, SUB), :]
             )
-            choose(block, value, t)
+            if t < tiles // 2:
+                evens = value
+            else:
+                choose(block, evens, value, t - tiles // 2)
         return change, total
 
     sums = (zero, zero)
@@ -409,10 +468,14 @@
                 if side == 1 and outermost:
                     old = old + energy_extra[t]
                 change = change + ((scales.kinetic * (moment * moment) + action) - old)
-                if outermost:
-                    cols = pl.ds(t * LANES, LANES)
-                    kept = head_ref[:, cols] if side == 0 else tail_ref[:, cols]
-                    chosen_ref[side, :, cols] = jnp.where(accepted, scales.back * value, kept)
+                if outermost and t < tiles // 2:
+                    evens = value
+                elif outermost:
+                    u = t - tiles // 2
+                    for c, part in zip((u, t), unpaired(evens, value, lane)):
+                        cols = pl.ds(c * LANES, LANES)
+                        kept = head_ref[:, cols] if side == 0 else tail_ref[:, cols]
+                        chosen_ref[side, :, cols] = jnp.where(accepted, scales.back * part, kept)
         block = 0 if side == 0 else blocks - 1
         for n, (member, column) in enumerate(slots(block, tiles, per_member)):
             size = per_member * LANES

time: 85.9 us -> 85.4 us (level)
  transfers between devices with their start and end apart: 4 -> 4, of which waited for: 3 -> 3; matrix products, arithmetic and copies ran while one was open for 0% -> 0% of each run, Pallas kernels for 13% -> 12%
where the time goes in v7:
time: 85.4 us; the launch traced here: 85 us
  waiting for transfers between devices  50.1 us (59%)
  Pallas kernels  18.6 us (22%)
  starting transfers between devices  13.3 us (16%)
  between operations  2.01 us (2%)
  local copies, waits for them, and re-layouts  1.07 us (1%)
    all_to_all x1, waiting for transfers between devices, body(): lax.all_to_all(outgoing, 'rep', split_axis=0, concat_axis=0, tiled=True)  26.1 us
    all_to_all x1, waiting for transfers between devices, body(): lax.all_to_all(ordered, 'rep', split_axis=0, concat_axis=0, tiled=True)  21.4 us
    pallas_call x1, Pallas kernels, body(): pl.pallas_call(functools.partial(inner_kernel, per_member), out_shape=(ja...  9.66 us
    all_to_all x1, starting transfers between devices, body(): lax.all_to_all(outgoing, 'rep', split_axis=0, concat_axis=0, tiled=True)  6.97 us
    all_to_all x1, starting transfers between devices, body(): lax.all_to_all(ordered, 'rep', split_axis=0, concat_axis=0, tiled=True)  4.85 us
    pallas_call x1, Pallas kernels, body(): pl.pallas_call(functools.partial(outer_kernel, per_member, len(halos)), g...  4.42 us
    ppermute x1, waiting for transfers between devices, body(): passing = lax.ppermute(passing, 'dom', forward)  2.57 us
    pallas_call x1, Pallas kernels, body(): pl.pallas_call(pack_kernel, grid=(1,), out_shape=jax.ShapeDtypeStruct((2,...  1.96 us
  transfers between devices with their start and end apart: 4, of which 3 were waited for; matrix products, arithmetic and copies ran while one was open for 0% of the time, Pallas kernels for 12%

profile of v7, /device:TPU:9, one launch (start us, length us, event | category | flops | bytes accessed | tf_op | source)
XLA Modules:
  0.0 85.0 jit_solution(14882343012668389371)
XLA Ops:
  1.3 2.0 %pack.1 = f32[2,2,16,8,128]{4,3,2,1,0:T(8,128)} custom-call(s32[1]{0:T(128)S(6)} %copy.14.labels_ref, f32[16]{0:T(128)} %betas_ref.5, f32[128,2048]{1,0:T(8,128)} %bitcast.5, f32[128,2048]{1,0:T(8,128)} %bitcast.6, f32[128,2048]{1,0:T(8,128)} %bitcast.10, f32[128,2048]{1,0:T(8,128)} %bitcast.11), custom_call_target="tpu_custom_call" | custom-call | tf_op jit(solution)/shard_map/pack/pallas_call | solution.py:562
  3.2 1.2 %collective-permute-start = (f32[2,2,16,8,128]{4,3,2,1,0:T(8,128)}, f32[2,2,16,8,128]{4,3,2,1,0:T(8,128)}, u32[]{:S(2)}, u32[]{:S(2)}) collective-permute-start(f32[2,2,16,8,128]{4,3,2,1,0:T(8,128)} %pack.1), channel_id=1, source_target_pairs={{0,1},{1,0},{2,3},{3,2},{4,5},{5,4},{6,7},{7,6},{8,9},{9,8},{10,11... | collective-permute-start | bytes 786440 | tf_op jit(solution)/shard_map/ppermute | solution.py:579
  5.1 9.7 %inner.1 = (f32[16,8,2176]{2,1,0:T(8,128)}, f32[2,2,16,24,128]{4,3,2,1,0:T(8,128)}, f32[2,16,16,128]{3,2,1,0:T(8,128)}, f32[3,8,128]{2,1,0:T(8,128)}) custom-call(s32[1]{0:T(128)S(6)} %copy.14.labels_ref, f32[16]{0:T(128)} %betas_ref.5, s32[1]{0:T(128)S(6)} %copy.15.accept_ref, f32[128,2048]{1,0:T(8,128)} %bitcast.7, f32[128,2048]{1,0:T(8,128)} %bitcast.12), custom_call_target="tpu_custom_call" | custom-call | flops 26214400 | bytes 4194304 | tf_op jit(solution)/shard_map/inner/pallas_call | solution.py:589
  14.8 0.0 collective-permute-done.refs_0_
  14.8 4.4 %outer.1 = f32[16,8,2176]{2,1,0:T(8,128)} custom-call(s32[1]{0:T(128)S(6)} %copy.14.labels_ref, f32[16]{0:T(128)} %betas_ref.5, s32[1]{0:T(128)S(6)} %copy.15.accept_ref, s32[16]{0:T(128)} %swap_ref.1, f32[2,2,16,8,128]{4,3,2,1,0:T(8,128)} %collective-permute-done.refs_0_, ...), custom_call_target="tpu_custom_call", output_to_operand_aliasing={{}: (10, {})} | custom-call | tf_op jit(solution)/shard_map/outer/pallas_call | solution.py:618
  19.2 0.0 copy-start.1
  19.3 7.0 %all-to-all-start = ((f32[16,8,2176]{2,1,0:T(8,128)}), f32[16,8,2176]{2,1,0:T(8,128)S(1)}, u32[]{:S(2)}, u32[]{:S(2)}) async-start(f32[16,8,2176]{2,1,0:T(8,128)} %outer.1), calls=%async_computation | async-start | bytes 2228224 | tf_op jit(solution)/shard_map/all_to_all | solution.py:645
  26.2 0.0 copy-done.1
  26.2 0.1 slice_bitcast_fusion._
  26.3 0.0 copy-start
  26.3 26.1 %all-to-all-done.got_ref = f32[16,8,2176]{2,1,0:T(8,128)S(1)} async-done(((f32[16,8,2176]{2,1,0:T(8,128)}), f32[16,8,2176]{2,1,0:T(8,128)S(1)}, u32[]{:S(2)}, u32[]{:S(2)}) %all-to-all-start) | async-done | bytes 1114144 | tf_op jit(solution)/shard_map/all_to_all | solution.py:645
  52.5 1.8 %place.1 = (f32[16,8,2048]{2,1,0:T(8,128)}, f32[16,128]{1,0:T(8,128)S(1)}) custom-call(f32[16,8,2176]{2,1,0:T(8,128)S(1)} %all-to-all-done.got_ref, f32[1,128,2048]{2,1,0:T(8,128)S(1)} %slice_bitcast_fusion._), custom_call_target="tpu_custom_call" | custom-call | tf_op jit(solution)/shard_map/place/pallas_call | solution.py:647
  54.3 0.0 copy-done
  54.3 4.9 %all-to-all-start.1 = ((f32[16,8,2048]{2,1,0:T(8,128)}), f32[16,8,2048]{2,1,0:T(8,128)S(1)}, u32[]{:S(2)}, u32[]{:S(2)}) async-start(f32[16,8,2048]{2,1,0:T(8,128)} %get-tuple-element.18), calls=%async_computation.1 | async-start | bytes 2097152 | tf_op jit(solution)/shard_map/all_to_all | solution.py:663
  59.1 0.2 collective-permute-start.1
  59.4 2.6 %collective-permute-done.1 = f32[16,128]{1,0:T(8,128)S(1)} collective-permute-done((f32[16,128]{1,0:T(8,128)S(1)}, f32[16,128]{1,0:T(8,128)S(1)}, u32[]{:S(2)}, u32[]{:S(2)}) %collective-permute-start.1) | collective-permute-done | bytes 8224 | tf_op jit(solution)/shard_map/ppermute | solution.py:667
  61.9 0.7 ladder.1
  62.7 21.4 %all-to-all-done.1 = f32[16,8,2048]{2,1,0:T(8,128)S(1)} async-done(((f32[16,8,2048]{2,1,0:T(8,128)}), f32[16,8,2048]{2,1,0:T(8,128)S(1)}, u32[]{:S(2)}, u32[]{:S(2)}) %all-to-all-start.1) | async-done | bytes 1048608 | tf_op jit(solution)/shard_map/all_to_all | solution.py:663
  84.0 1.0 %copy.16 = f32[1,128,2048]{2,1,0:T(8,128)} copy(f32[1,128,2048]{2,1,0:T(8,128)S(1)} %bitcast.13) | data formatting | bytes 2097152
  (1 shorter events, 0.0 us)
Async XLA Ops:
  3.2 11.6 %collective-permute-start = (f32[2,2,16,8,128]{4,3,2,1,0:T(8,128)}, f32[2,2,16,8,128]{4,3,2,1,0:T(8,128)}, u32[]{:S(2)}, u32[]{:S(2)}) collective-permute-start(f32[2,2,16,8,128]{4,3,2,1,0:T(8,128)} %pack.1), channel_id=1, source_target_pairs={{0,1},{1,0},{2,3},{3,2},{4,5},{5,4},{6,7},{7,6},{8,9},{9,8},{10,11... | collective-permute-start | bytes 786440 | tf_op jit(solution)/shard_map/ppermute | solution.py:579
  19.2 7.0 %copy-start.1 = (f32[16,8,2176]{2,1,0:T(8,128)S(1)}, f32[16,8,2176]{2,1,0:T(8,128)}, u32[]{:S(2)}) copy-start(f32[16,8,2176]{2,1,0:T(8,128)} %outer.1) | copy-start | bytes 3342340
  19.3 33.2 %all-to-all-start = ((f32[16,8,2176]{2,1,0:T(8,128)}), f32[16,8,2176]{2,1,0:T(8,128)S(1)}, u32[]{:S(2)}, u32[]{:S(2)}) async-start(f32[16,8,2176]{2,1,0:T(8,128)} %outer.1), calls=%async_computation | async-start | bytes 2228224 | tf_op jit(solution)/shard_map/all_to_all | solution.py:645
  26.3 27.9 %copy-start = (f32[1,128,2048]{2,1,0:T(8,128)}, f32[1,128,2048]{2,1,0:T(8,128)S(1)}, u32[]{:S(2)}) copy-start(f32[1,128,2048]{2,1,0:T(8,128)S(1)} %slice_bitcast_fusion._) | copy-start | bytes 3145732
  54.3 29.8 %all-to-all-start.1 = ((f32[16,8,2048]{2,1,0:T(8,128)}), f32[16,8,2048]{2,1,0:T(8,128)S(1)}, u32[]{:S(2)}, u32[]{:S(2)}) async-start(f32[16,8,2048]{2,1,0:T(8,128)} %get-tuple-element.18), calls=%async_computation.1 | async-start | bytes 2097152 | tf_op jit(solution)/shard_map/all_to_all | solution.py:663
  59.1 2.8 %collective-permute-start.1 = (f32[16,128]{1,0:T(8,128)S(1)}, f32[16,128]{1,0:T(8,128)S(1)}, u32[]{:S(2)}, u32[]{:S(2)}) collective-permute-start(f32[16,128]{1,0:T(8,128)S(1)} %get-tuple-element.19.notes_ref), channel_id=1, source_target_pairs={{0,1},{1,0},{2,3},{3,2},{4,5},{5,4},{6,7},{7,6},{8,9},{9,8},{10,11... | collective-permute-start | bytes 24584 | tf_op jit(solution)/shard_map/ppermute | solution.py:667

commit v8 on v7

--- a/solution.py
+++ b/solution.py
@@ -192,14 +192,15 @@
     rows, width = field_ref.shape
     tiles = width // LANES
     blocks = rows // SUB
-    chunk = rows // 8
+    chunks = 4
+    chunk = rows // chunks
 
     def load(a, k):
         source, target = ((field_hbm, field_ref), (momentum_hbm, momentum_ref))[a]
         part = pl.ds(pl.multiple_of(k * chunk, chunk), chunk)
         return pltpu.make_async_copy(source.at[part, :], target.at[part, :], in_sem.at[a, k])
 
-    for k in range(8):
+    for k in range(chunks):
         load(0, k).start()
         load(1, k).start()
     scales = Scales(chosen_scalars(labels_ref, betas_ref))
@@ -253,7 +254,7 @@
         return open_chunk(k, total)
 
     bring(0)
-    old_action = open_chunk(7, lax.fori_loop(0, 7, open_turn, zero))
+    old_action = open_chunk(chunks - 1, lax.fori_loop(0, chunks - 1, open_turn, zero))
 
     group = GROUP if (blocks - 2) % GROUP == 0 else 1
     for time in range(1, STEPS):
@@ -308,7 +309,7 @@
             kept = field_ref[pl.ds(row, SUB), cols]
             chosen_ref[pl.ds(row, SUB), cols] = jnp.where(accepted, scales.back * value, kept)
 
-    for block in (1, blocks - 2):
+    for block in range(1, blocks - 1):
         part = pl.ds(SUB + block * SUB, SUB)
         for u in range(tiles // 2):
             choose(block, last[u, part, :], last[u + tiles // 2, part, :], u)
@@ -328,33 +329,16 @@
             change = change + (
                 (scales.kinetic * (moment * moment) + action) - energy[t, pl.ds(source, SUB), :]
             )
-            if t < tiles // 2:
-                evens = value
-            else:
-                choose(block, evens, value, t - tiles // 2)
         return change, total
 
-    sums = (zero, zero)
-    if (blocks - 4) % per_turn == 0:
-        for i in range((blocks - 4) // per_turn):
-            sums = lax.fori_loop(
-                0,
-                1,
-                lambda _, carry, i=i: functools.reduce(
-                    lambda c, b: finish(2 + i * per_turn + b, c), range(per_turn), carry
-                ),
-                sums,
-            )
-            for b in range(per_turn):
-                for copy in emit(2 + i * per_turn + b):
-                    copy.start()
-                    stores.append(copy)
-    else:
-        for block in range(2, blocks - 2):
-            sums = finish(block, sums)
-            for copy in emit(block):
-                copy.start()
-                stores.append(copy)
+    turns = 4 if (blocks - 4) % 4 == 0 else 1
+
+    def finish_turn(i, carry):
+        for b in range(turns):
+            carry = finish(2 + i * turns + b, carry)
+        return carry
+
+    sums = lax.fori_loop(0, (blocks - 4) // turns, finish_turn, (zero, zero))
     sums_ref[0] = sums[0]
     sums_ref[1] = sums[1]
     sums_ref[2] = old_action
@@ -415,9 +399,9 @@
     zero = jnp.zeros((SUB, LANES), jnp.float32)
     old_extra = zero
     energy_extra = []
-    for copy in loads:
-        copy.wait()
     for side in range(2):
+        for copy in loads[4 * side : 4 * side + 3]:
+            copy.wait()
         edge = SUB if side == 0 else EDGE * SUB
         pad = 0 if side == 0 else (EDGE + 1) * SUB
         mine = 2 * SUB if side == 0 else (EDGE - 1) * SUB
@@ -450,44 +434,44 @@
             keep = sub > time if side == 0 else sub < SUB - 1 - time
             advance(before.at[side], after.at[side], edge, tiles, lane, scales)
             advance(before.at[side], after.at[side], mine, tiles, lane, scales, keep=keep)
+    copies = []
+    for side in range(2):
+        mine = 2 * SUB if side == 0 else (EDGE - 1) * SUB
+        block = 0 if side == 0 else blocks - 1
+        kept_ref = head_ref if side == 0 else tail_ref
+        for u in range(tiles // 2):
+            pair = (last[side, t, mine : mine + SUB, :] for t in (u, u + tiles // 2))
+            for c, part in zip((u, u + tiles // 2), unpaired(*pair, lane)):
+                cols = pl.ds(c * LANES, LANES)
+                chosen_ref[side, :, cols] = jnp.where(
+                    accepted, scales.back * part, kept_ref[:, cols]
+                )
+        for n, (member, column) in enumerate(slots(block, tiles, per_member)):
+            size = per_member * LANES
+            copy = pltpu.make_async_copy(
+                chosen_ref.at[side, :, pl.ds(column, size)],
+                send_hbm.at[member, :, pl.ds(0, size)],
+                send_sem.at[side, n],
+            )
+            copy.start()
+            copies.append(copy)
     change = sums_ref[0]
     total = sums_ref[1]
-    copies = []
     for side in range(2):
         own = 2 * SUB if side == 0 else 0
+        loads[4 * side + 3].wait()
         for b in range(2):
             place = b if side == 0 else EDGE - 2 + b
             row = own + place * SUB
-            outermost = (side == 0 and b == 0) or (side == 1 and b == 1)
             for t, value, near, below, right in around(last.at[side], row, tiles, lane):
                 gone = value - previous[side, t, pl.ds(row, SUB), :]
                 moment = gone + scales.half(near, value)
                 action = scales.site(value, below + right)
                 total = total + action
                 old = energy_ref[side, t, b * SUB : (b + 1) * SUB, :]
-                if side == 1 and outermost:
+                if side == 1 and b == 1:
                     old = old + energy_extra[t]
                 change = change + ((scales.kinetic * (moment * moment) + action) - old)
-                if outermost and t < tiles // 2:
-                    evens = value
-                elif outermost:
-                    u = t - tiles // 2
-                    for c, part in zip((u, t), unpaired(evens, value, lane)):
-                        cols = pl.ds(c * LANES, LANES)
-                        kept = head_ref[:, cols] if side == 0 else tail_ref[:, cols]
-                        chosen_ref[side, :, cols] = jnp.where(accepted, scales.back * part, kept)
-        block = 0 if side == 0 else blocks - 1
-        for n, (member, column) in enumerate(slots(block, tiles, per_member)):
-            size = per_member * LANES
-            copies.append(
-                pltpu.make_async_copy(
-                    chosen_ref.at[side, :, pl.ds(column, size)],
-                    send_hbm.at[member, :, pl.ds(0, size)],
-                    send_sem.at[side, n],
-                )
-            )
-    for copy in copies:
-        copy.start()
     old_action = sums_ref[2] + old_extra
     sites = blocks * SUB * tiles * LANES
     action = scales.action(jnp.where(accepted, total, old_action), sites)
@@ -603,7 +587,7 @@
             column,
             column,
             pltpu.VMEM((tiles, rows, LANES), f32),
-            dma((2, 8)),
+            dma((2, 4)),
             dma((members,)),
             dma((2, 3)),
         ],

time: 85.4 us -> 84.6 us (level)
  Pallas kernels: 18.6 us -> 17.7 us
    pallas_call x1, Pallas kernels: 9.66 us -> 8.79 us  [body(): pl.pallas_call(functools.partial(inner_kernel, per_member), out_shape=(ja...]
  transfers between devices with their start and end apart: 4 -> 4, of which waited for: 3 -> 3; matrix products, arithmetic and copies ran while one was open for 0% -> 0% of each run, Pallas kernels for 12% -> 11%
where the time goes in v8:
time: 84.6 us; the launch traced here: 84.1 us
  waiting for transfers between devices  50.1 us (59%)
  Pallas kernels  17.7 us (21%)
  starting transfers between devices  13.3 us (16%)
  between operations  2.01 us (2%)
  local copies, waits for them, and re-layouts  1.07 us (1%)
    all_to_all x1, waiting for transfers between devices, body(): lax.all_to_all(outgoing, 'rep', split_axis=0, concat_axis=0, tiled=True)  26.1 us
    all_to_all x1, waiting for transfers between devices, body(): lax.all_to_all(ordered, 'rep', split_axis=0, concat_axis=0, tiled=True)  21.4 us
    pallas_call x1, Pallas kernels, body(): pl.pallas_call(functools.partial(inner_kernel, per_member), out_shape=(ja...  8.79 us
    all_to_all x1, starting transfers between devices, body(): lax.all_to_all(outgoing, 'rep', split_axis=0, concat_axis=0, tiled=True)  6.97 us
    all_to_all x1, starting transfers between devices, body(): lax.all_to_all(ordered, 'rep', split_axis=0, concat_axis=0, tiled=True)  4.85 us
    pallas_call x1, Pallas kernels, body(): pl.pallas_call(functools.partial(outer_kernel, per_member, len(halos)), g...  4.42 us
    ppermute x1, waiting for transfers between devices, body(): passing = lax.ppermute(passing, 'dom', forward)  2.57 us
    pallas_call x1, Pallas kernels, body(): pl.pallas_call(pack_kernel, grid=(1,), out_shape=jax.ShapeDtypeStruct((2,...  1.96 us
  transfers between devices with their start and end apart: 4, of which 3 were waited for; matrix products, arithmetic and copies ran while one was open for 0% of the time, Pallas kernels for 11%

profile of v8, /device:TPU:9, one launch (start us, length us, event | category | flops | bytes accessed | tf_op | source)
XLA Modules:
  0.0 84.1 jit_solution(301572883218814328)
XLA Ops:
  1.3 2.0 %pack.1 = f32[2,2,16,8,128]{4,3,2,1,0:T(8,128)} custom-call(s32[1]{0:T(128)S(6)} %copy.14.labels_ref, f32[16]{0:T(128)} %betas_ref.5, f32[128,2048]{1,0:T(8,128)} %bitcast.5, f32[128,2048]{1,0:T(8,128)} %bitcast.6, f32[128,2048]{1,0:T(8,128)} %bitcast.10, f32[128,2048]{1,0:T(8,128)} %bitcast.11), custom_call_target="tpu_custom_call" | custom-call | tf_op jit(solution)/shard_map/pack/pallas_call | solution.py:546
  3.2 1.2 %collective-permute-start = (f32[2,2,16,8,128]{4,3,2,1,0:T(8,128)}, f32[2,2,16,8,128]{4,3,2,1,0:T(8,128)}, u32[]{:S(2)}, u32[]{:S(2)}) collective-permute-start(f32[2,2,16,8,128]{4,3,2,1,0:T(8,128)} %pack.1), channel_id=1, source_target_pairs={{0,1},{1,0},{2,3},{3,2},{4,5},{5,4},{6,7},{7,6},{8,9},{9,8},{10,11... | collective-permute-start | bytes 786440 | tf_op jit(solution)/shard_map/ppermute | solution.py:563
  5.1 8.8 %inner.1 = (f32[16,8,2176]{2,1,0:T(8,128)}, f32[2,2,16,24,128]{4,3,2,1,0:T(8,128)}, f32[2,16,16,128]{3,2,1,0:T(8,128)}, f32[3,8,128]{2,1,0:T(8,128)}) custom-call(s32[1]{0:T(128)S(6)} %copy.14.labels_ref, f32[16]{0:T(128)} %betas_ref.5, s32[1]{0:T(128)S(6)} %copy.15.accept_ref, f32[128,2048]{1,0:T(8,128)} %bitcast.7, f32[128,2048]{1,0:T(8,128)} %bitcast.12), custom_call_target="tpu_custom_call" | custom-call | flops 26214400 | bytes 4194304 | tf_op jit(solution)/shard_map/inner/pallas_call | solution.py:573
  13.9 0.0 collective-permute-done.refs_0_
  13.9 4.4 %outer.1 = f32[16,8,2176]{2,1,0:T(8,128)} custom-call(s32[1]{0:T(128)S(6)} %copy.14.labels_ref, f32[16]{0:T(128)} %betas_ref.5, s32[1]{0:T(128)S(6)} %copy.15.accept_ref, s32[16]{0:T(128)} %swap_ref.1, f32[2,2,16,8,128]{4,3,2,1,0:T(8,128)} %collective-permute-done.refs_0_, ...), custom_call_target="tpu_custom_call", output_to_operand_aliasing={{}: (10, {})} | custom-call | tf_op jit(solution)/shard_map/outer/pallas_call | solution.py:602
  18.4 0.0 copy-start.1
  18.4 7.0 %all-to-all-start = ((f32[16,8,2176]{2,1,0:T(8,128)}), f32[16,8,2176]{2,1,0:T(8,128)S(1)}, u32[]{:S(2)}, u32[]{:S(2)}) async-start(f32[16,8,2176]{2,1,0:T(8,128)} %outer.1), calls=%async_computation | async-start | bytes 2228224 | tf_op jit(solution)/shard_map/all_to_all | solution.py:629
  25.3 0.0 copy-done.1
  25.4 0.1 slice_bitcast_fusion._
  25.5 0.0 copy-start
  25.5 26.1 %all-to-all-done.got_ref = f32[16,8,2176]{2,1,0:T(8,128)S(1)} async-done(((f32[16,8,2176]{2,1,0:T(8,128)}), f32[16,8,2176]{2,1,0:T(8,128)S(1)}, u32[]{:S(2)}, u32[]{:S(2)}) %all-to-all-start) | async-done | bytes 1114144 | tf_op jit(solution)/shard_map/all_to_all | solution.py:629
  51.6 1.8 %place.1 = (f32[16,8,2048]{2,1,0:T(8,128)}, f32[16,128]{1,0:T(8,128)S(1)}) custom-call(f32[16,8,2176]{2,1,0:T(8,128)S(1)} %all-to-all-done.got_ref, f32[1,128,2048]{2,1,0:T(8,128)S(1)} %slice_bitcast_fusion._), custom_call_target="tpu_custom_call" | custom-call | tf_op jit(solution)/shard_map/place/pallas_call | solution.py:631
  53.4 0.0 copy-done
  53.4 4.9 %all-to-all-start.1 = ((f32[16,8,2048]{2,1,0:T(8,128)}), f32[16,8,2048]{2,1,0:T(8,128)S(1)}, u32[]{:S(2)}, u32[]{:S(2)}) async-start(f32[16,8,2048]{2,1,0:T(8,128)} %get-tuple-element.18), calls=%async_computation.1 | async-start | bytes 2097152 | tf_op jit(solution)/shard_map/all_to_all | solution.py:647
  58.2 0.2 collective-permute-start.1
  58.5 2.6 %collective-permute-done.1 = f32[16,128]{1,0:T(8,128)S(1)} collective-permute-done((f32[16,128]{1,0:T(8,128)S(1)}, f32[16,128]{1,0:T(8,128)S(1)}, u32[]{:S(2)}, u32[]{:S(2)}) %collective-permute-start.1) | collective-permute-done | bytes 8224 | tf_op jit(solution)/shard_map/ppermute | solution.py:651
  61.0 0.7 ladder.1
  61.8 21.4 %all-to-all-done.1 = f32[16,8,2048]{2,1,0:T(8,128)S(1)} async-done(((f32[16,8,2048]{2,1,0:T(8,128)}), f32[16,8,2048]{2,1,0:T(8,128)S(1)}, u32[]{:S(2)}, u32[]{:S(2)}) %all-to-all-start.1) | async-done | bytes 1048608 | tf_op jit(solution)/shard_map/all_to_all | solution.py:647
  83.2 1.0 %copy.16 = f32[1,128,2048]{2,1,0:T(8,128)} copy(f32[1,128,2048]{2,1,0:T(8,128)S(1)} %bitcast.13) | data formatting | bytes 2097152
  (1 shorter events, 0.0 us)
Async XLA Ops:
  3.2 10.7 %collective-permute-start = (f32[2,2,16,8,128]{4,3,2,1,0:T(8,128)}, f32[2,2,16,8,128]{4,3,2,1,0:T(8,128)}, u32[]{:S(2)}, u32[]{:S(2)}) collective-permute-start(f32[2,2,16,8,128]{4,3,2,1,0:T(8,128)} %pack.1), channel_id=1, source_target_pairs={{0,1},{1,0},{2,3},{3,2},{4,5},{5,4},{6,7},{7,6},{8,9},{9,8},{10,11... | collective-permute-start | bytes 786440 | tf_op jit(solution)/shard_map/ppermute | solution.py:563
  18.4 7.0 %copy-start.1 = (f32[16,8,2176]{2,1,0:T(8,128)S(1)}, f32[16,8,2176]{2,1,0:T(8,128)}, u32[]{:S(2)}) copy-start(f32[16,8,2176]{2,1,0:T(8,128)} %outer.1) | copy-start | bytes 3342340
  18.4 33.2 %all-to-all-start = ((f32[16,8,2176]{2,1,0:T(8,128)}), f32[16,8,2176]{2,1,0:T(8,128)S(1)}, u32[]{:S(2)}, u32[]{:S(2)}) async-start(f32[16,8,2176]{2,1,0:T(8,128)} %outer.1), calls=%async_computation | async-start | bytes 2228224 | tf_op jit(solution)/shard_map/all_to_all | solution.py:629
  25.5 27.9 %copy-start = (f32[1,128,2048]{2,1,0:T(8,128)}, f32[1,128,2048]{2,1,0:T(8,128)S(1)}, u32[]{:S(2)}) copy-start(f32[1,128,2048]{2,1,0:T(8,128)S(1)} %slice_bitcast_fusion._) | copy-start | bytes 3145732
  53.4 29.8 %all-to-all-start.1 = ((f32[16,8,2048]{2,1,0:T(8,128)}), f32[16,8,2048]{2,1,0:T(8,128)S(1)}, u32[]{:S(2)}, u32[]{:S(2)}) async-start(f32[16,8,2048]{2,1,0:T(8,128)} %get-tuple-element.18), calls=%async_computation.1 | async-start | bytes 2097152 | tf_op jit(solution)/shard_map/all_to_all | solution.py:647
  58.2 2.8 %collective-permute-start.1 = (f32[16,128]{1,0:T(8,128)S(1)}, f32[16,128]{1,0:T(8,128)S(1)}, u32[]{:S(2)}, u32[]{:S(2)}) collective-permute-start(f32[16,128]{1,0:T(8,128)S(1)} %get-tuple-element.19.notes_ref), channel_id=1, source_target_pairs={{0,1},{1,0},{2,3},{3,2},{4,5},{5,4},{6,7},{7,6},{8,9},{9,8},{10,11... | collective-permute-start | bytes 24584 | tf_op jit(solution)/shard_map/ppermute | solution.py:651

commit v9 on v8

--- a/solution.py
+++ b/solution.py
@@ -55,10 +55,6 @@
 
     def action(self, total, sites):
         return jnp.sum(total) / self.cold + quartic * sites
-
-
-def chosen_scalars(labels_ref, betas_ref):
-    return betas_ref[labels_ref[0]]
 
 
 def paired(values, lane):
@@ -124,8 +120,25 @@
         after[t, pl.ds(row, SUB), :] = new
 
 
-def pack_kernel(labels_ref, betas_ref, head_ref, tail_ref, head_m_ref, tail_m_ref, out_ref):
-    scales = Scales(chosen_scalars(labels_ref, betas_ref))
+def pack_kernel(
+    labels_ref,
+    betas_ref,
+    swap_ref,
+    head_ref,
+    tail_ref,
+    head_m_ref,
+    tail_m_ref,
+    edges_hbm,
+    cold_ref,
+    label_ref,
+    out_ref,
+    out_sem,
+):
+    cold = betas_ref[labels_ref[0]]
+    cold_ref[0] = cold
+    label_ref[0] = swap_ref[labels_ref[0]]
+    copies = []
+    scales = Scales(cold)
     lane = lane_index()
     row = row_index()
     tiles = head_ref.shape[1] // LANES
@@ -161,6 +174,11 @@
                 push = pushes[t] + scales.half((up + down) + near, value)
                 out_ref[side, 0, t] = value
                 out_ref[side, 1, t] = value + push
+        copy = pltpu.make_async_copy(out_ref.at[side], edges_hbm.at[side], out_sem.at[side])
+        copy.start()
+        copies.append(copy)
+    for copy in copies:
+        copy.wait()
 
 
 def slots(row_block, tiles, per_member):
@@ -170,14 +188,14 @@
 
 def inner_kernel(
     per_member,
-    labels_ref,
-    betas_ref,
+    cold_ref,
     accept_ref,
     field_hbm,
     momentum_hbm,
     send_hbm,
     state_hbm,
     energy_hbm,
+    sums_hbm,
     sums_ref,
     field_ref,
     momentum_ref,
@@ -203,7 +221,7 @@
     for k in range(chunks):
         load(0, k).start()
         load(1, k).start()
-    scales = Scales(chosen_scalars(labels_ref, betas_ref))
+    scales = Scales(cold_ref[0])
     accepted = accept_ref[0] == 1
     lane = lane_index()
     sub = row_index()
@@ -342,6 +360,9 @@
     sums_ref[0] = sums[0]
     sums_ref[1] = sums[1]
     sums_ref[2] = old_action
+    copy = pltpu.make_async_copy(sums_ref, sums_hbm, state_sem.at[0, 3])
+    copy.start()
+    stores.append(copy)
     for copy in stores:
         copy.wait()
 
@@ -349,19 +370,17 @@
 def outer_kernel(
     per_member,
     halos,
-    labels_ref,
-    betas_ref,
+    cold_ref,
     accept_ref,
-    swap_ref,
+    label_ref,
     *refs,
 ):
     halo_refs = refs[:halos]
     (
         state_hbm,
         energy_hbm,
-        sums_ref,
-        head_ref,
-        tail_ref,
+        sums_hbm,
+        field_hbm,
         _,
         send_hbm,
         first,
@@ -369,6 +388,8 @@
         energy_ref,
         halo_ref,
         chosen_ref,
+        field_ref,
+        sums_ref,
         note_ref,
         in_sem,
         send_sem,
@@ -383,13 +404,17 @@
             for n, buffer in enumerate((last, previous))
         ]
         parts.append((halo_refs[side % halos].at[1 - side], halo_ref.at[side]))
+        edge_rows = pl.ds(0 if side == 0 else field_hbm.shape[0] - SUB, SUB)
         parts.append((energy_hbm.at[side], energy_ref.at[side]))
+        parts.append((field_hbm.at[edge_rows, :], field_ref.at[side]))
+        if side == 1:
+            parts.append((sums_hbm, sums_ref))
         for n, (source, target) in enumerate(parts):
             copy = pltpu.make_async_copy(source, target, in_sem.at[side, n])
             copy.start()
             loads.append(copy)
-    scales = Scales(chosen_scalars(labels_ref, betas_ref))
-    label = swap_ref[labels_ref[0]].astype(jnp.float32)
+    scales = Scales(cold_ref[0])
+    label = label_ref[0].astype(jnp.float32)
     accepted = accept_ref[0] == 1
     lane = lane_index()
     sub = row_index()
@@ -400,7 +425,7 @@
     old_extra = zero
     energy_extra = []
     for side in range(2):
-        for copy in loads[4 * side : 4 * side + 3]:
+        for copy in loads[5 * side : 5 * side + 3]:
             copy.wait()
         edge = SUB if side == 0 else EDGE * SUB
         pad = 0 if side == 0 else (EDGE + 1) * SUB
@@ -438,7 +463,8 @@
     for side in range(2):
         mine = 2 * SUB if side == 0 else (EDGE - 1) * SUB
         block = 0 if side == 0 else blocks - 1
-        kept_ref = head_ref if side == 0 else tail_ref
+        loads[5 * side + 4].wait()
+        kept_ref = field_ref.at[side]
         for u in range(tiles // 2):
             pair = (last[side, t, mine : mine + SUB, :] for t in (u, u + tiles // 2))
             for c, part in zip((u, u + tiles // 2), unpaired(*pair, lane)):
@@ -455,11 +481,12 @@
             )
             copy.start()
             copies.append(copy)
+    loads[10].wait()
     change = sums_ref[0]
     total = sums_ref[1]
     for side in range(2):
         own = 2 * SUB if side == 0 else 0
-        loads[4 * side + 3].wait()
+        loads[5 * side + 3].wait()
         for b in range(2):
             place = b if side == 0 else EDGE - 2 + b
             row = own + place * SUB
@@ -476,17 +503,16 @@
     sites = blocks * SUB * tiles * LANES
     action = scales.action(jnp.where(accepted, total, old_action), sites)
     change = jnp.sum(change)
-    note_ref[...] = jnp.where(
+    note = jnp.where(
         lane == 0, label, jnp.where(lane == 1, action, jnp.where(lane == 2, change, 0.0))
     )
     for member in range(members):
-        copy = pltpu.make_async_copy(
-            note_ref,
-            send_hbm.at[member, :, pl.ds(per_member * LANES, LANES)],
-            note_sem.at[member],
-        )
-        copy.start()
-        copies.append(copy)
+        note_ref[member] = note
+    copy = pltpu.make_async_copy(
+        note_ref, send_hbm.at[:, :, pl.ds(per_member * LANES, LANES)], note_sem
+    )
+    copy.start()
+    copies.append(copy)
     for copy in copies:
         copy.wait()
 
@@ -510,7 +536,7 @@
         copy.wait()
 
 
-def ladder_kernel(sites, notes_ref, sums_ref, label_ref, change_ref, ladder_ref):
+def ladder_kernel(sites, notes_ref, sums_ref, change_ref, ladder_ref):
     me = lax.axis_index("rep")
     notes = notes_ref[...]
     sums = sums_ref[...]
@@ -520,7 +546,6 @@
     actions = pltpu.roll(sums, LANES - 1, 1)
     ladder_ref[0] = jnp.sum(jnp.where(held, actions, 0.0)) / sites
     own = replica == me
-    label_ref[0] = jnp.sum(jnp.where(own & (lane == 0), notes, 0.0)).astype(jnp.int32)
     change_ref[0] = jnp.sum(jnp.where(own & (lane == 2), sums, 0.0))
 
 
@@ -543,11 +568,16 @@
     dma = pltpu.SemaphoreType.DMA
     last16 = rows // (2 * SUB) - 1
     last8 = rows // SUB - 1
-    edges = pl.pallas_call(
+    edges, cold, new_label = pl.pallas_call(
         pack_kernel,
         grid=(1,),
-        out_shape=jax.ShapeDtypeStruct((2, 2, tiles, SUB, LANES), f32),
+        out_shape=(
+            jax.ShapeDtypeStruct((2, 2, tiles, SUB, LANES), f32),
+            jax.ShapeDtypeStruct((1,), f32),
+            jax.ShapeDtypeStruct((1,), jnp.int32),
+        ),
         in_specs=[
+            smem,
             smem,
             smem,
             pl.BlockSpec((2 * SUB, width), lambda i: (0, 0)),
@@ -555,9 +585,10 @@
             pl.BlockSpec((SUB, width), lambda i: (0, 0)),
             pl.BlockSpec((SUB, width), lambda i: (last8, 0)),
         ],
-        out_specs=pl.BlockSpec((2, 2, tiles, SUB, LANES), lambda i: (0, 0, 0, 0, 0)),
+        out_specs=(inhbm, smem, smem),
+        scratch_shapes=[pltpu.VMEM((2, 2, tiles, SUB, LANES), f32), dma((2,))],
         name="pack",
-    )(labels, betas, start, start, moment, moment)
+    )(labels, betas, swap_pairs, start, start, moment, moment)
     forward = [(i, (i + 1) % strips) for i in range(strips)]
     backward = [((i + 1) % strips, i) for i in range(strips)]
     halos = (lax.ppermute(edges, "dom", forward),)
@@ -578,9 +609,10 @@
             jax.ShapeDtypeStruct((2, tiles, 2 * SUB, LANES), f32),
             jax.ShapeDtypeStruct((3, SUB, LANES), f32),
         ),
-        in_specs=[smem, smem, smem, inhbm, inhbm],
-        out_specs=(inhbm, inhbm, inhbm, vmem),
+        in_specs=[smem, smem, inhbm, inhbm],
+        out_specs=(inhbm, inhbm, inhbm, inhbm),
         scratch_shapes=[
+            pltpu.VMEM((3, SUB, LANES), f32),
             strip,
             strip,
             strip,
@@ -589,28 +621,19 @@
             pltpu.VMEM((tiles, rows, LANES), f32),
             dma((2, 4)),
             dma((members,)),
-            dma((2, 3)),
+            dma((2, 4)),
         ],
         cost_estimate=pl.CostEstimate(
             flops=100 * rows * width, bytes_accessed=16 * rows * width, transcendentals=0
         ),
         compiler_params=pltpu.CompilerParams(vmem_limit_bytes=WHOLE_VMEM),
         name="inner",
-    )(labels, betas, accept, start, moment)
+    )(cold, accept, start, moment)
     window = pltpu.VMEM((2, tiles, (EDGE + 2) * SUB, LANES), f32)
-    count = 4 + len(halos)
     outgoing = pl.pallas_call(
         functools.partial(outer_kernel, per_member, len(halos)),
-        grid=(1,),
         out_shape=jax.ShapeDtypeStruct((members, SUB, piece + LANES), f32),
-        in_specs=[smem] * 4
-        + [anywhere] * len(halos)
-        + [inhbm, inhbm, vmem]
-        + [
-            pl.BlockSpec((SUB, width), lambda i: (0, 0)),
-            pl.BlockSpec((SUB, width), lambda i: (last8, 0)),
-            inhbm,
-        ],
+        in_specs=[smem] * 3 + [anywhere] * len(halos) + [inhbm] * 5,
         out_specs=inhbm,
         scratch_shapes=[
             window,
@@ -618,14 +641,16 @@
             pltpu.VMEM((2, tiles, 2 * SUB, LANES), f32),
             pltpu.VMEM((2, 2, tiles, SUB, LANES), f32),
             pltpu.VMEM((2, SUB, width), f32),
-            pltpu.VMEM((SUB, LANES), f32),
-            dma((2, 4)),
+            pltpu.VMEM((2, SUB, width), f32),
+            pltpu.VMEM((3, SUB, LANES), f32),
+            pltpu.VMEM((members, SUB, LANES), f32),
+            dma((2, 6)),
             dma((2, shares)),
-            dma((members,)),
+            dma,
         ],
-        input_output_aliases={count + 5: 0},
+        input_output_aliases={7 + len(halos): 0},
         name="outer",
-    )(labels, betas, accept, swap_pairs, *halos, state, energy, sums, start, start, outgoing)
+    )(cold, accept, new_label, *halos, state, energy, sums, start, outgoing)
     received = lax.all_to_all(outgoing, "rep", split_axis=0, concat_axis=0, tiled=True)
     out = strip_of(outgoing[:, :, :piece])
     ordered, notes = pl.pallas_call(
@@ -650,15 +675,14 @@
     for _ in range(strips - 1):
         passing = lax.ppermute(passing, "dom", forward)
         both = both + passing
-    new_label, change, ladder = pl.pallas_call(
+    change, ladder = pl.pallas_call(
         functools.partial(ladder_kernel, strips * rows * width),
         out_shape=(
-            jax.ShapeDtypeStruct((1,), jnp.int32),
             jax.ShapeDtypeStruct((1,), f32),
             jax.ShapeDtypeStruct((1,), f32),
         ),
         in_specs=[vmem, vmem],
-        out_specs=(smem, smem, smem),
+        out_specs=(smem, smem),
         compiler_params=pltpu.CompilerParams(vmem_limit_bytes=4 << 20),
         name="ladder",
     )(notes, both)

time: 84.6 us -> 85.3 us (level)
    pallas_call x2, Pallas kernels: 6.38 us -> 7.3 us  [the longest x1 4.85 us: body(): pl.pallas_call(functools.partial(outer_kernel, per_member, len(halos)), o...]
where the time goes in v9:
time: 85.3 us; the launch traced here: 84.9 us
  waiting for transfers between devices  50.1 us (59%)
  Pallas kernels  18.4 us (22%)
  starting transfers between devices  13.4 us (16%)
  between operations  2.02 us (2%)
  local copies, waits for them, and re-layouts  1.07 us (1%)
    all_to_all x1, waiting for transfers between devices, body(): lax.all_to_all(outgoing, 'rep', split_axis=0, concat_axis=0, tiled=True)  26.1 us
    all_to_all x1, waiting for transfers between devices, body(): lax.all_to_all(ordered, 'rep', split_axis=0, concat_axis=0, tiled=True)  21.4 us
    pallas_call x1, Pallas kernels, body(): pl.pallas_call(functools.partial(inner_kernel, per_member), out_shape=(ja...  8.6 us
    all_to_all x1, starting transfers between devices, body(): lax.all_to_all(outgoing, 'rep', split_axis=0, concat_axis=0, tiled=True)  6.97 us
    all_to_all x1, starting transfers between devices, body(): lax.all_to_all(ordered, 'rep', split_axis=0, concat_axis=0, tiled=True)  4.85 us
    pallas_call x1, Pallas kernels, body(): pl.pallas_call(functools.partial(outer_kernel, per_member, len(halos)), o...  4.85 us
    ppermute x1, waiting for transfers between devices, body(): passing = lax.ppermute(passing, 'dom', forward)  2.57 us
    pallas_call x1, Pallas kernels, body(): pl.pallas_call(pack_kernel, grid=(1,), out_shape=(jax.ShapeDtypeStruct((2...  2.45 us
  transfers between devices with their start and end apart: 4, of which 3 were waited for; matrix products, arithmetic and copies ran while one was open for 0% of the time, Pallas kernels for 11%

profile of v9, /device:TPU:9, one launch (start us, length us, event | category | flops | bytes accessed | tf_op | source)
XLA Modules:
  0.0 84.9 jit_solution(4697643510640791641)
XLA Ops:
  1.3 2.5 %pack.1 = (f32[2,2,16,8,128]{4,3,2,1,0:T(8,128)}, f32[1]{0:T(128)}, s32[1]{0:T(128)}) custom-call(s32[1]{0:T(128)S(6)} %copy.14.labels_ref, f32[16]{0:T(128)} %betas_ref.1, s32[16]{0:T(128)} %swap_ref.1, f32[128,2048]{1,0:T(8,128)} %bitcast.5, f32[128,2048]{1,0:T(8,128)} %bitcast.6, f32[128,2048]{1,0:T(8,128)} %bitcast.9, f32[128,2048]{1,0:T(8,128)} %bitcast.10), custom_call_target="tpu_custom_call" | custom-call | tf_op jit(solution)/shard_map/pack/pallas_call | solution.py:571
  3.7 1.3 %collective-permute-start = (f32[2,2,16,8,128]{4,3,2,1,0:T(8,128)}, f32[2,2,16,8,128]{4,3,2,1,0:T(8,128)}, u32[]{:S(2)}, u32[]{:S(2)}) collective-permute-start(f32[2,2,16,8,128]{4,3,2,1,0:T(8,128)} %get-tuple-element.18), channel_id=1, source_target_pairs={{0,1},{1,0},{2,3},{3,2},{4,5},{5,4},{6,7},{7,6},{8,9},{9,8},{10,11... | collective-permute-start | bytes 786440 | tf_op jit(solution)/shard_map/ppermute | solution.py:594
  5.7 8.6 %inner.1 = (f32[16,8,2176]{2,1,0:T(8,128)}, f32[2,2,16,24,128]{4,3,2,1,0:T(8,128)}, f32[2,16,16,128]{3,2,1,0:T(8,128)}, f32[3,8,128]{2,1,0:T(8,128)}) custom-call(f32[1]{0:T(128)} %get-tuple-element.16.cold_ref, s32[1]{0:T(128)S(6)} %copy.15.accept_ref, f32[128,2048]{1,0:T(8,128)} %bitcast.7, f32[128,2048]{1,0:T(8,128)} %bitcast.11), custom_call_target="tpu_custom_call" | custom-call | flops 26214400 | bytes 4194304 | tf_op jit(solution)/shard_map/inner/pallas_call | solution.py:604
  14.3 0.0 collective-permute-done.refs_0_
  14.3 4.8 %outer.1 = f32[16,8,2176]{2,1,0:T(8,128)} custom-call(f32[1]{0:T(128)} %get-tuple-element.16.cold_ref, s32[1]{0:T(128)S(6)} %copy.15.accept_ref, s32[1]{0:T(128)} %get-tuple-element.34.label_ref, f32[2,2,16,8,128]{4,3,2,1,0:T(8,128)} %collective-permute-done.refs_0_, ...), custom_call_target="tpu_custom_call", output_to_operand_aliasing={{}: (8, {})} | custom-call | tf_op jit(solution)/shard_map/outer/pallas_call | solution.py:633
  19.2 0.0 copy-start.1
  19.2 7.0 %all-to-all-start = ((f32[16,8,2176]{2,1,0:T(8,128)}), f32[16,8,2176]{2,1,0:T(8,128)S(1)}, u32[]{:S(2)}, u32[]{:S(2)}) async-start(f32[16,8,2176]{2,1,0:T(8,128)} %outer.1), calls=%async_computation | async-start | bytes 2228224 | tf_op jit(solution)/shard_map/all_to_all | solution.py:654
  26.2 0.0 copy-done.1
  26.2 0.1 slice_bitcast_fusion._
  26.3 0.0 copy-start
  26.3 26.1 %all-to-all-done.got_ref = f32[16,8,2176]{2,1,0:T(8,128)S(1)} async-done(((f32[16,8,2176]{2,1,0:T(8,128)}), f32[16,8,2176]{2,1,0:T(8,128)S(1)}, u32[]{:S(2)}, u32[]{:S(2)}) %all-to-all-start) | async-done | bytes 1114144 | tf_op jit(solution)/shard_map/all_to_all | solution.py:654
  52.4 1.8 %place.1 = (f32[16,8,2048]{2,1,0:T(8,128)}, f32[16,128]{1,0:T(8,128)S(1)}) custom-call(f32[16,8,2176]{2,1,0:T(8,128)S(1)} %all-to-all-done.got_ref, f32[1,128,2048]{2,1,0:T(8,128)S(1)} %slice_bitcast_fusion._), custom_call_target="tpu_custom_call" | custom-call | tf_op jit(solution)/shard_map/place/pallas_call | solution.py:656
  54.2 0.0 copy-done
  54.2 4.9 %all-to-all-start.1 = ((f32[16,8,2048]{2,1,0:T(8,128)}), f32[16,8,2048]{2,1,0:T(8,128)S(1)}, u32[]{:S(2)}, u32[]{:S(2)}) async-start(f32[16,8,2048]{2,1,0:T(8,128)} %get-tuple-element.23), calls=%async_computation.1 | async-start | bytes 2097152 | tf_op jit(solution)/shard_map/all_to_all | solution.py:672
  59.1 0.2 collective-permute-start.1
  59.3 2.6 %collective-permute-done.1 = f32[16,128]{1,0:T(8,128)S(1)} collective-permute-done((f32[16,128]{1,0:T(8,128)S(1)}, f32[16,128]{1,0:T(8,128)S(1)}, u32[]{:S(2)}, u32[]{:S(2)}) %collective-permute-start.1) | collective-permute-done | bytes 8224 | tf_op jit(solution)/shard_map/ppermute | solution.py:676
  61.9 0.7 ladder.1
  62.6 21.4 %all-to-all-done.1 = f32[16,8,2048]{2,1,0:T(8,128)S(1)} async-done(((f32[16,8,2048]{2,1,0:T(8,128)}), f32[16,8,2048]{2,1,0:T(8,128)S(1)}, u32[]{:S(2)}, u32[]{:S(2)}) %all-to-all-start.1) | async-done | bytes 1048608 | tf_op jit(solution)/shard_map/all_to_all | solution.py:672
  84.0 1.0 %copy.16 = f32[1,128,2048]{2,1,0:T(8,128)} copy(f32[1,128,2048]{2,1,0:T(8,128)S(1)} %bitcast.12) | data formatting | bytes 2097152
  (1 shorter events, 0.0 us)
Async XLA Ops:
  3.7 10.6 %collective-permute-start = (f32[2,2,16,8,128]{4,3,2,1,0:T(8,128)}, f32[2,2,16,8,128]{4,3,2,1,0:T(8,128)}, u32[]{:S(2)}, u32[]{:S(2)}) collective-permute-start(f32[2,2,16,8,128]{4,3,2,1,0:T(8,128)} %get-tuple-element.18), channel_id=1, source_target_pairs={{0,1},{1,0},{2,3},{3,2},{4,5},{5,4},{6,7},{7,6},{8,9},{9,8},{10,11... | collective-permute-start | bytes 786440 | tf_op jit(solution)/shard_map/ppermute | solution.py:594
  19.2 7.0 %copy-start.1 = (f32[16,8,2176]{2,1,0:T(8,128)S(1)}, f32[16,8,2176]{2,1,0:T(8,128)}, u32[]{:S(2)}) copy-start(f32[16,8,2176]{2,1,0:T(8,128)} %outer.1) | copy-start | bytes 3342340
  19.2 33.2 %all-to-all-start = ((f32[16,8,2176]{2,1,0:T(8,128)}), f32[16,8,2176]{2,1,0:T(8,128)S(1)}, u32[]{:S(2)}, u32[]{:S(2)}) async-start(f32[16,8,2176]{2,1,0:T(8,128)} %outer.1), calls=%async_computation | async-start | bytes 2228224 | tf_op jit(solution)/shard_map/all_to_all | solution.py:654
  26.3 27.9 %copy-start = (f32[1,128,2048]{2,1,0:T(8,128)}, f32[1,128,2048]{2,1,0:T(8,128)S(1)}, u32[]{:S(2)}) copy-start(f32[1,128,2048]{2,1,0:T(8,128)S(1)} %slice_bitcast_fusion._) | copy-start | bytes 3145732
  54.2 29.8 %all-to-all-start.1 = ((f32[16,8,2048]{2,1,0:T(8,128)}), f32[16,8,2048]{2,1,0:T(8,128)S(1)}, u32[]{:S(2)}, u32[]{:S(2)}) async-start(f32[16,8,2048]{2,1,0:T(8,128)} %get-tuple-element.23), calls=%async_computation.1 | async-start | bytes 2097152 | tf_op jit(solution)/shard_map/all_to_all | solution.py:672
  59.1 2.8 %collective-permute-start.1 = (f32[16,128]{1,0:T(8,128)S(1)}, f32[16,128]{1,0:T(8,128)S(1)}, u32[]{:S(2)}, u32[]{:S(2)}) collective-permute-start(f32[16,128]{1,0:T(8,128)S(1)} %get-tuple-element.24.notes_ref), channel_id=1, source_target_pairs={{0,1},{1,0},{2,3},{3,2},{4,5},{5,4},{6,7},{7,6},{8,9},{9,8},{10,11... | collective-permute-start | bytes 24584 | tf_op jit(solution)/shard_map/ppermute | solution.py:676

commit v10 on v9

--- a/solution.py
+++ b/solution.py
@@ -120,25 +120,8 @@
         after[t, pl.ds(row, SUB), :] = new
 
 
-def pack_kernel(
-    labels_ref,
-    betas_ref,
-    swap_ref,
-    head_ref,
-    tail_ref,
-    head_m_ref,
-    tail_m_ref,
-    edges_hbm,
-    cold_ref,
-    label_ref,
-    out_ref,
-    out_sem,
-):
-    cold = betas_ref[labels_ref[0]]
-    cold_ref[0] = cold
-    label_ref[0] = swap_ref[labels_ref[0]]
-    copies = []
-    scales = Scales(cold)
+def pack_kernel(labels_ref, betas_ref, head_ref, tail_ref, head_m_ref, tail_m_ref, out_ref):
+    scales = Scales(betas_ref[labels_ref[0]])
     lane = lane_index()
     row = row_index()
     tiles = head_ref.shape[1] // LANES
@@ -174,11 +157,6 @@
                 push = pushes[t] + scales.half((up + down) + near, value)
                 out_ref[side, 0, t] = value
                 out_ref[side, 1, t] = value + push
-        copy = pltpu.make_async_copy(out_ref.at[side], edges_hbm.at[side], out_sem.at[side])
-        copy.start()
-        copies.append(copy)
-    for copy in copies:
-        copy.wait()
 
 
 def slots(row_block, tiles, per_member):
@@ -188,7 +166,8 @@
 
 def inner_kernel(
     per_member,
-    cold_ref,
+    labels_ref,
+    betas_ref,
     accept_ref,
     field_hbm,
     momentum_hbm,
@@ -221,7 +200,7 @@
     for k in range(chunks):
         load(0, k).start()
         load(1, k).start()
-    scales = Scales(cold_ref[0])
+    scales = Scales(betas_ref[labels_ref[0]])
     accepted = accept_ref[0] == 1
     lane = lane_index()
     sub = row_index()
@@ -370,9 +349,10 @@
 def outer_kernel(
     per_member,
     halos,
-    cold_ref,
+    labels_ref,
+    betas_ref,
     accept_ref,
-    label_ref,
+    swap_ref,
     *refs,
 ):
     halo_refs = refs[:halos]
@@ -413,8 +393,8 @@
             copy = pltpu.make_async_copy(source, target, in_sem.at[side, n])
             copy.start()
             loads.append(copy)
-    scales = Scales(cold_ref[0])
-    label = label_ref[0].astype(jnp.float32)
+    scales = Scales(betas_ref[labels_ref[0]])
+    label = swap_ref[labels_ref[0]].astype(jnp.float32)
     accepted = accept_ref[0] == 1
     lane = lane_index()
     sub = row_index()
@@ -536,7 +516,7 @@
         copy.wait()
 
 
-def ladder_kernel(sites, notes_ref, sums_ref, change_ref, ladder_ref):
+def ladder_kernel(sites, notes_ref, sums_ref, label_ref, change_ref, ladder_ref):
     me = lax.axis_index("rep")
     notes = notes_ref[...]
     sums = sums_ref[...]
@@ -546,6 +526,7 @@
     actions = pltpu.roll(sums, LANES - 1, 1)
     ladder_ref[0] = jnp.sum(jnp.where(held, actions, 0.0)) / sites
     own = replica == me
+    label_ref[0] = jnp.sum(jnp.where(own & (lane == 0), notes, 0.0)).astype(jnp.int32)
     change_ref[0] = jnp.sum(jnp.where(own & (lane == 2), sums, 0.0))
 
 
@@ -568,16 +549,11 @@
     dma = pltpu.SemaphoreType.DMA
     last16 = rows // (2 * SUB) - 1
     last8 = rows // SUB - 1
-    edges, cold, new_label = pl.pallas_call(
+    edges = pl.pallas_call(
         pack_kernel,
         grid=(1,),
-        out_shape=(
-            jax.ShapeDtypeStruct((2, 2, tiles, SUB, LANES), f32),
-            jax.ShapeDtypeStruct((1,), f32),
-            jax.ShapeDtypeStruct((1,), jnp.int32),
-        ),
+        out_shape=jax.ShapeDtypeStruct((2, 2, tiles, SUB, LANES), f32),
         in_specs=[
-            smem,
             smem,
             smem,
             pl.BlockSpec((2 * SUB, width), lambda i: (0, 0)),
@@ -585,10 +561,9 @@
             pl.BlockSpec((SUB, width), lambda i: (0, 0)),
             pl.BlockSpec((SUB, width), lambda i: (last8, 0)),
         ],
-        out_specs=(inhbm, smem, smem),
-        scratch_shapes=[pltpu.VMEM((2, 2, tiles, SUB, LANES), f32), dma((2,))],
+        out_specs=pl.BlockSpec((2, 2, tiles, SUB, LANES), lambda i: (0, 0, 0, 0, 0)),
         name="pack",
-    )(labels, betas, swap_pairs, start, start, moment, moment)
+    )(labels, betas, start, start, moment, moment)
     forward = [(i, (i + 1) % strips) for i in range(strips)]
     backward = [((i + 1) % strips, i) for i in range(strips)]
     halos = (lax.ppermute(edges, "dom", forward),)
@@ -609,7 +584,8 @@
             jax.ShapeDtypeStruct((2, tiles, 2 * SUB, LANES), f32),
             jax.ShapeDtypeStruct((3, SUB, LANES), f32),
         ),
-        in_specs=[smem, smem, inhbm, inhbm],
+        grid=(1,),
+        in_specs=[smem, smem, smem, inhbm, inhbm],
         out_specs=(inhbm, inhbm, inhbm, inhbm),
         scratch_shapes=[
             pltpu.VMEM((3, SUB, LANES), f32),
@@ -628,12 +604,13 @@
         ),
         compiler_params=pltpu.CompilerParams(vmem_limit_bytes=WHOLE_VMEM),
         name="inner",
-    )(cold, accept, start, moment)
+    )(labels, betas, accept, start, moment)
     window = pltpu.VMEM((2, tiles, (EDGE + 2) * SUB, LANES), f32)
     outgoing = pl.pallas_call(
         functools.partial(outer_kernel, per_member, len(halos)),
         out_shape=jax.ShapeDtypeStruct((members, SUB, piece + LANES), f32),
-        in_specs=[smem] * 3 + [anywhere] * len(halos) + [inhbm] * 5,
+        grid=(1,),
+        in_specs=[smem] * 4 + [anywhere] * len(halos) + [inhbm] * 5,
         out_specs=inhbm,
         scratch_shapes=[
             window,
@@ -648,9 +625,9 @@
             dma((2, shares)),
             dma,
         ],
-        input_output_aliases={7 + len(halos): 0},
+        input_output_aliases={8 + len(halos): 0},
         name="outer",
-    )(cold, accept, new_label, *halos, state, energy, sums, start, outgoing)
+    )(labels, betas, accept, swap_pairs, *halos, state, energy, sums, start, outgoing)
     received = lax.all_to_all(outgoing, "rep", split_axis=0, concat_axis=0, tiled=True)
     out = strip_of(outgoing[:, :, :piece])
     ordered, notes = pl.pallas_call(
@@ -675,14 +652,15 @@
     for _ in range(strips - 1):
         passing = lax.ppermute(passing, "dom", forward)
         both = both + passing
-    change, ladder = pl.pallas_call(
+    new_label, change, ladder = pl.pallas_call(
         functools.partial(ladder_kernel, strips * rows * width),
         out_shape=(
+            jax.ShapeDtypeStruct((1,), jnp.int32),
             jax.ShapeDtypeStruct((1,), f32),
             jax.ShapeDtypeStruct((1,), f32),
         ),
         in_specs=[vmem, vmem],
-        out_specs=(smem, smem),
+        out_specs=(smem, smem, smem),
         compiler_params=pltpu.CompilerParams(vmem_limit_bytes=4 << 20),
         name="ladder",
     )(notes, both)

time: 85.3 us -> 84.2 us (0.987)
  Pallas kernels: 18.4 us -> 17.3 us
where the time goes in v10:
time: 84.2 us; the launch traced here: 83.8 us
  waiting for transfers between devices  50.1 us (60%)
  Pallas kernels  17.3 us (21%)
  starting transfers between devices  13.3 us (16%)
  between operations  2.01 us (2%)
  local copies, waits for them, and re-layouts  1.07 us (1%)
    all_to_all x1, waiting for transfers between devices, body(): lax.all_to_all(outgoing, 'rep', split_axis=0, concat_axis=0, tiled=True)  26.1 us
    all_to_all x1, waiting for transfers between devices, body(): lax.all_to_all(ordered, 'rep', split_axis=0, concat_axis=0, tiled=True)  21.4 us
    pallas_call x1, Pallas kernels, body(): pl.pallas_call(functools.partial(inner_kernel, per_member), out_shape=(ja...  8.62 us
    all_to_all x1, starting transfers between devices, body(): lax.all_to_all(outgoing, 'rep', split_axis=0, concat_axis=0, tiled=True)  6.97 us
    all_to_all x1, starting transfers between devices, body(): lax.all_to_all(ordered, 'rep', split_axis=0, concat_axis=0, tiled=True)  4.85 us
    pallas_call x1, Pallas kernels, body(): pl.pallas_call(functools.partial(outer_kernel, per_member, len(halos)), o...  4.23 us
    ppermute x1, waiting for transfers between devices, body(): passing = lax.ppermute(passing, 'dom', forward)  2.57 us
    pallas_call x1, Pallas kernels, body(): pl.pallas_call(pack_kernel, grid=(1,), out_shape=jax.ShapeDtypeStruct((2,...  1.96 us
  transfers between devices with their start and end apart: 4, of which 3 were waited for; matrix products, arithmetic and copies ran while one was open for 0% of the time, Pallas kernels for 11%

profile of v10, /device:TPU:9, one launch (start us, length us, event | category | flops | bytes accessed | tf_op | source)
XLA Modules:
  0.0 83.8 jit_solution(11163817090018874357)
XLA Ops:
  1.3 2.0 %pack.1 = f32[2,2,16,8,128]{4,3,2,1,0:T(8,128)} custom-call(s32[1]{0:T(128)S(6)} %copy.14.labels_ref, f32[16]{0:T(128)} %betas_ref.5, f32[128,2048]{1,0:T(8,128)} %bitcast.5, f32[128,2048]{1,0:T(8,128)} %bitcast.6, f32[128,2048]{1,0:T(8,128)} %bitcast.9, f32[128,2048]{1,0:T(8,128)} %bitcast.10), custom_call_target="tpu_custom_call" | custom-call | tf_op jit(solution)/shard_map/pack/pallas_call | solution.py:552
  3.2 1.2 %collective-permute-start = (f32[2,2,16,8,128]{4,3,2,1,0:T(8,128)}, f32[2,2,16,8,128]{4,3,2,1,0:T(8,128)}, u32[]{:S(2)}, u32[]{:S(2)}) collective-permute-start(f32[2,2,16,8,128]{4,3,2,1,0:T(8,128)} %pack.1), channel_id=1, source_target_pairs={{0,1},{1,0},{2,3},{3,2},{4,5},{5,4},{6,7},{7,6},{8,9},{9,8},{10,11... | collective-permute-start | bytes 786440 | tf_op jit(solution)/shard_map/ppermute | solution.py:569
  5.1 8.6 %inner.1 = (f32[16,8,2176]{2,1,0:T(8,128)}, f32[2,2,16,24,128]{4,3,2,1,0:T(8,128)}, f32[2,16,16,128]{3,2,1,0:T(8,128)}, f32[3,8,128]{2,1,0:T(8,128)}) custom-call(s32[1]{0:T(128)S(6)} %copy.14.labels_ref, f32[16]{0:T(128)} %betas_ref.5, s32[1]{0:T(128)S(6)} %copy.15.accept_ref, f32[128,2048]{1,0:T(8,128)} %bitcast.7, f32[128,2048]{1,0:T(8,128)} %bitcast.11), custom_call_target="tpu_custom_call" | custom-call | flops 26214400 | bytes 4194304 | tf_op jit(solution)/shard_map/inner/pallas_call | solution.py:579
  13.8 0.0 collective-permute-done.refs_0_
  13.8 4.2 %outer.1 = f32[16,8,2176]{2,1,0:T(8,128)} custom-call(s32[1]{0:T(128)S(6)} %copy.14.labels_ref, f32[16]{0:T(128)} %betas_ref.5, s32[1]{0:T(128)S(6)} %copy.15.accept_ref, s32[16]{0:T(128)} %swap_ref.1, f32[2,2,16,8,128]{4,3,2,1,0:T(8,128)} %collective-permute-done.refs_0_, ...), custom_call_target="tpu_custom_call", output_to_operand_aliasing={{}: (9, {})} | custom-call | tf_op jit(solution)/shard_map/outer/pallas_call | solution.py:609
  18.0 0.0 copy-start.1
  18.0 7.0 %all-to-all-start = ((f32[16,8,2176]{2,1,0:T(8,128)}), f32[16,8,2176]{2,1,0:T(8,128)S(1)}, u32[]{:S(2)}, u32[]{:S(2)}) async-start(f32[16,8,2176]{2,1,0:T(8,128)} %outer.1), calls=%async_computation | async-start | bytes 2228224 | tf_op jit(solution)/shard_map/all_to_all | solution.py:631
  25.0 0.0 copy-done.1
  25.0 0.1 slice_bitcast_fusion._
  25.1 0.0 copy-start
  25.1 26.1 %all-to-all-done.got_ref = f32[16,8,2176]{2,1,0:T(8,128)S(1)} async-done(((f32[16,8,2176]{2,1,0:T(8,128)}), f32[16,8,2176]{2,1,0:T(8,128)S(1)}, u32[]{:S(2)}, u32[]{:S(2)}) %all-to-all-start) | async-done | bytes 1114144 | tf_op jit(solution)/shard_map/all_to_all | solution.py:631
  51.2 1.8 %place.1 = (f32[16,8,2048]{2,1,0:T(8,128)}, f32[16,128]{1,0:T(8,128)S(1)}) custom-call(f32[16,8,2176]{2,1,0:T(8,128)S(1)} %all-to-all-done.got_ref, f32[1,128,2048]{2,1,0:T(8,128)S(1)} %slice_bitcast_fusion._), custom_call_target="tpu_custom_call" | custom-call | tf_op jit(solution)/shard_map/place/pallas_call | solution.py:633
  53.0 0.0 copy-done
  53.0 4.9 %all-to-all-start.1 = ((f32[16,8,2048]{2,1,0:T(8,128)}), f32[16,8,2048]{2,1,0:T(8,128)S(1)}, u32[]{:S(2)}, u32[]{:S(2)}) async-start(f32[16,8,2048]{2,1,0:T(8,128)} %get-tuple-element.18), calls=%async_computation.1 | async-start | bytes 2097152 | tf_op jit(solution)/shard_map/all_to_all | solution.py:649
  57.9 0.2 collective-permute-start.1
  58.1 2.6 %collective-permute-done.1 = f32[16,128]{1,0:T(8,128)S(1)} collective-permute-done((f32[16,128]{1,0:T(8,128)S(1)}, f32[16,128]{1,0:T(8,128)S(1)}, u32[]{:S(2)}, u32[]{:S(2)}) %collective-permute-start.1) | collective-permute-done | bytes 8224 | tf_op jit(solution)/shard_map/ppermute | solution.py:653
  60.7 0.7 ladder.1
  61.4 21.4 %all-to-all-done.1 = f32[16,8,2048]{2,1,0:T(8,128)S(1)} async-done(((f32[16,8,2048]{2,1,0:T(8,128)}), f32[16,8,2048]{2,1,0:T(8,128)S(1)}, u32[]{:S(2)}, u32[]{:S(2)}) %all-to-all-start.1) | async-done | bytes 1048608 | tf_op jit(solution)/shard_map/all_to_all | solution.py:649
  82.8 1.0 %copy.16 = f32[1,128,2048]{2,1,0:T(8,128)} copy(f32[1,128,2048]{2,1,0:T(8,128)S(1)} %bitcast.12) | data formatting | bytes 2097152
  (1 shorter events, 0.0 us)
Async XLA Ops:
  3.2 10.5 %collective-permute-start = (f32[2,2,16,8,128]{4,3,2,1,0:T(8,128)}, f32[2,2,16,8,128]{4,3,2,1,0:T(8,128)}, u32[]{:S(2)}, u32[]{:S(2)}) collective-permute-start(f32[2,2,16,8,128]{4,3,2,1,0:T(8,128)} %pack.1), channel_id=1, source_target_pairs={{0,1},{1,0},{2,3},{3,2},{4,5},{5,4},{6,7},{7,6},{8,9},{9,8},{10,11... | collective-permute-start | bytes 786440 | tf_op jit(solution)/shard_map/ppermute | solution.py:569
  18.0 7.0 %copy-start.1 = (f32[16,8,2176]{2,1,0:T(8,128)S(1)}, f32[16,8,2176]{2,1,0:T(8,128)}, u32[]{:S(2)}) copy-start(f32[16,8,2176]{2,1,0:T(8,128)} %outer.1) | copy-start | bytes 3342340
  18.0 33.2 %all-to-all-start = ((f32[16,8,2176]{2,1,0:T(8,128)}), f32[16,8,2176]{2,1,0:T(8,128)S(1)}, u32[]{:S(2)}, u32[]{:S(2)}) async-start(f32[16,8,2176]{2,1,0:T(8,128)} %outer.1), calls=%async_computation | async-start | bytes 2228224 | tf_op jit(solution)/shard_map/all_to_all | solution.py:631
  25.1 27.9 %copy-start = (f32[1,128,2048]{2,1,0:T(8,128)}, f32[1,128,2048]{2,1,0:T(8,128)S(1)}, u32[]{:S(2)}) copy-start(f32[1,128,2048]{2,1,0:T(8,128)S(1)} %slice_bitcast_fusion._) | copy-start | bytes 3145732
  53.0 29.8 %all-to-all-start.1 = ((f32[16,8,2048]{2,1,0:T(8,128)}), f32[16,8,2048]{2,1,0:T(8,128)S(1)}, u32[]{:S(2)}, u32[]{:S(2)}) async-start(f32[16,8,2048]{2,1,0:T(8,128)} %get-tuple-element.18), calls=%async_computation.1 | async-start | bytes 2097152 | tf_op jit(solution)/shard_map/all_to_all | solution.py:649
  57.9 2.8 %collective-permute-start.1 = (f32[16,128]{1,0:T(8,128)S(1)}, f32[16,128]{1,0:T(8,128)S(1)}, u32[]{:S(2)}, u32[]{:S(2)}) collective-permute-start(f32[16,128]{1,0:T(8,128)S(1)} %get-tuple-element.19.notes_ref), channel_id=1, source_target_pairs={{0,1},{1,0},{2,3},{3,2},{4,5},{5,4},{6,7},{7,6},{8,9},{9,8},{10,11... | collective-permute-start | bytes 24584 | tf_op jit(solution)/shard_map/ppermute | solution.py:653
